TPU v7x, 256 devices: a whole 4x4x8 slice. The times are simulated.
256 devices in a mesh: dp: 8 (over x_hi, y), ctx: 32 (over x_lo, z, core).
Axes of the slice: x: 4 (x_hi: 2, x_lo: 2; x = x_hi * 2 + x_lo), y: 4, z: 8, core: 2. Of those that a mesh axis runs over, the one named last changes fastest.
Arguments:
- query: bfloat16 [32768, 512], P(('dp', 'ctx')), may hold values from -6 to 6
- key: bfloat16 [32768, 512], P(('dp', 'ctx')), may hold values from -6 to 6
- value: bfloat16 [32768, 512], P(('dp', 'ctx'))
- gate: bfloat16 [32768, 512], P(('dp', 'ctx')), may hold values from -6 to 6
- out_weight: bfloat16 [512, 1024], replicated, may hold values from -0.25 to 0.25
- items: bfloat16 [1024, 1024], P('ctx'), may hold values from -0.1875 to 0.1875
- cotangent: bfloat16 [32768, 1024], P(('dp', 'ctx')), may hold values from -6 to 6
- user_blocks: int32 [8, 4], P('dp'), may hold values from 1 to 16, 32 in all within a row
- tail_rows: int32 [8, 4], P('dp'), may hold values from 1 to 128
- packing: int32 [8, 32], P('dp'), may hold values from 0 to 31, each once within a row
- cand_ids: int32 [8, 4, 128], P('dp'), may hold values from 0 to 1023
Outputs:
- scores: float32 [32768, 128], P(('dp', 'ctx'))
- grad_query: bfloat16 [32768, 512], P(('dp', 'ctx'))
- grad_key: bfloat16 [32768, 512], P(('dp', 'ctx'))
- grad_value: bfloat16 [32768, 512], P(('dp', 'ctx'))
- grad_gate: bfloat16 [32768, 512], P(('dp', 'ctx'))
- grad_out_weight: float32 [512, 1024], replicated
Inputs may be any that keep to these rules, and one draw needn't show every extreme that they name: `user_blocks`: in each group the 4 counts sum to 32 and the largest is exactly 16. `packing`: each group's row is a permutation of its 32 logical blocks; slots run device by device along ctx. `cand_ids`: rows of the item table.
All inputs are finite; a program needn't handle non-finite values.
Results may differ from a plain program's by a relative error of at most 0.0058.
Values may be sent and summed in bfloat16 or wider, within the bound.
No kernel may reach another device: no remote copies, remote signals or barrier semaphores. Data moves between devices by JAX's collectives and lax.ppermute only.
A program may use at most 128 MiB of HBM per device.

v0:
```python
import jax
import jax.numpy as jnp
from jax import lax
from jax.experimental import pallas as pl
from jax.experimental.pallas import tpu as pltpu
from jax.sharding import Mesh, PartitionSpec as P

AXES = ("xh", "y", "xl", "z", "core")
SIZES = (2, 4, 2, 8, 2)
DP = ("xh", "y")
CTX = ("xl", "z", "core")
SCALE = 128 ** (-0.5)
EPS = 1e-05
F32 = jnp.float32
BF16 = jnp.bfloat16
I32 = jnp.int32

VM = pl.BlockSpec(memory_space=pltpu.VMEM)
SM = pl.BlockSpec(memory_space=pltpu.SMEM)
HBM = pl.BlockSpec(memory_space=pltpu.HBM)


def dot(a, b, ca, cb):
    return lax.dot_general(a, b, (((ca,), (cb,)), ((), ())), preferred_element_type=F32)


def slot_of(place):
    down, other = place // 4, place % 4
    xl = (lax.axis_index("xl") + other // 2) % 2
    z = (lax.axis_index("z") + 8 - down) % 8
    core = (lax.axis_index("core") + other) % 2
    return xl * 16 + z * 2 + core


def fill_places(pk_ref, inv_ref):
    def one(place, carry):
        inv_ref[pk_ref[0, slot_of(place)]] = place
        return carry

    lax.fori_loop(0, 32, one, 0)


def user_of(ub_ref, tl_ref, logical):
    end0 = ub_ref[0, 0]
    end1 = end0 + ub_ref[0, 1]
    end2 = end1 + ub_ref[0, 2]
    user = (
        (logical >= end0).astype(I32) + (logical >= end1).astype(I32) + (logical >= end2).astype(I32)
    )
    first = jnp.where(user == 0, 0, jnp.where(user == 1, end0, jnp.where(user == 2, end1, end2)))
    return user, first, ub_ref[0, user], tl_ref[0, user]


def load_chunks(refs, buffer, sems):
    copies = [
        pltpu.make_async_copy(ref, buffer.at[pl.ds(4 * i, 4)], sems.at[i]) for i, ref in enumerate(refs)
    ]
    for copy in copies:
        copy.start()
    return copies


def iota(shape, axis):
    return lax.broadcasted_iota(I32, shape, axis)


def head_columns(other):
    xl = (lax.axis_index("xl") + other // 2) % 2
    core = (lax.axis_index("core") + other) % 2
    return pl.ds(pl.multiple_of((xl * 2 + core) * 128, 128), 128)


def pack_kernel(k_ref, v_ref, q_ref, g_ref, t_ref, o0, o1, o2, o3, rows, sems):
    copies = [
        pltpu.make_async_copy(ref, rows.at[i], sems.at[i])
        for i, ref in enumerate((k_ref, v_ref, q_ref, g_ref))
    ]
    for copy in copies:
        copy.start()
    outs = (o0, o1, o2, o3)
    for d, out in enumerate(outs):
        out[512:] = t_ref[:, head_columns(d)]
    for i, copy in enumerate(copies):
        copy.wait()
        for d, out in enumerate(outs):
            out[i * 128 : i * 128 + 128] = rows[i, :, head_columns(d)]


def mixed_grad_kernel(c0, c1, c2, c3, w_ref, gm_ref, wbuf, sem):
    copy = pltpu.make_async_copy(
        w_ref.at[head_columns(0)], wbuf, sem
    )
    copy.start()
    copy.wait()
    for d, cot in enumerate((c0, c1, c2, c3)):
        gm_ref[d] = dot(cot[...], wbuf[...], 1, 1)


def merge_kernel(p0, p1, p2, p3, kv_ref, qp_ref, gate_ref):
    for d, piece in enumerate((p0, p1, p2, p3)):
        kv_ref[d, 0] = piece[:128]
        kv_ref[d, 1] = piece[128:256]
        qp_ref[d, :128] = piece[256:384]
        qp_ref[d, 128:] = piece[512:]
        gate_ref[d] = piece[384:512]


def forward_kernel(ub, tl, pk, q_ref, gate_ref, gm_ref, *rest):
    chunks, (att_ref, stat_ref), (kv, inv, sems) = rest[:8], rest[8:10], rest[10:]
    copies = load_chunks(chunks, kv, sems)
    fill_places(pk, inv)
    for copy in copies:
        copy.wait()
    row = iota((128, 512), 0)
    col = iota((128, 512), 1)
    lane = iota((128, 128), 1)

    def one(slot, carry):
        logical = pk[0, slot_of(slot)]
        user, first, blocks, tail = user_of(ub, tl, logical)
        own = logical - first
        query = q_ref[slot, :128]

        def step(j, acc):
            places = [inv[first + jnp.minimum(4 * j + i, own)] for i in range(4)]
            keys = jnp.concatenate([kv[p, 0] for p in places], axis=0)
            values = jnp.concatenate([kv[p, 1] for p in places], axis=0)
            logits = dot(query, keys, 1, 1) * SCALE
            silu = logits / (1.0 + jnp.exp(-logits))
            weights = jnp.where(col + (4 * j - own) * 128 <= row, silu, 0.0).astype(BF16)
            return acc + dot(weights, values, 1, 0)

        acc = lax.fori_loop(0, own // 4 + 1, step, jnp.zeros((128, 128), F32))
        limit = jnp.where(own == blocks - 1, tail, 128)
        valid = iota((128, 128), 0) < limit
        att = jnp.where(valid, acc, 0.0)
        att_ref[slot] = att
        grad = jnp.where(valid, gm_ref[slot] * gate_ref[slot].astype(F32), 0.0)
        mean = jnp.mean(att, axis=1, keepdims=True)
        centered = att - mean
        spread = jnp.sum(centered * centered, axis=1, keepdims=True)
        total = jnp.sum(grad, axis=1, keepdims=True)
        cross = jnp.sum(grad * centered, axis=1, keepdims=True)
        stats = jnp.where(
            lane == 0, mean, jnp.where(lane == 1, spread, jnp.where(lane == 2, total, cross))
        )
        stat_ref[slot] = stats.T[:8]
        return carry

    lax.fori_loop(0, 4, one, 0)


def norm_kernel(
    ub, tl, pk, att_ref, s0, s1, s2, s3, gate_ref, gm_ref, da_ref, gg_ref, mixed_ref
):
    line = iota((128, 128), 0)
    for slot in range(4):
        user, first, blocks, tail = user_of(ub, tl, pk[0, slot_of(slot)])
        own = pk[0, slot_of(slot)] - first
        limit = jnp.where(own == blocks - 1, tail, 128)
        valid = line < limit
        stats = [s[slot ^ e] for e, s in enumerate((s0, s1, s2, s3))]
        mean = (stats[0][0:1] + stats[1][0:1] + stats[2][0:1] + stats[3][0:1]) * 0.25
        var = jnp.zeros((1, 128), F32)
        total = jnp.zeros((1, 128), F32)
        cross = jnp.zeros((1, 128), F32)
        for stat in stats:
            away = stat[0:1] - mean
            var = var + stat[1:2] + 128.0 * away * away
            total = total + stat[2:3]
            cross = cross + stat[3:4] + away * stat[2:3]
        inv_std = lax.rsqrt(var * (1.0 / 512) + EPS)
        rows = jnp.where(
            line == 0,
            mean,
            jnp.where(
                line == 1,
                inv_std,
                jnp.where(line == 2, total * (1.0 / 512), cross * inv_std * (1.0 / 512)),
            ),
        ).T
        mean, inv_std, total, cross = (rows[:, i : i + 1] for i in range(4))
        normed = (att_ref[slot] - mean) * inv_std
        gate = gate_ref[slot].astype(F32)
        gmix = jnp.where(valid, gm_ref[slot], 0.0)
        da = (gmix * gate - total - normed * cross) * inv_std
        da_ref[slot] = jnp.where(valid, da, 0.0).astype(BF16)
        gg_ref[slot] = (gmix * normed).astype(BF16)
        mixed_ref[pl.ds(slot * 128, 128), :] = jnp.where(valid, normed * gate, 0.0).astype(BF16)


def weight_kernel(mixed_ref, c0, c1, c2, c3, gw_ref):
    for part in range(4):
        term = jnp.zeros((128, 256), F32)
        for d, cot in enumerate((c0, c1, c2, c3)):
            term = term + dot(mixed_ref[pl.ds(d * 128, 128), :], cot[:, pl.ds(part * 256, 256)], 0, 0)
        term = term.astype(BF16)
        for r in range(8):
            for c in range(2):
                gw_ref[r * 8 + part * 2 + c] = term[r * 16 : r * 16 + 16, c * 128 : c * 128 + 128]


def score_kernel(ub, tl, pk, mixed_ref, cand_ref, *rest):
    chunks, (sc_ref,), (qp, sems) = rest[:8], rest[8:9], rest[9:]
    copies = load_chunks(chunks, qp, sems)
    row = iota((32, 128), 0)
    for copy in copies:
        copy.wait()
    table = jnp.concatenate([qp[p, 128:160] for p in range(32)], axis=0).T
    for slot in range(4):
        user = user_of(ub, tl, pk[0, slot_of(slot)])[0]
        cand = jnp.broadcast_to(cand_ref[pl.ds(user, 1), :], (32, 128))
        pick = jnp.concatenate(
            [(cand - slot_of(p) * 32 == row).astype(F32).astype(BF16) for p in range(32)], axis=0
        )
        chosen = dot(table, pick, 1, 0).astype(BF16)
        sc_ref[slot] = dot(mixed_ref[pl.ds(slot * 128, 128), :], chosen, 1, 0).astype(BF16)


def query_kernel(ub, tl, pk, q_ref, da_ref, gg_ref, sc_ref, *rest):
    chunks, outs, (kv, gq, inv, sems) = rest[:8], rest[8:12], rest[12:]
    copies = load_chunks(chunks, kv, sems)
    fill_places(pk, inv)
    for copy in copies:
        copy.wait()
    row = iota((128, 512), 0)
    col = iota((128, 512), 1)

    def one(slot, carry):
        logical = pk[0, slot_of(slot)]
        first = user_of(ub, tl, logical)[1]
        own = logical - first
        query = q_ref[slot, :128]
        grad = da_ref[slot]

        def step(j, acc):
            places = [inv[first + jnp.minimum(4 * j + i, own)] for i in range(4)]
            keys = jnp.concatenate([kv[p, 0] for p in places], axis=0)
            values = jnp.concatenate([kv[p, 1] for p in places], axis=0)
            logits = dot(query, keys, 1, 1) * SCALE
            slopes = dot(grad, values, 1, 1)
            sigma = 1.0 / (1.0 + jnp.exp(-logits))
            slope = sigma * (1.0 + logits * (1.0 - sigma))
            ds = jnp.where(col + (4 * j - own) * 128 <= row, slopes * slope, 0.0).astype(BF16)
            return acc + dot(ds, keys, 1, 0)

        acc = lax.fori_loop(0, own // 4 + 1, step, jnp.zeros((128, 128), F32))
        gq[slot] = (acc * SCALE).astype(BF16)
        return carry

    lax.fori_loop(0, 4, one, 0)
    for slot in range(4):
        outs[slot][0] = gq[slot]
        outs[slot][1] = gg_ref[slot]
        outs[slot][2] = sc_ref[slot]


def key_kernel(ub, tl, pk, kv_ref, *rest):
    qs, das, outs, (qbuf, dbuf, both, inv, qsems, dsems) = (
        rest[:8], rest[8:16], rest[16:20], rest[20:],
    )
    copies = load_chunks(qs, qbuf, qsems) + load_chunks(das, dbuf, dsems)
    fill_places(pk, inv)
    for copy in copies:
        copy.wait()
    row = iota((128, 512), 0)
    col = iota((128, 512), 1)

    def one(slot, carry):
        logical = pk[0, slot_of(slot)]
        user, first, blocks, tail = user_of(ub, tl, logical)
        count = first + blocks - logical
        key = kv_ref[slot, 0]
        value = kv_ref[slot, 1]

        def step(j, carry):
            gk, gv = carry
            places = [inv[logical + jnp.minimum(4 * j + i, count - 1)] for i in range(4)]
            queries = jnp.concatenate([qbuf[p, :128] for p in places], axis=0)
            grads = jnp.concatenate([dbuf[p] for p in places], axis=0)
            logits = dot(key, queries, 1, 1) * SCALE
            slopes = dot(value, grads, 1, 1)
            sigma = 1.0 / (1.0 + jnp.exp(-logits))
            silu = logits * sigma
            slope = sigma * (1.0 + logits * (1.0 - sigma))
            later = col + j * 512
            allowed = (later >= row) & (later < count * 128)
            weights = jnp.where(allowed, silu, 0.0).astype(BF16)
            ds = jnp.where(allowed, slopes * slope, 0.0).astype(BF16)
            return gk + dot(ds, queries, 1, 0), gv + dot(weights, grads, 1, 0)

        zero = jnp.zeros((128, 128), F32)
        gk, gv = lax.fori_loop(0, (count + 3) // 4, step, (zero, zero))
        both[slot, 0] = (gk * SCALE).astype(BF16)
        both[slot, 1] = gv.astype(BF16)
        return carry

    lax.fori_loop(0, 4, one, 0)
    for slot in range(4):
        outs[slot][...] = both[slot]


def unpack_early_kernel(p0, p1, p2, p3, gq_ref, gg_ref, sc_ref):
    scores = jnp.zeros((128, 128), F32)
    for d, piece in enumerate((p0, p1, p2, p3)):
        gq_ref[:, head_columns(d)] = piece[0]
        gg_ref[:, head_columns(d)] = piece[1]
        scores = scores + piece[2].astype(F32)
    sc_ref[...] = scores


def unpack_late_kernel(p0, p1, p2, p3, gk_ref, gv_ref):
    for d, piece in enumerate((p0, p1, p2, p3)):
        gk_ref[:, head_columns(d)] = piece[0]
        gv_ref[:, head_columns(d)] = piece[1]


def sum_kernel(parts_ref, out_ref):
    total = jnp.sum(parts_ref[...].astype(F32), axis=0).astype(BF16)
    for i in range(8):
        out_ref[i] = total


def spread_kernel(line_ref, out_ref):
    for i in range(16):
        out_ref[i] = line_ref[...]


def assemble_kernel(own_ref, far_ref, out_ref):
    me = lax.axis_index("core")
    for r in range(8):
        for xl in range(2):
            for z in range(8):
                own = own_ref[r * 2 + xl, z].astype(F32)
                far = far_ref[r * 2 + xl, z].astype(F32)
                for core in range(2):
                    rows = pl.ds((xl * 2 + core) * 128 + r * 16, 16)
                    out_ref[rows, pl.ds(z * 128, 128)] = jnp.where(me == core, own, far)


def call(kernel, ins, outs, scratch=(), us=2, mib=8):
    return pl.pallas_call(
        kernel,
        in_specs=[spec for spec, _ in ins],
        out_specs=[VM] * len(outs),
        out_shape=[jax.ShapeDtypeStruct(shape, kind) for shape, kind in outs],
        scratch_shapes=list(scratch),
        compiler_params=pltpu.CompilerParams(vmem_limit_bytes=mib << 20),
        cost_estimate=pl.CostEstimate(
            flops=us * 1000000000, bytes_accessed=us * 1000000, transcendentals=0
        ),
    )(*[value for _, value in ins])


def flip(array, axis):
    return lax.ppermute(array, axis, [(0, 1), (1, 0)])


def ring(array):
    up, down = [array], [array]
    for step in range(4):
        up.append(lax.ppermute(up[-1], "z", [(i, (i + 1) % 8) for i in range(8)]))
        if step < 3:
            down.append(lax.ppermute(down[-1], "z", [(i, (i + 7) % 8) for i in range(8)]))
    return up + down[:0:-1]


def after(value, *waits):
    return lax.optimization_barrier((value,) + waits)[0]


def vm(*arrays):
    return [(VM, a) for a in arrays]


def raw(arrays):
    return [(HBM, pltpu.with_memory_space_constraint(a, pltpu.HBM)) for a in arrays]


def swap(pieces):
    both = lax.ppermute(pieces[3], ("xl", "core"), [(i, 3 - i) for i in range(4)])
    return [pieces[0], flip(pieces[1], "core"), flip(pieces[2], "xl"), both]


def body(
    query, key, value, gate, out_weight, items, cotangent, user_blocks, tail_rows, packing, cand_ids
):
    facts = [(SM, user_blocks), (SM, tail_rows), (SM, packing)]
    block = (4, 128, 128)
    places = pltpu.SMEM((32,), I32)
    sems = pltpu.SemaphoreType.DMA((8,))
    kv_buffer = pltpu.VMEM((32, 2, 128, 128), BF16)
    table = dot(items, out_weight, 1, 1).astype(BF16)
    packed = call(
        pack_kernel,
        raw([key, value, query, gate]) + vm(table),
        [((544, 128), BF16)] * 4,
        [pltpu.VMEM((4, 128, 512), BF16), pltpu.SemaphoreType.DMA((4,))],
    )
    first = swap(packed)
    kv, qp, gate_h = call(
        merge_kernel,
        vm(*first),
        [((4, 2, 128, 128), BF16), ((4, 160, 128), BF16), (block, BF16)],
    )
    kvs = ring(kv)
    cots = [cotangent] + swap([after(cotangent, packed[0])] * 4)[1:]
    (gm,) = call(
        mixed_grad_kernel,
        vm(*cots) + raw([out_weight]),
        [(block, F32)],
        [pltpu.VMEM((128, 1024), BF16), pltpu.SemaphoreType.DMA],
    )
    att, stats = call(
        forward_kernel,
        facts + vm(qp, gate_h, gm) + raw(kvs),
        [(block, F32), ((4, 8, 128), F32)],
        [kv_buffer, places, sems],
        us=6,
    )
    qps = ring(after(qp, kvs[3], kvs[5]))
    stats = after(stats, qps[1], qps[7])
    all_stats = swap([stats] * 4)
    da, gg, mixed = call(
        norm_kernel,
        facts + vm(after(att, qps[2], qps[6]), *all_stats, gate_h, gm),
        [(block, BF16), (block, BF16), ((512, 128), BF16)],
    )
    das = ring(da)
    (gw,) = call(weight_kernel, vm(mixed, *cots), [((64, 16, 128), BF16)])
    parts = lax.all_to_all(after(gw, qps[3], qps[5], das[1], das[7]), ("xh", "y", "z"), split_axis=0, concat_axis=0, tiled=True)
    (sc,) = call(
        score_kernel,
        facts + vm(mixed, cand_ids[0]) + raw(qps),
        [(block, BF16)],
        [pltpu.VMEM((32, 160, 128), BF16), sems],
    )
    early = call(
        query_kernel,
        facts + vm(qp, da, gg, sc) + raw(kvs),
        [((3, 128, 128), BF16)] * 4,
        [kv_buffer, pltpu.VMEM(block, BF16), places, sems],
        us=6,
    )
    early = swap(early)
    (piece,) = call(sum_kernel, vm(parts), [((8, 16, 128), BF16)])
    line = lax.all_to_all(piece, "z", split_axis=0, concat_axis=0, tiled=True)
    (lines,) = call(spread_kernel, vm(line), [((16, 8, 16, 128), BF16)])
    near = lax.all_to_all(lines, ("xh", "y", "xl"), split_axis=0, concat_axis=0, tiled=True)
    late = call(
        key_kernel,
        facts + vm(kv) + raw(qps) + raw(das),
        [((2, 128, 128), BF16)] * 4,
        [
            pltpu.VMEM((32, 160, 128), BF16),
            pltpu.VMEM((32, 128, 128), BF16),
            pltpu.VMEM((4, 2, 128, 128), BF16),
            places,
            sems,
            sems,
        ],
        us=8,
        mib=12,
    )
    late = swap(late)
    far = flip(near, "core")
    (gow,) = call(assemble_kernel, vm(near, far), [((512, 1024), F32)])
    rows = (128, 512)
    gq, gg, scores = call(
        unpack_early_kernel, vm(*early), [(rows, BF16), (rows, BF16), ((128, 128), F32)]
    )
    gk, gv = call(unpack_late_kernel, vm(*late), [(rows, BF16)] * 2)
    return (scores, gq, gk, gv, gg, gow)


def solution(mesh):
    inner = Mesh(mesh.devices.reshape(SIZES), AXES)
    rows = P(DP + CTX, None)
    in_specs = (
        rows, rows, rows, rows, P(), P(CTX, None), rows,
        P(DP, None), P(DP, None), P(DP, None), P(DP, None, None),
    )
    out_specs = (rows, rows, rows, rows, rows, P())
    return jax.shard_map(body, mesh=inner, in_specs=in_specs, out_specs=out_specs, check_vma=False)
```

profile of v0, /device:TPU:1, one launch (start us, length us, event | category | flops | bytes accessed | tf_op | source)
XLA Modules:
  0.0 156.1 jit_solution(1588385840616935114)
XLA Ops:
  4.3 3.3 %collective-permute-start = (bf16[544,128]{1,0:T(8,128)(2,1)S(1)}, bf16[544,128]{1,0:T(8,128)(2,1)S(1)}, u32[]{:S(2)}, u32[]{:S(2)}) collective-permute-start(bf16[544,128]{1,0:T(8,128)(2,1)S(1)} %get-tuple-element.37), channel_id=1, source_target_pairs={{0,1},{1,0},{2,3},{3,2},{4,5},{5,4},{6,7},{7,6},{8,9},{9,8},{10,11... | collective-permute-start | bytes 417800 | tf_op jit(solution)/shard_map/ppermute | solution.py:356
  9.3 3.5 %collective-permute-done.1.p2 = bf16[544,128]{1,0:T(8,128)(2,1)S(1)} collective-permute-done((bf16[544,128]{1,0:T(8,128)(2,1)S(1)}, bf16[544,128]{1,0:T(8,128)(2,1)S(1)}, u32[]{:S(2)}, u32[]{:S(2)}) %collective-permute-start.1) | collective-permute-done | bytes 139296 | tf_op jit(solution)/shard_map/ppermute | solution.py:356
  12.8 3.2 %collective-permute-done.2.p3 = bf16[544,128]{1,0:T(8,128)(2,1)S(1)} collective-permute-done((bf16[544,128]{1,0:T(8,128)(2,1)S(1)}, bf16[544,128]{1,0:T(8,128)(2,1)S(1)}, u32[]{:S(2)}, u32[]{:S(2)}) %collective-permute-start.2) | collective-permute-done | bytes 139296 | tf_op jit(solution)/shard_map/ppermute | solution.py:381
  16.2 3.9 %collective-permute-start.10 = (bf16[4,2,128,128]{3,2,1,0:T(8,128)(2,1)S(1)}, bf16[4,2,128,128]{3,2,1,0:T(8,128)(2,1)S(1)}, u32[]{:S(2)}, u32[]{:S(2)}) collective-permute-start(bf16[4,2,128,128]{3,2,1,0:T(8,128)(2,1)S(1)} %get-tuple-element.43.rest_0_.kv_ref), channel_id=1, source_target_pairs={{0,14},{2,0},{4,2},{6,4},{8,6},{10,8},{12,10},{14,12},{1,15},{3,1}... | collective-permute-start | bytes 786440 | tf_op jit(solution)/shard_map/ppermute | solution.py:364
  20.1 6.5 %collective-permute-done.6.rest_1_ = bf16[4,2,128,128]{3,2,1,0:T(8,128)(2,1)S(1)} collective-permute-done((bf16[4,2,128,128]{3,2,1,0:T(8,128)(2,1)S(1)}, bf16[4,2,128,128]{3,2,1,0:T(8,128)(2,1)S(1)}, u32[]{:S(2)}, u32[]{:S(2)}) %collective-permute-start.6) | collective-permute-done | bytes 262176 | tf_op jit(solution)/shard_map/ppermute | solution.py:362
  26.6 2.7 %collective-permute-start.11 = (bf16[4,2,128,128]{3,2,1,0:T(8,128)(2,1)S(1)}, bf16[4,2,128,128]{3,2,1,0:T(8,128)(2,1)S(1)}, u32[]{:S(2)}, u32[]{:S(2)}) collective-permute-start(bf16[4,2,128,128]{3,2,1,0:T(8,128)(2,1)S(1)} %collective-permute-done.10.rest_7_), channel_id=1, source_target_pairs={{0,14},{2,0},{4,2},{6,4},{8,6},{10,8},{12,10},{14,12},{1,15},{3,1}... | collective-permute-start | bytes 786440 | tf_op jit(solution)/shard_map/ppermute | solution.py:364
  29.2 5.7 %collective-permute-done.7.rest_2_ = bf16[4,2,128,128]{3,2,1,0:T(8,128)(2,1)S(1)} collective-permute-done((bf16[4,2,128,128]{3,2,1,0:T(8,128)(2,1)S(1)}, bf16[4,2,128,128]{3,2,1,0:T(8,128)(2,1)S(1)}, u32[]{:S(2)}, u32[]{:S(2)}) %collective-permute-start.7) | collective-permute-done | bytes 262176 | tf_op jit(solution)/shard_map/ppermute | solution.py:362
  34.9 2.7 %collective-permute-start.12 = (bf16[4,2,128,128]{3,2,1,0:T(8,128)(2,1)S(1)}, bf16[4,2,128,128]{3,2,1,0:T(8,128)(2,1)S(1)}, u32[]{:S(2)}, u32[]{:S(2)}) collective-permute-start(bf16[4,2,128,128]{3,2,1,0:T(8,128)(2,1)S(1)} %collective-permute-done.11.rest_6_), channel_id=1, source_target_pairs={{0,14},{2,0},{4,2},{6,4},{8,6},{10,8},{12,10},{14,12},{1,15},{3,1}... | collective-permute-start | bytes 786440 | tf_op jit(solution)/shard_map/ppermute | solution.py:364
  42.5 2.7 %collective-permute-start.15 = (bf16[4,160,128]{2,1,0:T(8,128)(2,1)S(1)}, bf16[4,160,128]{2,1,0:T(8,128)(2,1)S(1)}, u32[]{:S(2)}, u32[]{:S(2)}) collective-permute-start(bf16[4,160,128]{2,1,0:T(8,128)(2,1)S(1)} %get-tuple-element.45.q_ref.rest_0_), channel_id=1, source_target_pairs={{0,14},{2,0},{4,2},{6,4},{8,6},{10,8},{12,10},{14,12},{1,15},{3,1}... | collective-permute-start | bytes 491528 | tf_op jit(solution)/shard_map/ppermute | solution.py:364
  45.2 2.4 %collective-permute-done.4.c2 = bf16[128,1024]{1,0:T(8,128)(2,1)S(1)} collective-permute-done((bf16[128,1024]{1,0:T(8,128)(2,1)S(1)}, bf16[128,1024]{1,0:T(8,128)(2,1)S(1)}, u32[]{:S(2)}, u32[]{:S(2)}) %collective-permute-start.4) | collective-permute-done | bytes 262176 | tf_op jit(solution)/shard_map/ppermute | solution.py:356
  47.7 6.0 %collective-permute-done.5.c3 = bf16[128,1024]{1,0:T(8,128)(2,1)S(1)} collective-permute-done((bf16[128,1024]{1,0:T(8,128)(2,1)S(1)}, bf16[128,1024]{1,0:T(8,128)(2,1)S(1)}, u32[]{:S(2)}, u32[]{:S(2)}) %collective-permute-start.5) | collective-permute-done | bytes 262176 | tf_op jit(solution)/shard_map/ppermute | solution.py:381
  55.3 2.6 %collective-permute-start.16 = (bf16[4,160,128]{2,1,0:T(8,128)(2,1)S(1)}, bf16[4,160,128]{2,1,0:T(8,128)(2,1)S(1)}, u32[]{:S(2)}, u32[]{:S(2)}) collective-permute-start(bf16[4,160,128]{2,1,0:T(8,128)(2,1)S(1)} %collective-permute-done.15.rest_7_), channel_id=1, source_target_pairs={{0,14},{2,0},{4,2},{6,4},{8,6},{10,8},{12,10},{14,12},{1,15},{3,1}... | collective-permute-start | bytes 491528 | tf_op jit(solution)/shard_map/ppermute | solution.py:364
  58.6 5.4 %shard_map.157 = (f32[4,128,128]{2,1,0:T(8,128)S(1)}, f32[4,8,128]{2,1,0:T(8,128)S(1)}) custom-call(s32[1,4]{1,0:T(1,128)S(1)} %copy-done.8, s32[1,4]{1,0:T(1,128)S(1)} %copy-done.9, s32[1,32]{1,0:T(1,128)S(1)} %copy-done.10, bf16[4,160,128]{2,1,0:T(8,128)(2,1)S(1)} %get-tuple-element.45.q_ref.rest_0_, bf16[4,128,128]{2,1,0:T(8,128)(2,1)S(1)} %get-tuple-element.41.gate_ref, ...), custom_call_target="tpu_custom_call" | custom-call | flops 6000000000 | bytes 6000000 | tf_op jit(solution)/shard_map/pallas_call | solution.py:342
  73.5 2.7 %collective-permute-start.22 = (bf16[4,160,128]{2,1,0:T(8,128)(2,1)S(1)}, bf16[4,160,128]{2,1,0:T(8,128)(2,1)S(1)}, u32[]{:S(2)}, u32[]{:S(2)}) collective-permute-start(bf16[4,160,128]{2,1,0:T(8,128)(2,1)S(1)} %collective-permute-done.16.rest_6_), channel_id=1, source_target_pairs={{0,14},{2,0},{4,2},{6,4},{8,6},{10,8},{12,10},{14,12},{1,15},{3,1}... | collective-permute-start | bytes 491528 | tf_op jit(solution)/shard_map/ppermute | solution.py:364
  79.7 11.7 %all-to-all-start = ((bf16[64,16,128]{2,1,0:T(8,128)(2,1)}), bf16[64,16,128]{2,1,0:T(8,128)(2,1)S(1)}, u32[]{:S(2)}, u32[]{:S(2)}) async-start(bf16[64,16,128]{2,1,0:T(8,128)(2,1)} %shard_map.164), calls=%async_computation | async-start | bytes 524288 | tf_op jit(solution)/shard_map/all_to_all | solution.py:431
  94.2 6.2 %collective-permute-done.27.rest_10_ = bf16[4,128,128]{2,1,0:T(8,128)(2,1)S(1)} collective-permute-done((bf16[4,128,128]{2,1,0:T(8,128)(2,1)S(1)}, bf16[4,128,128]{2,1,0:T(8,128)(2,1)S(1)}, u32[]{:S(2)}, u32[]{:S(2)}) %collective-permute-start.27) | collective-permute-done | bytes 131104 | tf_op jit(solution)/shard_map/ppermute | solution.py:362
  100.4 2.7 %collective-permute-start.32 = (bf16[4,128,128]{2,1,0:T(8,128)(2,1)S(1)}, bf16[4,128,128]{2,1,0:T(8,128)(2,1)S(1)}, u32[]{:S(2)}, u32[]{:S(2)}) collective-permute-start(bf16[4,128,128]{2,1,0:T(8,128)(2,1)S(1)} %collective-permute-done.31.rest_14_), channel_id=1, source_target_pairs={{0,14},{2,0},{4,2},{6,4},{8,6},{10,8},{12,10},{14,12},{1,15},{3,1}... | collective-permute-start | bytes 393224 | tf_op jit(solution)/shard_map/ppermute | solution.py:364
  104.7 5.1 %all-to-all-start.1 = ((bf16[8,16,128]{2,1,0:T(8,128)(2,1)}), bf16[8,16,128]{2,1,0:T(8,128)(2,1)S(1)}, u32[]{:S(2)}, u32[]{:S(2)}) async-start(bf16[8,16,128]{2,1,0:T(8,128)(2,1)} %shard_map.165), calls=%async_computation.1 | async-start | bytes 65536 | tf_op jit(solution)/shard_map/all_to_all | solution.py:447
  110.5 3.0 %shard_map.159.sc_ref = bf16[4,128,128]{2,1,0:T(8,128)(2,1)S(1)} custom-call(s32[1,4]{1,0:T(1,128)S(1)} %copy-done.8, s32[1,4]{1,0:T(1,128)S(1)} %copy-done.9, s32[1,32]{1,0:T(1,128)S(1)} %copy-done.10, bf16[512,128]{1,0:T(8,128)(2,1)S(1)} %get-tuple-element.51.mixed_ref, s32[4,128]{1,0:T(4,128)S(1)} %bitcast.3, bf16[4,160,128]{2,1,0:T(8,128)(2,1)} %copy-done.4, ...), custom_call_target="tpu_custom_call" | custom-call | flops 2000000000 | bytes 2000000 | tf_op jit(solution)/shard_map/pallas_call | solution.py:342
  117.5 6.7 %all-to-all-start.2 = ((bf16[16,8,16,128]{3,2,1,0:T(8,128)(2,1)}), bf16[16,8,16,128]{3,2,1,0:T(8,128)(2,1)S(1)}, u32[]{:S(2)}, u32[]{:S(2)}) async-start(bf16[16,8,16,128]{3,2,1,0:T(8,128)(2,1)} %shard_map.166), calls=%async_computation.2 | async-start | bytes 1048576 | tf_op jit(solution)/shard_map/all_to_all | solution.py:449
  124.3 4.9 %shard_map.160 = (bf16[3,128,128]{2,1,0:T(8,128)(2,1)S(1)}, bf16[3,128,128]{2,1,0:T(8,128)(2,1)S(1)}, bf16[3,128,128]{2,1,0:T(8,128)(2,1)S(1)}, bf16[3,128,128]{2,1,0:T(8,128)(2,1)S(1)}) custom-call(s32[1,4]{1,0:T(1,128)S(1)} %copy-done.8, s32[1,4]{1,0:T(1,128)S(1)} %copy-done.9, s32[1,32]{1,0:T(1,128)S(1)} %copy-done.10, ...), custom_call_target="tpu_custom_call" | custom-call | flops 6000000000 | bytes 6000000 | tf_op jit(solution)/shard_map/pallas_call | solution.py:342
  129.2 4.9 %collective-permute-start.23 = (bf16[3,128,128]{2,1,0:T(8,128)(2,1)S(1)}, bf16[3,128,128]{2,1,0:T(8,128)(2,1)S(1)}, u32[]{:S(2)}, u32[]{:S(2)}) collective-permute-start(bf16[3,128,128]{2,1,0:T(8,128)(2,1)S(1)} %get-tuple-element.53), channel_id=1, source_target_pairs={{0,1},{1,0},{2,3},{3,2},{4,5},{5,4},{6,7},{7,6},{8,9},{9,8},{10,11... | collective-permute-start | bytes 294920 | tf_op jit(solution)/shard_map/ppermute | solution.py:356
  135.9 3.3 %collective-permute-start.36 = (bf16[16,8,16,128]{3,2,1,0:T(8,128)(2,1)S(1)}, bf16[16,8,16,128]{3,2,1,0:T(8,128)(2,1)S(1)}, u32[]{:S(2)}, u32[]{:S(2)}) collective-permute-start(bf16[16,8,16,128]{3,2,1,0:T(8,128)(2,1)S(1)} %all-to-all-done.2.own_ref), channel_id=1, source_target_pairs={{0,1},{1,0},{2,3},{3,2},{4,5},{5,4},{6,7},{7,6},{8,9},{9,8},{10,11... | collective-permute-start | bytes 1572872 | tf_op jit(solution)/shard_map/ppermute | solution.py:356
  139.9 8.4 %shard_map.162 = (bf16[2,128,128]{2,1,0:T(8,128)(2,1)S(1)}, bf16[2,128,128]{2,1,0:T(8,128)(2,1)S(1)}, bf16[2,128,128]{2,1,0:T(8,128)(2,1)S(1)}, bf16[2,128,128]{2,1,0:T(8,128)(2,1)S(1)}) custom-call(s32[1,4]{1,0:T(1,128)S(1)} %copy-done.8, s32[1,4]{1,0:T(1,128)S(1)} %copy-done.9, s32[1,32]{1,0:T(1,128)S(1)} %copy-done.10, ...), custom_call_target="tpu_custom_call" | custom-call | flops 8000000000 | bytes 8000000 | tf_op jit(solution)/shard_map/pallas_call | solution.py:342
  (135 shorter events, 44.8 us)
Async XLA Ops:
  7.6 8.4 %collective-permute-start.2 = (bf16[544,128]{1,0:T(8,128)(2,1)S(1)}, bf16[544,128]{1,0:T(8,128)(2,1)S(1)}, u32[]{:S(2)}, u32[]{:S(2)}) collective-permute-start(bf16[544,128]{1,0:T(8,128)(2,1)S(1)} %get-tuple-element.39), channel_id=1, source_target_pairs={{0,17},{1,16},{16,1},{17,0},{2,19},{3,18},{18,3},{19,2},{4,21},{5,... | collective-permute-start | bytes 417800 | tf_op jit(solution)/shard_map/ppermute | solution.py:381
  16.1 10.5 %collective-permute-start.6 = (bf16[4,2,128,128]{3,2,1,0:T(8,128)(2,1)S(1)}, bf16[4,2,128,128]{3,2,1,0:T(8,128)(2,1)S(1)}, u32[]{:S(2)}, u32[]{:S(2)}) collective-permute-start(bf16[4,2,128,128]{3,2,1,0:T(8,128)(2,1)S(1)} %get-tuple-element.43.rest_0_.kv_ref), channel_id=1, source_target_pairs={{0,2},{2,4},{4,6},{6,8},{8,10},{10,12},{12,14},{14,0},{1,3},{3,5},... | collective-permute-start | bytes 786440 | tf_op jit(solution)/shard_map/ppermute | solution.py:362
  16.2 10.4 %collective-permute-start.10 = (bf16[4,2,128,128]{3,2,1,0:T(8,128)(2,1)S(1)}, bf16[4,2,128,128]{3,2,1,0:T(8,128)(2,1)S(1)}, u32[]{:S(2)}, u32[]{:S(2)}) collective-permute-start(bf16[4,2,128,128]{3,2,1,0:T(8,128)(2,1)S(1)} %get-tuple-element.43.rest_0_.kv_ref), channel_id=1, source_target_pairs={{0,14},{2,0},{4,2},{6,4},{8,6},{10,8},{12,10},{14,12},{1,15},{3,1}... | collective-permute-start | bytes 786440 | tf_op jit(solution)/shard_map/ppermute | solution.py:364
  26.6 8.4 %collective-permute-start.7 = (bf16[4,2,128,128]{3,2,1,0:T(8,128)(2,1)S(1)}, bf16[4,2,128,128]{3,2,1,0:T(8,128)(2,1)S(1)}, u32[]{:S(2)}, u32[]{:S(2)}) collective-permute-start(bf16[4,2,128,128]{3,2,1,0:T(8,128)(2,1)S(1)} %collective-permute-done.6.rest_1_), channel_id=1, source_target_pairs={{0,2},{2,4},{4,6},{6,8},{8,10},{10,12},{12,14},{14,0},{1,3},{3,5},... | collective-permute-start | bytes 786440 | tf_op jit(solution)/shard_map/ppermute | solution.py:362
  26.6 8.3 %collective-permute-start.11 = (bf16[4,2,128,128]{3,2,1,0:T(8,128)(2,1)S(1)}, bf16[4,2,128,128]{3,2,1,0:T(8,128)(2,1)S(1)}, u32[]{:S(2)}, u32[]{:S(2)}) collective-permute-start(bf16[4,2,128,128]{3,2,1,0:T(8,128)(2,1)S(1)} %collective-permute-done.10.rest_7_), channel_id=1, source_target_pairs={{0,14},{2,0},{4,2},{6,4},{8,6},{10,8},{12,10},{14,12},{1,15},{3,1}... | collective-permute-start | bytes 786440 | tf_op jit(solution)/shard_map/ppermute | solution.py:364
  39.7 7.9 %collective-permute-start.4 = (bf16[128,1024]{1,0:T(8,128)(2,1)S(1)}, bf16[128,1024]{1,0:T(8,128)(2,1)S(1)}, u32[]{:S(2)}, u32[]{:S(2)}) collective-permute-start(bf16[128,1024]{1,0:T(8,128)(2,1)S(1)} %copy-done.1), channel_id=1, source_target_pairs={{0,16},{16,0},{1,17},{17,1},{2,18},{18,2},{3,19},{19,3},{4,20},{20... | collective-permute-start | bytes 786440 | tf_op jit(solution)/shard_map/ppermute | solution.py:356
  40.9 12.7 %collective-permute-start.5 = (bf16[128,1024]{1,0:T(8,128)(2,1)S(1)}, bf16[128,1024]{1,0:T(8,128)(2,1)S(1)}, u32[]{:S(2)}, u32[]{:S(2)}) collective-permute-start(bf16[128,1024]{1,0:T(8,128)(2,1)S(1)} %copy-done.1), channel_id=1, source_target_pairs={{0,17},{1,16},{16,1},{17,0},{2,19},{3,18},{18,3},{19,2},{4,21},{5,... | collective-permute-start | bytes 786440 | tf_op jit(solution)/shard_map/ppermute | solution.py:381
  42.3 15.6 %collective-permute-start.9 = (bf16[4,2,128,128]{3,2,1,0:T(8,128)(2,1)S(1)}, bf16[4,2,128,128]{3,2,1,0:T(8,128)(2,1)S(1)}, u32[]{:S(2)}, u32[]{:S(2)}) collective-permute-start(bf16[4,2,128,128]{3,2,1,0:T(8,128)(2,1)S(1)} %collective-permute-done.8.rest_3_), channel_id=1, source_target_pairs={{0,2},{2,4},{4,6},{6,8},{8,10},{10,12},{12,14},{14,0},{1,3},{3,5},... | collective-permute-start | bytes 786440 | tf_op jit(solution)/shard_map/ppermute | solution.py:362
  42.4 12.8 %collective-permute-start.13 = (bf16[4,160,128]{2,1,0:T(8,128)(2,1)S(1)}, bf16[4,160,128]{2,1,0:T(8,128)(2,1)S(1)}, u32[]{:S(2)}, u32[]{:S(2)}) collective-permute-start(bf16[4,160,128]{2,1,0:T(8,128)(2,1)S(1)} %get-tuple-element.45.q_ref.rest_0_), channel_id=1, source_target_pairs={{0,2},{2,4},{4,6},{6,8},{8,10},{10,12},{12,14},{14,0},{1,3},{3,5},... | collective-permute-start | bytes 491528 | tf_op jit(solution)/shard_map/ppermute | solution.py:362
  42.5 12.8 %collective-permute-start.15 = (bf16[4,160,128]{2,1,0:T(8,128)(2,1)S(1)}, bf16[4,160,128]{2,1,0:T(8,128)(2,1)S(1)}, u32[]{:S(2)}, u32[]{:S(2)}) collective-permute-start(bf16[4,160,128]{2,1,0:T(8,128)(2,1)S(1)} %get-tuple-element.45.q_ref.rest_0_), channel_id=1, source_target_pairs={{0,14},{2,0},{4,2},{6,4},{8,6},{10,8},{12,10},{14,12},{1,15},{3,1}... | collective-permute-start | bytes 491528 | tf_op jit(solution)/shard_map/ppermute | solution.py:364
  55.2 11.8 %collective-permute-start.14 = (bf16[4,160,128]{2,1,0:T(8,128)(2,1)S(1)}, bf16[4,160,128]{2,1,0:T(8,128)(2,1)S(1)}, u32[]{:S(2)}, u32[]{:S(2)}) collective-permute-start(bf16[4,160,128]{2,1,0:T(8,128)(2,1)S(1)} %collective-permute-done.13.rest_1_), channel_id=1, source_target_pairs={{0,2},{2,4},{4,6},{6,8},{8,10},{10,12},{12,14},{14,0},{1,3},{3,5},... | collective-permute-start | bytes 491528 | tf_op jit(solution)/shard_map/ppermute | solution.py:362
  55.3 11.7 %collective-permute-start.16 = (bf16[4,160,128]{2,1,0:T(8,128)(2,1)S(1)}, bf16[4,160,128]{2,1,0:T(8,128)(2,1)S(1)}, u32[]{:S(2)}, u32[]{:S(2)}) collective-permute-start(bf16[4,160,128]{2,1,0:T(8,128)(2,1)S(1)} %collective-permute-done.15.rest_7_), channel_id=1, source_target_pairs={{0,14},{2,0},{4,2},{6,4},{8,6},{10,8},{12,10},{14,12},{1,15},{3,1}... | collective-permute-start | bytes 491528 | tf_op jit(solution)/shard_map/ppermute | solution.py:364
  79.7 24.2 %all-to-all-start = ((bf16[64,16,128]{2,1,0:T(8,128)(2,1)}), bf16[64,16,128]{2,1,0:T(8,128)(2,1)S(1)}, u32[]{:S(2)}, u32[]{:S(2)}) async-start(bf16[64,16,128]{2,1,0:T(8,128)(2,1)} %shard_map.164), calls=%async_computation | async-start | bytes 524288 | tf_op jit(solution)/shard_map/all_to_all | solution.py:431
  91.5 8.9 %collective-permute-start.27 = (bf16[4,128,128]{2,1,0:T(8,128)(2,1)S(1)}, bf16[4,128,128]{2,1,0:T(8,128)(2,1)S(1)}, u32[]{:S(2)}, u32[]{:S(2)}) collective-permute-start(bf16[4,128,128]{2,1,0:T(8,128)(2,1)S(1)} %collective-permute-done.26.rest_9_), channel_id=1, source_target_pairs={{0,2},{2,4},{4,6},{6,8},{8,10},{10,12},{12,14},{14,0},{1,3},{3,5},... | collective-permute-start | bytes 393224 | tf_op jit(solution)/shard_map/ppermute | solution.py:362
  94.2 15.6 %collective-permute-start.21 = (bf16[4,160,128]{2,1,0:T(8,128)(2,1)S(1)}, bf16[4,160,128]{2,1,0:T(8,128)(2,1)S(1)}, u32[]{:S(2)}, u32[]{:S(2)}) collective-permute-start(bf16[4,160,128]{2,1,0:T(8,128)(2,1)S(1)} %collective-permute-done.20.rest_3_), channel_id=1, source_target_pairs={{0,2},{2,4},{4,6},{6,8},{8,10},{10,12},{12,14},{14,0},{1,3},{3,5},... | collective-permute-start | bytes 491528 | tf_op jit(solution)/shard_map/ppermute | solution.py:362
  100.4 13.1 %collective-permute-start.28 = (bf16[4,128,128]{2,1,0:T(8,128)(2,1)S(1)}, bf16[4,128,128]{2,1,0:T(8,128)(2,1)S(1)}, u32[]{:S(2)}, u32[]{:S(2)}) collective-permute-start(bf16[4,128,128]{2,1,0:T(8,128)(2,1)S(1)} %collective-permute-done.27.rest_10_), channel_id=1, source_target_pairs={{0,2},{2,4},{4,6},{6,8},{8,10},{10,12},{12,14},{14,0},{1,3},{3,5},... | collective-permute-start | bytes 393224 | tf_op jit(solution)/shard_map/ppermute | solution.py:362
  100.4 35.5 %collective-permute-start.32 = (bf16[4,128,128]{2,1,0:T(8,128)(2,1)S(1)}, bf16[4,128,128]{2,1,0:T(8,128)(2,1)S(1)}, u32[]{:S(2)}, u32[]{:S(2)}) collective-permute-start(bf16[4,128,128]{2,1,0:T(8,128)(2,1)S(1)} %collective-permute-done.31.rest_14_), channel_id=1, source_target_pairs={{0,14},{2,0},{4,2},{6,4},{8,6},{10,8},{12,10},{14,12},{1,15},{3,1}... | collective-permute-start | bytes 393224 | tf_op jit(solution)/shard_map/ppermute | solution.py:364
  104.7 12.0 %all-to-all-start.1 = ((bf16[8,16,128]{2,1,0:T(8,128)(2,1)}), bf16[8,16,128]{2,1,0:T(8,128)(2,1)S(1)}, u32[]{:S(2)}, u32[]{:S(2)}) async-start(bf16[8,16,128]{2,1,0:T(8,128)(2,1)} %shard_map.165), calls=%async_computation.1 | async-start | bytes 65536 | tf_op jit(solution)/shard_map/all_to_all | solution.py:447
  113.5 25.7 %collective-permute-start.29 = (bf16[4,128,128]{2,1,0:T(8,128)(2,1)S(1)}, bf16[4,128,128]{2,1,0:T(8,128)(2,1)S(1)}, u32[]{:S(2)}, u32[]{:S(2)}) collective-permute-start(bf16[4,128,128]{2,1,0:T(8,128)(2,1)S(1)} %collective-permute-done.28.rest_11_), channel_id=1, source_target_pairs={{0,2},{2,4},{4,6},{6,8},{8,10},{10,12},{12,14},{14,0},{1,3},{3,5},... | collective-permute-start | bytes 393224 | tf_op jit(solution)/shard_map/ppermute | solution.py:362
  117.5 18.4 %all-to-all-start.2 = ((bf16[16,8,16,128]{3,2,1,0:T(8,128)(2,1)}), bf16[16,8,16,128]{3,2,1,0:T(8,128)(2,1)S(1)}, u32[]{:S(2)}, u32[]{:S(2)}) async-start(bf16[16,8,16,128]{3,2,1,0:T(8,128)(2,1)} %shard_map.166), calls=%async_computation.2 | async-start | bytes 1048576 | tf_op jit(solution)/shard_map/all_to_all | solution.py:449
  129.2 19.2 %collective-permute-start.23 = (bf16[3,128,128]{2,1,0:T(8,128)(2,1)S(1)}, bf16[3,128,128]{2,1,0:T(8,128)(2,1)S(1)}, u32[]{:S(2)}, u32[]{:S(2)}) collective-permute-start(bf16[3,128,128]{2,1,0:T(8,128)(2,1)S(1)} %get-tuple-element.53), channel_id=1, source_target_pairs={{0,1},{1,0},{2,3},{3,2},{4,5},{5,4},{6,7},{7,6},{8,9},{9,8},{10,11... | collective-permute-start | bytes 294920 | tf_op jit(solution)/shard_map/ppermute | solution.py:356
  134.2 14.7 %collective-permute-start.24 = (bf16[3,128,128]{2,1,0:T(8,128)(2,1)S(1)}, bf16[3,128,128]{2,1,0:T(8,128)(2,1)S(1)}, u32[]{:S(2)}, u32[]{:S(2)}) collective-permute-start(bf16[3,128,128]{2,1,0:T(8,128)(2,1)S(1)} %get-tuple-element.54), channel_id=1, source_target_pairs={{0,16},{16,0},{1,17},{17,1},{2,18},{18,2},{3,19},{19,3},{4,20},{20... | collective-permute-start | bytes 294920 | tf_op jit(solution)/shard_map/ppermute | solution.py:356
  135.8 14.7 %collective-permute-start.25 = (bf16[3,128,128]{2,1,0:T(8,128)(2,1)S(1)}, bf16[3,128,128]{2,1,0:T(8,128)(2,1)S(1)}, u32[]{:S(2)}, u32[]{:S(2)}) collective-permute-start(bf16[3,128,128]{2,1,0:T(8,128)(2,1)S(1)} %get-tuple-element.55), channel_id=1, source_target_pairs={{0,17},{1,16},{16,1},{17,0},{2,19},{3,18},{18,3},{19,2},{4,21},{5,... | collective-permute-start | bytes 294920 | tf_op jit(solution)/shard_map/ppermute | solution.py:381
  135.9 18.8 %collective-permute-start.36 = (bf16[16,8,16,128]{3,2,1,0:T(8,128)(2,1)S(1)}, bf16[16,8,16,128]{3,2,1,0:T(8,128)(2,1)S(1)}, u32[]{:S(2)}, u32[]{:S(2)}) collective-permute-start(bf16[16,8,16,128]{3,2,1,0:T(8,128)(2,1)S(1)} %all-to-all-done.2.own_ref), channel_id=1, source_target_pairs={{0,1},{1,0},{2,3},{3,2},{4,5},{5,4},{6,7},{7,6},{8,9},{9,8},{10,11... | collective-permute-start | bytes 1572872 | tf_op jit(solution)/shard_map/ppermute | solution.py:356
  (48 other events, 610.6 us)
where the time goes:
time: 156 us
  starting transfers between devices  74.9 us (48%)
  waiting for transfers between devices  44.3 us (28%)
  Pallas kernels  31.2 us (20%)
  local copies, waits for them, and re-layouts  2.96 us (2%)
  matrix products  1.63 us (1%)
    pallas_call x14, Pallas kernels, call(): pl.pallas_call(kernel, in_specs=[spec for spec, _ in ins], out_specs=[VM]...  31.2 us
    ppermute x9, starting transfers between devices, ring(): lax.ppermute(down[-1], 'z', [(i, (i + 7) % 8) for i in range(8)])  24 us
    ppermute x12, waiting for transfers between devices, ring(): up.append(lax.ppermute(up[-1], 'z', [(i, (i + 1) % 8) for i in range(8)]))  21.7 us
    ppermute x11, starting transfers between devices, flip(): return lax.ppermute(array, axis, [(0, 1), (1, 0)])  19.5 us
    ppermute x5, waiting for transfers between devices, swap(): lax.ppermute(pieces[3], ('xl', 'core'), [(i, 3 - i) for i in range(4)])  13.2 us
    all_to_all x1, starting transfers between devices, body(): lax.all_to_all(after(gw, qps[3], qps[5], das[1], das[7]), ('xh', 'y', 'z'...  11.7 us
    ppermute x11, waiting for transfers between devices, flip(): return lax.ppermute(array, axis, [(0, 1), (1, 0)])  7.1 us
    all_to_all x1, starting transfers between devices, body(): lax.all_to_all(lines, ('xh', 'y', 'xl'), split_axis=0, concat_axis=0, til...  6.68 us
  transfers between devices with their start and end apart: 40, of which 15 were waited for; matrix products, arithmetic and copies ran while one was open for 0% of the time, Pallas kernels for 18%

commit v1 on v0

--- a/solution.py
+++ b/solution.py
@@ -70,20 +70,34 @@
     return pl.ds(pl.multiple_of((xl * 2 + core) * 128, 128), 128)
 
 
-def pack_kernel(k_ref, v_ref, q_ref, g_ref, t_ref, o0, o1, o2, o3, rows, sems):
+def pack_kernel(
+    k_ref, v_ref, q_ref, g_ref, i_ref, w_ref, o0, o1, o2, o3, rows, items, weight, side, sems
+):
     copies = [
-        pltpu.make_async_copy(ref, rows.at[i], sems.at[i])
-        for i, ref in enumerate((k_ref, v_ref, q_ref, g_ref))
+        pltpu.make_async_copy(ref, to, sems.at[i])
+        for i, (ref, to) in enumerate(
+            (
+                (k_ref, rows.at[0]),
+                (v_ref, rows.at[1]),
+                (q_ref, rows.at[2]),
+                (g_ref, rows.at[3]),
+                (i_ref, items),
+                (w_ref, weight),
+            )
+        )
     ]
     for copy in copies:
         copy.start()
     outs = (o0, o1, o2, o3)
-    for d, out in enumerate(outs):
-        out[512:] = t_ref[:, head_columns(d)]
-    for i, copy in enumerate(copies):
-        copy.wait()
+    for i in range(4):
+        copies[i].wait()
         for d, out in enumerate(outs):
             out[i * 128 : i * 128 + 128] = rows[i, :, head_columns(d)]
+    copies[4].wait()
+    copies[5].wait()
+    side[...] = dot(items[...], weight[...], 1, 1).astype(BF16)
+    for d, out in enumerate(outs):
+        out[512:] = side[:, head_columns(d)]
 
 
 def mixed_grad_kernel(c0, c1, c2, c3, w_ref, gm_ref, wbuf, sem):
@@ -105,32 +119,67 @@
         gate_ref[d] = piece[384:512]
 
 
-def forward_kernel(ub, tl, pk, q_ref, gate_ref, gm_ref, *rest):
-    chunks, (att_ref, stat_ref), (kv, inv, sems) = rest[:8], rest[8:10], rest[10:]
-    copies = load_chunks(chunks, kv, sems)
+def masked_step(query, kv, spots, reach, acc):
+    keys = jnp.concatenate([kv[p, 0] for p in spots], axis=0)
+    values = jnp.concatenate([kv[p, 1] for p in spots], axis=0)
+    row = iota((128, 128), 0) - iota((128, 128), 1)
+    logits = dot(query, keys, 1, 1) * SCALE
+    silu = logits / (1.0 + jnp.exp(-logits))
+    weights = [
+        jnp.where(row >= reach[i] * 128, silu[:, i * 128 : i * 128 + 128], 0.0).astype(BF16)
+        for i in range(4)
+    ]
+    return acc + dot(jnp.concatenate(weights, axis=1), values, 1, 0)
+
+
+def forward_near_kernel(ub, tl, pk, q_ref, *rest):
+    chunks, (att_ref,), (kv, inv, sems) = rest[:7], rest[7:8], rest[8:]
+    copies = [
+        pltpu.make_async_copy(ref, kv.at[pl.ds(4 * c, 4)], sems.at[c])
+        for c, ref in zip((0, 1, 2, 3, 5, 6, 7), chunks)
+    ]
+    for copy in copies:
+        copy.start()
     fill_places(pk, inv)
     for copy in copies:
         copy.wait()
-    row = iota((128, 512), 0)
-    col = iota((128, 512), 1)
+
+    def one(slot, carry):
+        logical = pk[0, slot_of(slot)]
+        first = user_of(ub, tl, logical)[1]
+        own = logical - first
+        query = q_ref[slot, :128]
+
+        def step(j, acc):
+            spots, reach = [], []
+            for i in range(4):
+                entry = 4 * j + i
+                place = inv[first + jnp.minimum(entry, own)]
+                late = (place // 4 == 4) | (entry > own)
+                spots.append(jnp.where(late, 0, place))
+                reach.append(jnp.where(late, 1, jnp.where(entry == own, 0, -1)))
+            return masked_step(query, kv, spots, reach, acc)
+
+        att_ref[slot] = lax.fori_loop(0, own // 4 + 1, step, jnp.zeros((128, 128), F32))
+        return carry
+
+    lax.fori_loop(0, 4, one, 0)
+
+
+def forward_far_kernel(
+    ub, tl, pk, q_ref, gate_ref, gm_ref, near_ref, kv, att_ref, stat_ref
+):
     lane = iota((128, 128), 1)
 
     def one(slot, carry):
         logical = pk[0, slot_of(slot)]
         user, first, blocks, tail = user_of(ub, tl, logical)
         own = logical - first
-        query = q_ref[slot, :128]
-
-        def step(j, acc):
-            places = [inv[first + jnp.minimum(4 * j + i, own)] for i in range(4)]
-            keys = jnp.concatenate([kv[p, 0] for p in places], axis=0)
-            values = jnp.concatenate([kv[p, 1] for p in places], axis=0)
-            logits = dot(query, keys, 1, 1) * SCALE
-            silu = logits / (1.0 + jnp.exp(-logits))
-            weights = jnp.where(col + (4 * j - own) * 128 <= row, silu, 0.0).astype(BF16)
-            return acc + dot(weights, values, 1, 0)
-
-        acc = lax.fori_loop(0, own // 4 + 1, step, jnp.zeros((128, 128), F32))
+        reach = []
+        for i in range(4):
+            other = pk[0, slot_of(16 + i)]
+            reach.append(jnp.where((other >= first) & (other < logical), -1, 1))
+        acc = masked_step(q_ref[slot, :128], kv, range(4), reach, near_ref[slot])
         limit = jnp.where(own == blocks - 1, tail, 128)
         valid = iota((128, 128), 0) < limit
         att = jnp.where(valid, acc, 0.0)
@@ -217,7 +266,7 @@
         sc_ref[slot] = dot(mixed_ref[pl.ds(slot * 128, 128), :], chosen, 1, 0).astype(BF16)
 
 
-def query_kernel(ub, tl, pk, q_ref, da_ref, gg_ref, sc_ref, *rest):
+def query_kernel(ub, tl, pk, q_ref, da_ref, gg_ref, *rest):
     chunks, outs, (kv, gq, inv, sems) = rest[:8], rest[8:12], rest[12:]
     copies = load_chunks(chunks, kv, sems)
     fill_places(pk, inv)
@@ -252,10 +301,9 @@
     for slot in range(4):
         outs[slot][0] = gq[slot]
         outs[slot][1] = gg_ref[slot]
-        outs[slot][2] = sc_ref[slot]
-
-
-def key_kernel(ub, tl, pk, kv_ref, *rest):
+
+
+def key_kernel(ub, tl, pk, kv_ref, sc_ref, *rest):
     qs, das, outs, (qbuf, dbuf, both, inv, qsems, dsems) = (
         rest[:8], rest[8:16], rest[16:20], rest[20:],
     )
@@ -297,22 +345,23 @@
 
     lax.fori_loop(0, 4, one, 0)
     for slot in range(4):
-        outs[slot][...] = both[slot]
-
-
-def unpack_early_kernel(p0, p1, p2, p3, gq_ref, gg_ref, sc_ref):
-    scores = jnp.zeros((128, 128), F32)
+        outs[slot][:2] = both[slot]
+        outs[slot][2] = sc_ref[slot]
+
+
+def unpack_early_kernel(p0, p1, p2, p3, gq_ref, gg_ref):
     for d, piece in enumerate((p0, p1, p2, p3)):
         gq_ref[:, head_columns(d)] = piece[0]
         gg_ref[:, head_columns(d)] = piece[1]
-        scores = scores + piece[2].astype(F32)
-    sc_ref[...] = scores
-
-
-def unpack_late_kernel(p0, p1, p2, p3, gk_ref, gv_ref):
+
+
+def unpack_late_kernel(p0, p1, p2, p3, gk_ref, gv_ref, sc_ref):
+    scores = jnp.zeros((128, 128), F32)
     for d, piece in enumerate((p0, p1, p2, p3)):
         gk_ref[:, head_columns(d)] = piece[0]
         gv_ref[:, head_columns(d)] = piece[1]
+        scores = scores + piece[2].astype(F32)
+    sc_ref[...] = scores
 
 
 def sum_kernel(parts_ref, out_ref):
@@ -356,13 +405,22 @@
     return lax.ppermute(array, axis, [(0, 1), (1, 0)])
 
 
-def ring(array):
-    up, down = [array], [array]
-    for step in range(4):
-        up.append(lax.ppermute(up[-1], "z", [(i, (i + 1) % 8) for i in range(8)]))
-        if step < 3:
-            down.append(lax.ppermute(down[-1], "z", [(i, (i + 7) % 8) for i in range(8)]))
-    return up + down[:0:-1]
+def up(array):
+    return lax.ppermute(array, "z", [(i, (i + 1) % 8) for i in range(8)])
+
+
+def down(array):
+    return lax.ppermute(array, "z", [(i, (i + 7) % 8) for i in range(8)])
+
+
+def ring(array, hold):
+    ups, downs = [array], [array]
+    for n in range(4):
+        waits = hold(n)
+        ups.append(up(after(ups[-1], *waits) if waits else ups[-1]))
+        if n < 3:
+            downs.append(down(after(downs[-1], *waits) if waits else downs[-1]))
+    return ups + downs[:0:-1]
 
 
 def after(value, *waits):
@@ -390,12 +448,17 @@
     places = pltpu.SMEM((32,), I32)
     sems = pltpu.SemaphoreType.DMA((8,))
     kv_buffer = pltpu.VMEM((32, 2, 128, 128), BF16)
-    table = dot(items, out_weight, 1, 1).astype(BF16)
     packed = call(
         pack_kernel,
-        raw([key, value, query, gate]) + vm(table),
+        raw([key, value, query, gate, items, out_weight]),
         [((544, 128), BF16)] * 4,
-        [pltpu.VMEM((4, 128, 512), BF16), pltpu.SemaphoreType.DMA((4,))],
+        [
+            pltpu.VMEM((4, 128, 512), BF16),
+            pltpu.VMEM((32, 1024), BF16),
+            pltpu.VMEM((512, 1024), BF16),
+            pltpu.VMEM((32, 512), BF16),
+            pltpu.SemaphoreType.DMA((6,)),
+        ],
     )
     first = swap(packed)
     kv, qp, gate_h = call(
@@ -403,22 +466,27 @@
         vm(*first),
         [((4, 2, 128, 128), BF16), ((4, 160, 128), BF16), (block, BF16)],
     )
-    kvs = ring(kv)
-    cots = [cotangent] + swap([after(cotangent, packed[0])] * 4)[1:]
+    cots = [cotangent] + swap([after(cotangent, first[2])] * 4)[1:]
+    kvs = ring(kv, lambda n: cots[1:] if n == 2 else [])
     (gm,) = call(
         mixed_grad_kernel,
         vm(*cots) + raw([out_weight]),
         [(block, F32)],
         [pltpu.VMEM((128, 1024), BF16), pltpu.SemaphoreType.DMA],
     )
-    att, stats = call(
-        forward_kernel,
-        facts + vm(qp, gate_h, gm) + raw(kvs),
-        [(block, F32), ((4, 8, 128), F32)],
+    (att_near,) = call(
+        forward_near_kernel,
+        facts + vm(qp) + raw(kvs[:4] + kvs[5:]),
+        [(block, F32)],
         [kv_buffer, places, sems],
         us=6,
     )
-    qps = ring(after(qp, kvs[3], kvs[5]))
+    att, stats = call(
+        forward_far_kernel,
+        facts + vm(qp, gate_h, gm, att_near, kvs[4]),
+        [(block, F32), ((4, 8, 128), F32)],
+    )
+    qps = ring(after(qp, kvs[3], kvs[5]), lambda n: [])
     stats = after(stats, qps[1], qps[7])
     all_stats = swap([stats] * 4)
     da, gg, mixed = call(
@@ -426,31 +494,48 @@
         facts + vm(after(att, qps[2], qps[6]), *all_stats, gate_h, gm),
         [(block, BF16), (block, BF16), ((512, 128), BF16)],
     )
-    das = ring(da)
     (gw,) = call(weight_kernel, vm(mixed, *cots), [((64, 16, 128), BF16)])
-    parts = lax.all_to_all(after(gw, qps[3], qps[5], das[1], das[7]), ("xh", "y", "z"), split_axis=0, concat_axis=0, tiled=True)
+    early = call(
+        query_kernel,
+        facts + vm(qp, da, gg) + raw(kvs),
+        [((2, 128, 128), BF16)] * 4,
+        [kv_buffer, pltpu.VMEM(block, BF16), places, sems],
+        us=6,
+    )
+    first_up, first_down = up(da), down(da)
+    parts = lax.all_to_all(
+        after(gw, qps[3], qps[5], first_up, first_down),
+        ("xh", "y", "z"),
+        split_axis=0,
+        concat_axis=0,
+        tiled=True,
+    )
+    ups, downs = [da, first_up, up(first_up)], [da, first_down, down(first_down)]
+    (piece,) = call(
+        sum_kernel, vm(after(parts, ups[2], downs[2], early[0])), [((8, 16, 128), BF16)]
+    )
+    ups.append(up(after(ups[2], early[0])))
+    downs.append(down(after(downs[2], early[0])))
+    ups.append(up(ups[3]))
+    das = ups + downs[:0:-1]
     (sc,) = call(
         score_kernel,
         facts + vm(mixed, cand_ids[0]) + raw(qps),
         [(block, BF16)],
         [pltpu.VMEM((32, 160, 128), BF16), sems],
     )
-    early = call(
-        query_kernel,
-        facts + vm(qp, da, gg, sc) + raw(kvs),
-        [((3, 128, 128), BF16)] * 4,
-        [kv_buffer, pltpu.VMEM(block, BF16), places, sems],
-        us=6,
-    )
     early = swap(early)
-    (piece,) = call(sum_kernel, vm(parts), [((8, 16, 128), BF16)])
     line = lax.all_to_all(piece, "z", split_axis=0, concat_axis=0, tiled=True)
-    (lines,) = call(spread_kernel, vm(line), [((16, 8, 16, 128), BF16)])
-    near = lax.all_to_all(lines, ("xh", "y", "xl"), split_axis=0, concat_axis=0, tiled=True)
+    (lines,) = call(
+        spread_kernel, vm(after(line, ups[3], downs[3], sc)), [((16, 8, 16, 128), BF16)]
+    )
+    near = lax.all_to_all(
+        after(lines, ups[4]), ("xh", "y", "xl"), split_axis=0, concat_axis=0, tiled=True
+    )
     late = call(
         key_kernel,
-        facts + vm(kv) + raw(qps) + raw(das),
-        [((2, 128, 128), BF16)] * 4,
+        facts + vm(kv, sc) + raw(qps) + raw(das),
+        [((3, 128, 128), BF16)] * 4,
         [
             pltpu.VMEM((32, 160, 128), BF16),
             pltpu.VMEM((32, 128, 128), BF16),
@@ -463,13 +548,13 @@
         mib=12,
     )
     late = swap(late)
-    far = flip(near, "core")
+    far = flip(after(near, late[0]), "core")
     (gow,) = call(assemble_kernel, vm(near, far), [((512, 1024), F32)])
     rows = (128, 512)
-    gq, gg, scores = call(
-        unpack_early_kernel, vm(*early), [(rows, BF16), (rows, BF16), ((128, 128), F32)]
-    )
-    gk, gv = call(unpack_late_kernel, vm(*late), [(rows, BF16)] * 2)
+    gq, gg = call(unpack_early_kernel, vm(*early), [(rows, BF16)] * 2)
+    gk, gv, scores = call(
+        unpack_late_kernel, vm(*late), [(rows, BF16), (rows, BF16), ((128, 128), F32)]
+    )
     return (scores, gq, gk, gv, gg, gow)
 
 

time: 156 us -> 145 us (0.929)
  waiting for transfers between devices: 44.3 us -> 35.4 us
  Pallas kernels: 31.2 us -> 35.3 us
  starting transfers between devices: 74.9 us -> 72.3 us
  local copies, waits for them, and re-layouts: 2.96 us -> 0.78 us
  matrix products: 1.63 us -> 0 us
    ppermute x21, waiting for transfers between devices: 21.7 us -> 12.9 us  [the longest x12 12.9 us: up(): return lax.ppermute(array, 'z', [(i, (i + 1) % 8) for i in range(8)])]
    ppermute x11, waiting for transfers between devices: 7.1 us -> 1.77 us  [flip(): return lax.ppermute(array, axis, [(0, 1), (1, 0)])]
    pallas_call x14 -> x15, Pallas kernels: 31.2 us -> 35.3 us  [call(): pl.pallas_call(kernel, in_specs=[spec for spec, _ in ins], out_specs=[VM]...]
    ppermute x11, starting transfers between devices: 19.5 us -> 15.8 us  [flip(): return lax.ppermute(array, axis, [(0, 1), (1, 0)])]
    all_to_all x2, waiting for transfers between devices: 0.89 us -> 3.76 us  [the longest x1 2.76 us: body(): lax.all_to_all(after(gw, qps[3], qps[5], first_up, first_down), ('xh', 'y...]
    ppermute x5, starting transfers between devices: 4.47 us -> 6.97 us  [swap(): lax.ppermute(pieces[3], ('xl', 'core'), [(i, 3 - i) for i in range(4)])]
    ppermute x5, waiting for transfers between devices: 13.2 us -> 15.4 us  [swap(): lax.ppermute(pieces[3], ('xl', 'core'), [(i, 3 - i) for i in range(4)])]
    unnamed x64 -> x60, local copies, waits for them, and re-layouts: 2.96 us -> 0.78 us
  transfers between devices with their start and end apart: 40 -> 40, of which waited for: 15 -> 16; matrix products, arithmetic and copies ran while one was open for 0% -> 0% of each run, Pallas kernels for 18% -> 21%
where the time goes in v1:
time: 145 us
  starting transfers between devices  72.3 us (50%)
  waiting for transfers between devices  35.4 us (24%)
  Pallas kernels  35.3 us (24%)
    pallas_call x15, Pallas kernels, call(): pl.pallas_call(kernel, in_specs=[spec for spec, _ in ins], out_specs=[VM]...  35.3 us
    ppermute x9, starting transfers between devices, down(): return lax.ppermute(array, 'z', [(i, (i + 7) % 8) for i in range(8)])  20 us
    ppermute x11, starting transfers between devices, flip(): return lax.ppermute(array, axis, [(0, 1), (1, 0)])  15.8 us
    ppermute x5, waiting for transfers between devices, swap(): lax.ppermute(pieces[3], ('xl', 'core'), [(i, 3 - i) for i in range(4)])  15.4 us
    ppermute x12, waiting for transfers between devices, up(): return lax.ppermute(array, 'z', [(i, (i + 1) % 8) for i in range(8)])  12.9 us
    all_to_all x1, starting transfers between devices, body(): lax.all_to_all(after(gw, qps[3], qps[5], first_up, first_down), ('xh', 'y...  11.5 us
    ppermute x12, starting transfers between devices, up(): return lax.ppermute(array, 'z', [(i, (i + 1) % 8) for i in range(8)])  8.56 us
    ppermute x5, starting transfers between devices, swap(): lax.ppermute(pieces[3], ('xl', 'core'), [(i, 3 - i) for i in range(4)])  6.97 us
  transfers between devices with their start and end apart: 40, of which 16 were waited for; matrix products, arithmetic and copies ran while one was open for 0% of the time, Pallas kernels for 21%

profile of v1, /device:TPU:1, one launch (start us, length us, event | category | flops | bytes accessed | tf_op | source)
XLA Modules:
  0.0 144.8 jit_solution(13928364817538169554)
XLA Ops:
  7.6 5.5 %collective-permute-done.2.p3 = bf16[544,128]{1,0:T(8,128)(2,1)S(1)} collective-permute-done((bf16[544,128]{1,0:T(8,128)(2,1)S(1)}, bf16[544,128]{1,0:T(8,128)(2,1)S(1)}, u32[]{:S(2)}, u32[]{:S(2)}) %collective-permute-start.2) | collective-permute-done | bytes 139296 | tf_op jit(solution)/shard_map/ppermute | solution.py:439
  13.8 4.0 %collective-permute-start.9 = (bf16[4,2,128,128]{3,2,1,0:T(8,128)(2,1)S(1)}, bf16[4,2,128,128]{3,2,1,0:T(8,128)(2,1)S(1)}, u32[]{:S(2)}, u32[]{:S(2)}) collective-permute-start(bf16[4,2,128,128]{3,2,1,0:T(8,128)(2,1)S(1)} %get-tuple-element.48.rest_0_.kv_ref), channel_id=1, source_target_pairs={{0,14},{2,0},{4,2},{6,4},{8,6},{10,8},{12,10},{14,12},{1,15},{3,1}... | collective-permute-start | bytes 786440 | tf_op jit(solution)/shard_map/ppermute | solution.py:413
  19.9 4.5 %collective-permute-done.6.rest_1_ = bf16[4,2,128,128]{3,2,1,0:T(8,128)(2,1)S(1)} collective-permute-done((bf16[4,2,128,128]{3,2,1,0:T(8,128)(2,1)S(1)}, bf16[4,2,128,128]{3,2,1,0:T(8,128)(2,1)S(1)}, u32[]{:S(2)}, u32[]{:S(2)}) %collective-permute-start.6) | collective-permute-done | bytes 262176 | tf_op jit(solution)/shard_map/ppermute | solution.py:409
  24.4 2.7 %collective-permute-start.10 = (bf16[4,2,128,128]{3,2,1,0:T(8,128)(2,1)S(1)}, bf16[4,2,128,128]{3,2,1,0:T(8,128)(2,1)S(1)}, u32[]{:S(2)}, u32[]{:S(2)}) collective-permute-start(bf16[4,2,128,128]{3,2,1,0:T(8,128)(2,1)S(1)} %collective-permute-done.9.rest_6_.rest_7_), channel_id=1, source_target_pairs={{0,14},{2,0},{4,2},{6,4},{8,6},{10,8},{12,10},{14,12},{1,15},{3,1}... | collective-permute-start | bytes 786440 | tf_op jit(solution)/shard_map/ppermute | solution.py:413
  27.1 4.6 %collective-permute-done.5.c3 = bf16[128,1024]{1,0:T(8,128)(2,1)S(1)} collective-permute-done((bf16[128,1024]{1,0:T(8,128)(2,1)S(1)}, bf16[128,1024]{1,0:T(8,128)(2,1)S(1)}, u32[]{:S(2)}, u32[]{:S(2)}) %collective-permute-start.5) | collective-permute-done | bytes 262176 | tf_op jit(solution)/shard_map/ppermute | solution.py:439
  33.1 2.7 %collective-permute-start.11 = (bf16[4,2,128,128]{3,2,1,0:T(8,128)(2,1)S(1)}, bf16[4,2,128,128]{3,2,1,0:T(8,128)(2,1)S(1)}, u32[]{:S(2)}, u32[]{:S(2)}) collective-permute-start(bf16[4,2,128,128]{3,2,1,0:T(8,128)(2,1)S(1)} %collective-permute-done.10.rest_5_.rest_6_), channel_id=1, source_target_pairs={{0,14},{2,0},{4,2},{6,4},{8,6},{10,8},{12,10},{14,12},{1,15},{3,1}... | collective-permute-start | bytes 786440 | tf_op jit(solution)/shard_map/ppermute | solution.py:413
  37.3 3.6 %collective-permute-done.8.rest_3_ = bf16[4,2,128,128]{3,2,1,0:T(8,128)(2,1)S(1)} collective-permute-done((bf16[4,2,128,128]{3,2,1,0:T(8,128)(2,1)S(1)}, bf16[4,2,128,128]{3,2,1,0:T(8,128)(2,1)S(1)}, u32[]{:S(2)}, u32[]{:S(2)}) %collective-permute-start.8) | collective-permute-done | bytes 262176 | tf_op jit(solution)/shard_map/ppermute | solution.py:409
  41.0 2.7 %collective-permute-start.15 = (bf16[4,160,128]{2,1,0:T(8,128)(2,1)S(1)}, bf16[4,160,128]{2,1,0:T(8,128)(2,1)S(1)}, u32[]{:S(2)}, u32[]{:S(2)}) collective-permute-start(bf16[4,160,128]{2,1,0:T(8,128)(2,1)S(1)} %get-tuple-element.55.q_ref.rest_0_), channel_id=1, source_target_pairs={{0,14},{2,0},{4,2},{6,4},{8,6},{10,8},{12,10},{14,12},{1,15},{3,1}... | collective-permute-start | bytes 491528 | tf_op jit(solution)/shard_map/ppermute | solution.py:413
  43.7 5.4 %shard_map.157.near_ref = f32[4,128,128]{2,1,0:T(8,128)S(1)} custom-call(s32[1,4]{1,0:T(1,128)S(1)} %copy-done.7, s32[1,4]{1,0:T(1,128)S(1)} %copy-done.8, s32[1,32]{1,0:T(1,128)S(1)} %copy-done.9, bf16[4,160,128]{2,1,0:T(8,128)(2,1)S(1)} %get-tuple-element.55.q_ref.rest_0_, bf16[4,2,128,128]{3,2,1,0:T(8,128)(2,1)} %copy-done.1, ...), custom_call_target="tpu_custom_call" | custom-call | flops 6000000000 | bytes 6000000 | tf_op jit(solution)/shard_map/pallas_call | solution.py:391
  49.1 2.5 %collective-permute-start.14 = (bf16[4,160,128]{2,1,0:T(8,128)(2,1)S(1)}, bf16[4,160,128]{2,1,0:T(8,128)(2,1)S(1)}, u32[]{:S(2)}, u32[]{:S(2)}) collective-permute-start(bf16[4,160,128]{2,1,0:T(8,128)(2,1)S(1)} %collective-permute-done.13.rest_1_), channel_id=1, source_target_pairs={{0,2},{2,4},{4,6},{6,8},{8,10},{10,12},{12,14},{14,0},{1,3},{3,5},... | collective-permute-start | bytes 491528 | tf_op jit(solution)/shard_map/ppermute | solution.py:409
  53.2 2.8 %shard_map.158 = (f32[4,128,128]{2,1,0:T(8,128)S(1)}, f32[4,8,128]{2,1,0:T(8,128)S(1)}) custom-call(s32[1,4]{1,0:T(1,128)S(1)} %copy-done.7, s32[1,4]{1,0:T(1,128)S(1)} %copy-done.8, s32[1,32]{1,0:T(1,128)S(1)} %copy-done.9, bf16[4,160,128]{2,1,0:T(8,128)(2,1)S(1)} %get-tuple-element.55.q_ref.rest_0_, bf16[4,128,128]{2,1,0:T(8,128)(2,1)S(1)} %get-tuple-element.50.gate_ref, ...), custom_call_target="tpu_custom_call" | custom-call | flops 2000000000 | bytes 2000000 | tf_op jit(solution)/shard_map/pallas_call | solution.py:391
  56.1 3.9 %collective-permute-start.17 = (f32[4,8,128]{2,1,0:T(8,128)S(1)}, f32[4,8,128]{2,1,0:T(8,128)S(1)}, u32[]{:S(2)}, u32[]{:S(2)}) collective-permute-start(f32[4,8,128]{2,1,0:T(8,128)S(1)} %get-tuple-element.58.s0), channel_id=1, source_target_pairs={{0,1},{1,0},{2,3},{3,2},{4,5},{5,4},{6,7},{7,6},{8,9},{9,8},{10,11... | collective-permute-start | bytes 49160 | tf_op jit(solution)/shard_map/ppermute | solution.py:405
  67.8 2.7 %collective-permute-start.22 = (bf16[4,160,128]{2,1,0:T(8,128)(2,1)S(1)}, bf16[4,160,128]{2,1,0:T(8,128)(2,1)S(1)}, u32[]{:S(2)}, u32[]{:S(2)}) collective-permute-start(bf16[4,160,128]{2,1,0:T(8,128)(2,1)S(1)} %collective-permute-done.16.rest_6_), channel_id=1, source_target_pairs={{0,14},{2,0},{4,2},{6,4},{8,6},{10,8},{12,10},{14,12},{1,15},{3,1}... | collective-permute-start | bytes 491528 | tf_op jit(solution)/shard_map/ppermute | solution.py:413
  71.7 2.7 %collective-permute-start.28 = (bf16[4,128,128]{2,1,0:T(8,128)(2,1)S(1)}, bf16[4,128,128]{2,1,0:T(8,128)(2,1)S(1)}, u32[]{:S(2)}, u32[]{:S(2)}) collective-permute-start(bf16[4,128,128]{2,1,0:T(8,128)(2,1)S(1)} %collective-permute-done.27.rest_15_), channel_id=1, source_target_pairs={{0,14},{2,0},{4,2},{6,4},{8,6},{10,8},{12,10},{14,12},{1,15},{3,1}... | collective-permute-start | bytes 393224 | tf_op jit(solution)/shard_map/ppermute | solution.py:413
  74.4 11.5 %all-to-all-start = ((bf16[64,16,128]{2,1,0:T(8,128)(2,1)}), bf16[64,16,128]{2,1,0:T(8,128)(2,1)S(1)}, u32[]{:S(2)}, u32[]{:S(2)}) async-start(bf16[64,16,128]{2,1,0:T(8,128)(2,1)} %shard_map.165), calls=%async_computation | async-start | bytes 524288 | tf_op jit(solution)/shard_map/all_to_all | solution.py:506
  86.0 5.8 %shard_map.161 = (bf16[2,128,128]{2,1,0:T(8,128)(2,1)S(1)}, bf16[2,128,128]{2,1,0:T(8,128)(2,1)S(1)}, bf16[2,128,128]{2,1,0:T(8,128)(2,1)S(1)}, bf16[2,128,128]{2,1,0:T(8,128)(2,1)S(1)}) custom-call(s32[1,4]{1,0:T(1,128)S(1)} %copy-done.7, s32[1,4]{1,0:T(1,128)S(1)} %copy-done.8, s32[1,32]{1,0:T(1,128)S(1)} %copy-done.9, ...), custom_call_target="tpu_custom_call" | custom-call | flops 6000000000 | bytes 6000000 | tf_op jit(solution)/shard_map/pallas_call | solution.py:391
  91.9 2.4 %collective-permute-start.21 = (bf16[4,160,128]{2,1,0:T(8,128)(2,1)S(1)}, bf16[4,160,128]{2,1,0:T(8,128)(2,1)S(1)}, u32[]{:S(2)}, u32[]{:S(2)}) collective-permute-start(bf16[4,160,128]{2,1,0:T(8,128)(2,1)S(1)} %collective-permute-done.20.rest_3_), channel_id=1, source_target_pairs={{0,2},{2,4},{4,6},{6,8},{8,10},{10,12},{12,14},{14,0},{1,3},{3,5},... | collective-permute-start | bytes 491528 | tf_op jit(solution)/shard_map/ppermute | solution.py:409
  95.7 2.8 %all-to-all-done.parts_ref = bf16[64,16,128]{2,1,0:T(8,128)(2,1)S(1)} async-done(((bf16[64,16,128]{2,1,0:T(8,128)(2,1)}), bf16[64,16,128]{2,1,0:T(8,128)(2,1)S(1)}, u32[]{:S(2)}, u32[]{:S(2)}) %all-to-all-start) | async-done | bytes 262176 | tf_op jit(solution)/shard_map/all_to_all | solution.py:506
  99.2 3.6 %all-to-all-start.1 = ((bf16[8,16,128]{2,1,0:T(8,128)(2,1)}), bf16[8,16,128]{2,1,0:T(8,128)(2,1)S(1)}, u32[]{:S(2)}, u32[]{:S(2)}) async-start(bf16[8,16,128]{2,1,0:T(8,128)(2,1)} %shard_map.166), calls=%async_computation.1 | async-start | bytes 65536 | tf_op jit(solution)/shard_map/all_to_all | solution.py:528
  103.4 3.0 %shard_map.160.sc_ref = bf16[4,128,128]{2,1,0:T(8,128)(2,1)S(1)} custom-call(s32[1,4]{1,0:T(1,128)S(1)} %copy-done.7, s32[1,4]{1,0:T(1,128)S(1)} %copy-done.8, s32[1,32]{1,0:T(1,128)S(1)} %copy-done.9, bf16[512,128]{1,0:T(8,128)(2,1)S(1)} %get-tuple-element.59.mixed_ref, s32[4,128]{1,0:T(4,128)S(1)} %bitcast.1, bf16[4,160,128]{2,1,0:T(8,128)(2,1)} %copy-done.4, ...), custom_call_target="tpu_custom_call" | custom-call | flops 2000000000 | bytes 2000000 | tf_op jit(solution)/shard_map/pallas_call | solution.py:391
  112.1 5.9 %all-to-all-start.2 = ((bf16[16,8,16,128]{3,2,1,0:T(8,128)(2,1)}), bf16[16,8,16,128]{3,2,1,0:T(8,128)(2,1)S(1)}, u32[]{:S(2)}, u32[]{:S(2)}) async-start(bf16[16,8,16,128]{3,2,1,0:T(8,128)(2,1)} %shard_map.167), calls=%async_computation.2 | async-start | bytes 1048576 | tf_op jit(solution)/shard_map/all_to_all | solution.py:532
  118.0 8.0 %shard_map.162 = (bf16[3,128,128]{2,1,0:T(8,128)(2,1)S(1)}, bf16[3,128,128]{2,1,0:T(8,128)(2,1)S(1)}, bf16[3,128,128]{2,1,0:T(8,128)(2,1)S(1)}, bf16[3,128,128]{2,1,0:T(8,128)(2,1)S(1)}) custom-call(s32[1,4]{1,0:T(1,128)S(1)} %copy-done.7, s32[1,4]{1,0:T(1,128)S(1)} %copy-done.8, s32[1,32]{1,0:T(1,128)S(1)} %copy-done.9, ...), custom_call_target="tpu_custom_call" | custom-call | flops 8000000000 | bytes 8000000 | tf_op jit(solution)/shard_map/pallas_call | solution.py:391
  127.0 5.8 %collective-permute-start.36 = (bf16[16,8,16,128]{3,2,1,0:T(8,128)(2,1)S(1)}, bf16[16,8,16,128]{3,2,1,0:T(8,128)(2,1)S(1)}, u32[]{:S(2)}, u32[]{:S(2)}) collective-permute-start(bf16[16,8,16,128]{3,2,1,0:T(8,128)(2,1)S(1)} %all-to-all-done.2.own_ref), channel_id=1, source_target_pairs={{0,1},{1,0},{2,3},{3,2},{4,5},{5,4},{6,7},{7,6},{8,9},{9,8},{10,11... | collective-permute-start | bytes 1572872 | tf_op jit(solution)/shard_map/ppermute | solution.py:405
  140.0 2.6 %collective-permute-done.32.p3 = bf16[3,128,128]{2,1,0:T(8,128)(2,1)S(1)} collective-permute-done((bf16[3,128,128]{2,1,0:T(8,128)(2,1)S(1)}, bf16[3,128,128]{2,1,0:T(8,128)(2,1)S(1)}, u32[]{:S(2)}, u32[]{:S(2)}) %collective-permute-start.32) | collective-permute-done | bytes 98336 | tf_op jit(solution)/shard_map/ppermute | solution.py:439
  (131 shorter events, 42.2 us)
Async XLA Ops:
  6.1 7.1 %collective-permute-start.2 = (bf16[544,128]{1,0:T(8,128)(2,1)S(1)}, bf16[544,128]{1,0:T(8,128)(2,1)S(1)}, u32[]{:S(2)}, u32[]{:S(2)}) collective-permute-start(bf16[544,128]{1,0:T(8,128)(2,1)S(1)} %get-tuple-element.47), channel_id=1, source_target_pairs={{0,17},{1,16},{16,1},{17,0},{2,19},{3,18},{18,3},{19,2},{4,21},{5,... | collective-permute-start | bytes 417800 | tf_op jit(solution)/shard_map/ppermute | solution.py:439
  13.2 11.2 %collective-permute-start.6 = (bf16[4,2,128,128]{3,2,1,0:T(8,128)(2,1)S(1)}, bf16[4,2,128,128]{3,2,1,0:T(8,128)(2,1)S(1)}, u32[]{:S(2)}, u32[]{:S(2)}) collective-permute-start(bf16[4,2,128,128]{3,2,1,0:T(8,128)(2,1)S(1)} %get-tuple-element.48.rest_0_.kv_ref), channel_id=1, source_target_pairs={{0,2},{2,4},{4,6},{6,8},{8,10},{10,12},{12,14},{14,0},{1,3},{3,5},... | collective-permute-start | bytes 786440 | tf_op jit(solution)/shard_map/ppermute | solution.py:409
  13.8 10.7 %collective-permute-start.9 = (bf16[4,2,128,128]{3,2,1,0:T(8,128)(2,1)S(1)}, bf16[4,2,128,128]{3,2,1,0:T(8,128)(2,1)S(1)}, u32[]{:S(2)}, u32[]{:S(2)}) collective-permute-start(bf16[4,2,128,128]{3,2,1,0:T(8,128)(2,1)S(1)} %get-tuple-element.48.rest_0_.kv_ref), channel_id=1, source_target_pairs={{0,14},{2,0},{4,2},{6,4},{8,6},{10,8},{12,10},{14,12},{1,15},{3,1}... | collective-permute-start | bytes 786440 | tf_op jit(solution)/shard_map/ppermute | solution.py:413
  17.8 9.3 %collective-permute-start.3 = (bf16[128,1024]{1,0:T(8,128)(2,1)S(1)}, bf16[128,1024]{1,0:T(8,128)(2,1)S(1)}, u32[]{:S(2)}, u32[]{:S(2)}) collective-permute-start(bf16[128,1024]{1,0:T(8,128)(2,1)S(1)} %copy-done), channel_id=1, source_target_pairs={{0,1},{1,0},{2,3},{3,2},{4,5},{5,4},{6,7},{7,6},{8,9},{9,8},{10,11... | collective-permute-start | bytes 786440 | tf_op jit(solution)/shard_map/ppermute | solution.py:405
  17.8 9.3 %collective-permute-start.4 = (bf16[128,1024]{1,0:T(8,128)(2,1)S(1)}, bf16[128,1024]{1,0:T(8,128)(2,1)S(1)}, u32[]{:S(2)}, u32[]{:S(2)}) collective-permute-start(bf16[128,1024]{1,0:T(8,128)(2,1)S(1)} %copy-done), channel_id=1, source_target_pairs={{0,16},{16,0},{1,17},{17,1},{2,18},{18,2},{3,19},{19,3},{4,20},{20... | collective-permute-start | bytes 786440 | tf_op jit(solution)/shard_map/ppermute | solution.py:405
  19.0 12.8 %collective-permute-start.5 = (bf16[128,1024]{1,0:T(8,128)(2,1)S(1)}, bf16[128,1024]{1,0:T(8,128)(2,1)S(1)}, u32[]{:S(2)}, u32[]{:S(2)}) collective-permute-start(bf16[128,1024]{1,0:T(8,128)(2,1)S(1)} %copy-done), channel_id=1, source_target_pairs={{0,17},{1,16},{16,1},{17,0},{2,19},{3,18},{18,3},{19,2},{4,21},{5,... | collective-permute-start | bytes 786440 | tf_op jit(solution)/shard_map/ppermute | solution.py:439
  24.4 8.7 %collective-permute-start.7 = (bf16[4,2,128,128]{3,2,1,0:T(8,128)(2,1)S(1)}, bf16[4,2,128,128]{3,2,1,0:T(8,128)(2,1)S(1)}, u32[]{:S(2)}, u32[]{:S(2)}) collective-permute-start(bf16[4,2,128,128]{3,2,1,0:T(8,128)(2,1)S(1)} %collective-permute-done.6.rest_1_), channel_id=1, source_target_pairs={{0,2},{2,4},{4,6},{6,8},{8,10},{10,12},{12,14},{14,0},{1,3},{3,5},... | collective-permute-start | bytes 786440 | tf_op jit(solution)/shard_map/ppermute | solution.py:409
  24.4 8.7 %collective-permute-start.10 = (bf16[4,2,128,128]{3,2,1,0:T(8,128)(2,1)S(1)}, bf16[4,2,128,128]{3,2,1,0:T(8,128)(2,1)S(1)}, u32[]{:S(2)}, u32[]{:S(2)}) collective-permute-start(bf16[4,2,128,128]{3,2,1,0:T(8,128)(2,1)S(1)} %collective-permute-done.9.rest_6_.rest_7_), channel_id=1, source_target_pairs={{0,14},{2,0},{4,2},{6,4},{8,6},{10,8},{12,10},{14,12},{1,15},{3,1}... | collective-permute-start | bytes 786440 | tf_op jit(solution)/shard_map/ppermute | solution.py:413
  33.1 7.8 %collective-permute-start.8 = (bf16[4,2,128,128]{3,2,1,0:T(8,128)(2,1)S(1)}, bf16[4,2,128,128]{3,2,1,0:T(8,128)(2,1)S(1)}, u32[]{:S(2)}, u32[]{:S(2)}) collective-permute-start(bf16[4,2,128,128]{3,2,1,0:T(8,128)(2,1)S(1)} %collective-permute-done.7.rest_2_), channel_id=1, source_target_pairs={{0,2},{2,4},{4,6},{6,8},{8,10},{10,12},{12,14},{14,0},{1,3},{3,5},... | collective-permute-start | bytes 786440 | tf_op jit(solution)/shard_map/ppermute | solution.py:409
  33.1 7.8 %collective-permute-start.11 = (bf16[4,2,128,128]{3,2,1,0:T(8,128)(2,1)S(1)}, bf16[4,2,128,128]{3,2,1,0:T(8,128)(2,1)S(1)}, u32[]{:S(2)}, u32[]{:S(2)}) collective-permute-start(bf16[4,2,128,128]{3,2,1,0:T(8,128)(2,1)S(1)} %collective-permute-done.10.rest_5_.rest_6_), channel_id=1, source_target_pairs={{0,14},{2,0},{4,2},{6,4},{8,6},{10,8},{12,10},{14,12},{1,15},{3,1}... | collective-permute-start | bytes 786440 | tf_op jit(solution)/shard_map/ppermute | solution.py:413
  40.9 8.2 %collective-permute-start.13 = (bf16[4,160,128]{2,1,0:T(8,128)(2,1)S(1)}, bf16[4,160,128]{2,1,0:T(8,128)(2,1)S(1)}, u32[]{:S(2)}, u32[]{:S(2)}) collective-permute-start(bf16[4,160,128]{2,1,0:T(8,128)(2,1)S(1)} %get-tuple-element.55.q_ref.rest_0_), channel_id=1, source_target_pairs={{0,2},{2,4},{4,6},{6,8},{8,10},{10,12},{12,14},{14,0},{1,3},{3,5},... | collective-permute-start | bytes 491528 | tf_op jit(solution)/shard_map/ppermute | solution.py:409
  41.0 10.6 %collective-permute-start.15 = (bf16[4,160,128]{2,1,0:T(8,128)(2,1)S(1)}, bf16[4,160,128]{2,1,0:T(8,128)(2,1)S(1)}, u32[]{:S(2)}, u32[]{:S(2)}) collective-permute-start(bf16[4,160,128]{2,1,0:T(8,128)(2,1)S(1)} %get-tuple-element.55.q_ref.rest_0_), channel_id=1, source_target_pairs={{0,14},{2,0},{4,2},{6,4},{8,6},{10,8},{12,10},{14,12},{1,15},{3,1}... | collective-permute-start | bytes 491528 | tf_op jit(solution)/shard_map/ppermute | solution.py:413
  43.7 9.5 %collective-permute-start.12 = (bf16[4,2,128,128]{3,2,1,0:T(8,128)(2,1)S(1)}, bf16[4,2,128,128]{3,2,1,0:T(8,128)(2,1)S(1)}, u32[]{:S(2)}, u32[]{:S(2)}) collective-permute-start(bf16[4,2,128,128]{3,2,1,0:T(8,128)(2,1)S(1)} %collective-permute-done.8.rest_3_), channel_id=1, source_target_pairs={{0,2},{2,4},{4,6},{6,8},{8,10},{10,12},{12,14},{14,0},{1,3},{3,5},... | collective-permute-start | bytes 786440 | tf_op jit(solution)/shard_map/ppermute | solution.py:409
  49.1 12.6 %collective-permute-start.14 = (bf16[4,160,128]{2,1,0:T(8,128)(2,1)S(1)}, bf16[4,160,128]{2,1,0:T(8,128)(2,1)S(1)}, u32[]{:S(2)}, u32[]{:S(2)}) collective-permute-start(bf16[4,160,128]{2,1,0:T(8,128)(2,1)S(1)} %collective-permute-done.13.rest_1_), channel_id=1, source_target_pairs={{0,2},{2,4},{4,6},{6,8},{8,10},{10,12},{12,14},{14,0},{1,3},{3,5},... | collective-permute-start | bytes 491528 | tf_op jit(solution)/shard_map/ppermute | solution.py:409
  51.6 10.0 %collective-permute-start.16 = (bf16[4,160,128]{2,1,0:T(8,128)(2,1)S(1)}, bf16[4,160,128]{2,1,0:T(8,128)(2,1)S(1)}, u32[]{:S(2)}, u32[]{:S(2)}) collective-permute-start(bf16[4,160,128]{2,1,0:T(8,128)(2,1)S(1)} %collective-permute-done.15.rest_7_), channel_id=1, source_target_pairs={{0,14},{2,0},{4,2},{6,4},{8,6},{10,8},{12,10},{14,12},{1,15},{3,1}... | collective-permute-start | bytes 491528 | tf_op jit(solution)/shard_map/ppermute | solution.py:413
  71.7 22.9 %collective-permute-start.24 = (bf16[4,128,128]{2,1,0:T(8,128)(2,1)S(1)}, bf16[4,128,128]{2,1,0:T(8,128)(2,1)S(1)}, u32[]{:S(2)}, u32[]{:S(2)}) collective-permute-start(bf16[4,128,128]{2,1,0:T(8,128)(2,1)S(1)} %collective-permute-done.23.rest_9_), channel_id=1, source_target_pairs={{0,2},{2,4},{4,6},{6,8},{8,10},{10,12},{12,14},{14,0},{1,3},{3,5},... | collective-permute-start | bytes 393224 | tf_op jit(solution)/shard_map/ppermute | solution.py:409
  71.7 22.5 %collective-permute-start.28 = (bf16[4,128,128]{2,1,0:T(8,128)(2,1)S(1)}, bf16[4,128,128]{2,1,0:T(8,128)(2,1)S(1)}, u32[]{:S(2)}, u32[]{:S(2)}) collective-permute-start(bf16[4,128,128]{2,1,0:T(8,128)(2,1)S(1)} %collective-permute-done.27.rest_15_), channel_id=1, source_target_pairs={{0,14},{2,0},{4,2},{6,4},{8,6},{10,8},{12,10},{14,12},{1,15},{3,1}... | collective-permute-start | bytes 393224 | tf_op jit(solution)/shard_map/ppermute | solution.py:413
  74.4 24.1 %all-to-all-start = ((bf16[64,16,128]{2,1,0:T(8,128)(2,1)}), bf16[64,16,128]{2,1,0:T(8,128)(2,1)S(1)}, u32[]{:S(2)}, u32[]{:S(2)}) async-start(bf16[64,16,128]{2,1,0:T(8,128)(2,1)} %shard_map.165), calls=%async_computation | async-start | bytes 524288 | tf_op jit(solution)/shard_map/all_to_all | solution.py:506
  91.9 10.9 %collective-permute-start.21 = (bf16[4,160,128]{2,1,0:T(8,128)(2,1)S(1)}, bf16[4,160,128]{2,1,0:T(8,128)(2,1)S(1)}, u32[]{:S(2)}, u32[]{:S(2)}) collective-permute-start(bf16[4,160,128]{2,1,0:T(8,128)(2,1)S(1)} %collective-permute-done.20.rest_3_), channel_id=1, source_target_pairs={{0,2},{2,4},{4,6},{6,8},{8,10},{10,12},{12,14},{14,0},{1,3},{3,5},... | collective-permute-start | bytes 491528 | tf_op jit(solution)/shard_map/ppermute | solution.py:409
  94.2 13.4 %collective-permute-start.29 = (bf16[4,128,128]{2,1,0:T(8,128)(2,1)S(1)}, bf16[4,128,128]{2,1,0:T(8,128)(2,1)S(1)}, u32[]{:S(2)}, u32[]{:S(2)}) collective-permute-start(bf16[4,128,128]{2,1,0:T(8,128)(2,1)S(1)} %collective-permute-done.28.rest_14_), channel_id=1, source_target_pairs={{0,14},{2,0},{4,2},{6,4},{8,6},{10,8},{12,10},{14,12},{1,15},{3,1}... | collective-permute-start | bytes 393224 | tf_op jit(solution)/shard_map/ppermute | solution.py:413
  94.6 11.8 %collective-permute-start.25 = (bf16[4,128,128]{2,1,0:T(8,128)(2,1)S(1)}, bf16[4,128,128]{2,1,0:T(8,128)(2,1)S(1)}, u32[]{:S(2)}, u32[]{:S(2)}) collective-permute-start(bf16[4,128,128]{2,1,0:T(8,128)(2,1)S(1)} %collective-permute-done.24.rest_10_), channel_id=1, source_target_pairs={{0,2},{2,4},{4,6},{6,8},{8,10},{10,12},{12,14},{14,0},{1,3},{3,5},... | collective-permute-start | bytes 393224 | tf_op jit(solution)/shard_map/ppermute | solution.py:409
  99.2 10.1 %all-to-all-start.1 = ((bf16[8,16,128]{2,1,0:T(8,128)(2,1)}), bf16[8,16,128]{2,1,0:T(8,128)(2,1)S(1)}, u32[]{:S(2)}, u32[]{:S(2)}) async-start(bf16[8,16,128]{2,1,0:T(8,128)(2,1)} %shard_map.166), calls=%async_computation.1 | async-start | bytes 65536 | tf_op jit(solution)/shard_map/all_to_all | solution.py:528
  112.1 14.9 %all-to-all-start.2 = ((bf16[16,8,16,128]{3,2,1,0:T(8,128)(2,1)}), bf16[16,8,16,128]{3,2,1,0:T(8,128)(2,1)S(1)}, u32[]{:S(2)}, u32[]{:S(2)}) async-start(bf16[16,8,16,128]{3,2,1,0:T(8,128)(2,1)} %shard_map.167), calls=%async_computation.2 | async-start | bytes 1048576 | tf_op jit(solution)/shard_map/all_to_all | solution.py:532
  127.0 16.3 %collective-permute-start.36 = (bf16[16,8,16,128]{3,2,1,0:T(8,128)(2,1)S(1)}, bf16[16,8,16,128]{3,2,1,0:T(8,128)(2,1)S(1)}, u32[]{:S(2)}, u32[]{:S(2)}) collective-permute-start(bf16[16,8,16,128]{3,2,1,0:T(8,128)(2,1)S(1)} %all-to-all-done.2.own_ref), channel_id=1, source_target_pairs={{0,1},{1,0},{2,3},{3,2},{4,5},{5,4},{6,7},{7,6},{8,9},{9,8},{10,11... | collective-permute-start | bytes 1572872 | tf_op jit(solution)/shard_map/ppermute | solution.py:405
  (46 other events, 475.8 us)

commit v2 on v1

--- a/solution.py
+++ b/solution.py
@@ -1,3 +1,5 @@
+import functools
+
 import jax
 import jax.numpy as jnp
 from jax import lax
@@ -243,10 +245,8 @@
         term = jnp.zeros((128, 256), F32)
         for d, cot in enumerate((c0, c1, c2, c3)):
             term = term + dot(mixed_ref[pl.ds(d * 128, 128), :], cot[:, pl.ds(part * 256, 256)], 0, 0)
-        term = term.astype(BF16)
-        for r in range(8):
-            for c in range(2):
-                gw_ref[r * 8 + part * 2 + c] = term[r * 16 : r * 16 + 16, c * 128 : c * 128 + 128]
+        gw_ref[2 * part] = term[:, :128].astype(BF16)
+        gw_ref[2 * part + 1] = term[:, 128:].astype(BF16)
 
 
 def score_kernel(ub, tl, pk, mixed_ref, cand_ref, *rest):
@@ -303,50 +303,85 @@
         outs[slot][1] = gg_ref[slot]
 
 
-def key_kernel(ub, tl, pk, kv_ref, sc_ref, *rest):
-    qs, das, outs, (qbuf, dbuf, both, inv, qsems, dsems) = (
-        rest[:8], rest[8:16], rest[16:20], rest[20:],
-    )
-    copies = load_chunks(qs, qbuf, qsems) + load_chunks(das, dbuf, dsems)
+def key_step(key, value, queries, grads, reach, carry):
+    gk, gv = carry
+    col = iota((128, 128), 1) - iota((128, 128), 0)
+    logits = dot(key, queries, 1, 1) * SCALE
+    slopes = dot(value, grads, 1, 1)
+    sigma = 1.0 / (1.0 + jnp.exp(-logits))
+    silu = logits * sigma
+    change = slopes * (sigma * (1.0 + logits * (1.0 - sigma)))
+    weights, ds = [], []
+    for i in range(4):
+        cols = slice(i * 128, i * 128 + 128)
+        allowed = col >= reach[i] * 128
+        weights.append(jnp.where(allowed, silu[:, cols], 0.0).astype(BF16))
+        ds.append(jnp.where(allowed, change[:, cols], 0.0).astype(BF16))
+    gk = gk + dot(jnp.concatenate(ds, axis=1), queries, 1, 0)
+    gv = gv + dot(jnp.concatenate(weights, axis=1), grads, 1, 0)
+    return gk, gv
+
+
+def key_near_kernel(ub, tl, pk, kv_ref, *rest):
+    qs, das, (sum_ref,), (qbuf, dbuf, inv, sems) = rest[:7], rest[7:14], rest[14:15], rest[15:]
+    copies = []
+    for i, c in enumerate((0, 1, 2, 3, 5, 6, 7)):
+        copies.append(pltpu.make_async_copy(qs[i], qbuf.at[pl.ds(4 * c, 4)], sems.at[i]))
+        copies.append(pltpu.make_async_copy(das[i], dbuf.at[pl.ds(4 * c, 4)], sems.at[7 + i]))
+    for copy in copies:
+        copy.start()
     fill_places(pk, inv)
     for copy in copies:
         copy.wait()
-    row = iota((128, 512), 0)
-    col = iota((128, 512), 1)
 
     def one(slot, carry):
         logical = pk[0, slot_of(slot)]
         user, first, blocks, tail = user_of(ub, tl, logical)
         count = first + blocks - logical
-        key = kv_ref[slot, 0]
-        value = kv_ref[slot, 1]
 
         def step(j, carry):
-            gk, gv = carry
-            places = [inv[logical + jnp.minimum(4 * j + i, count - 1)] for i in range(4)]
-            queries = jnp.concatenate([qbuf[p, :128] for p in places], axis=0)
-            grads = jnp.concatenate([dbuf[p] for p in places], axis=0)
-            logits = dot(key, queries, 1, 1) * SCALE
-            slopes = dot(value, grads, 1, 1)
-            sigma = 1.0 / (1.0 + jnp.exp(-logits))
-            silu = logits * sigma
-            slope = sigma * (1.0 + logits * (1.0 - sigma))
-            later = col + j * 512
-            allowed = (later >= row) & (later < count * 128)
-            weights = jnp.where(allowed, silu, 0.0).astype(BF16)
-            ds = jnp.where(allowed, slopes * slope, 0.0).astype(BF16)
-            return gk + dot(ds, queries, 1, 0), gv + dot(weights, grads, 1, 0)
+            spots, reach = [], []
+            for i in range(4):
+                entry = 4 * j + i
+                place = inv[logical + jnp.minimum(entry, count - 1)]
+                late = (place // 4 == 4) | (entry >= count)
+                spots.append(jnp.where(late, 0, place))
+                reach.append(jnp.where(late, 1, jnp.where(entry == 0, 0, -1)))
+            queries = jnp.concatenate([qbuf[p, :128] for p in spots], axis=0)
+            grads = jnp.concatenate([dbuf[p] for p in spots], axis=0)
+            return key_step(kv_ref[slot, 0], kv_ref[slot, 1], queries, grads, reach, carry)
 
         zero = jnp.zeros((128, 128), F32)
         gk, gv = lax.fori_loop(0, (count + 3) // 4, step, (zero, zero))
+        sum_ref[slot, 0] = gk
+        sum_ref[slot, 1] = gv
+        return carry
+
+    lax.fori_loop(0, 4, one, 0)
+
+
+def key_far_kernel(ub, tl, pk, kv_ref, near_ref, q_ref, da_ref, sc_ref, o0, o1, o2, o3, both):
+    def one(slot, carry):
+        logical = pk[0, slot_of(slot)]
+        user, first, blocks, tail = user_of(ub, tl, logical)
+        reach = []
+        for i in range(4):
+            other = pk[0, slot_of(16 + i)]
+            reach.append(jnp.where((other > logical) & (other < first + blocks), -1, 1))
+        queries = jnp.concatenate([q_ref[i, :128] for i in range(4)], axis=0)
+        grads = jnp.concatenate([da_ref[i] for i in range(4)], axis=0)
+        gk, gv = key_step(
+            kv_ref[slot, 0], kv_ref[slot, 1], queries, grads, reach,
+            (near_ref[slot, 0], near_ref[slot, 1]),
+        )
         both[slot, 0] = (gk * SCALE).astype(BF16)
         both[slot, 1] = gv.astype(BF16)
         return carry
 
     lax.fori_loop(0, 4, one, 0)
-    for slot in range(4):
-        outs[slot][:2] = both[slot]
-        outs[slot][2] = sc_ref[slot]
+    for slot, out in enumerate((o0, o1, o2, o3)):
+        out[:2] = both[slot]
+        out[2] = sc_ref[slot]
 
 
 def unpack_early_kernel(p0, p1, p2, p3, gq_ref, gg_ref):
@@ -364,27 +399,21 @@
     sc_ref[...] = scores
 
 
-def sum_kernel(parts_ref, out_ref):
+def sum_kernel(copies, parts_ref, out_ref):
     total = jnp.sum(parts_ref[...].astype(F32), axis=0).astype(BF16)
-    for i in range(8):
+    for i in range(copies):
         out_ref[i] = total
-
-
-def spread_kernel(line_ref, out_ref):
-    for i in range(16):
-        out_ref[i] = line_ref[...]
 
 
 def assemble_kernel(own_ref, far_ref, out_ref):
     me = lax.axis_index("core")
-    for r in range(8):
+    for group in range(8):
         for xl in range(2):
-            for z in range(8):
-                own = own_ref[r * 2 + xl, z].astype(F32)
-                far = far_ref[r * 2 + xl, z].astype(F32)
-                for core in range(2):
-                    rows = pl.ds((xl * 2 + core) * 128 + r * 16, 16)
-                    out_ref[rows, pl.ds(z * 128, 128)] = jnp.where(me == core, own, far)
+            own = own_ref[group * 2 + xl].astype(F32)
+            far = far_ref[group * 2 + xl].astype(F32)
+            for core in range(2):
+                rows = pl.ds((xl * 2 + core) * 128, 128)
+                out_ref[rows, pl.ds(group * 128, 128)] = jnp.where(me == core, own, far)
 
 
 def call(kernel, ins, outs, scratch=(), us=2, mib=8):
@@ -486,15 +515,14 @@
         facts + vm(qp, gate_h, gm, att_near, kvs[4]),
         [(block, F32), ((4, 8, 128), F32)],
     )
-    qps = ring(after(qp, kvs[3], kvs[5]), lambda n: [])
-    stats = after(stats, qps[1], qps[7])
+    qps = ring(after(qp, kvs[4]), lambda n: [])
     all_stats = swap([stats] * 4)
     da, gg, mixed = call(
         norm_kernel,
-        facts + vm(after(att, qps[2], qps[6]), *all_stats, gate_h, gm),
+        facts + vm(after(att, qps[1], qps[7]), *all_stats, gate_h, gm),
         [(block, BF16), (block, BF16), ((512, 128), BF16)],
     )
-    (gw,) = call(weight_kernel, vm(mixed, *cots), [((64, 16, 128), BF16)])
+    (gw,) = call(weight_kernel, vm(mixed, *cots), [((8, 128, 128), BF16)])
     early = call(
         query_kernel,
         facts + vm(qp, da, gg) + raw(kvs),
@@ -502,20 +530,18 @@
         [kv_buffer, pltpu.VMEM(block, BF16), places, sems],
         us=6,
     )
-    first_up, first_down = up(da), down(da)
-    parts = lax.all_to_all(
-        after(gw, qps[3], qps[5], first_up, first_down),
-        ("xh", "y", "z"),
-        split_axis=0,
-        concat_axis=0,
-        tiled=True,
-    )
-    ups, downs = [da, first_up, up(first_up)], [da, first_down, down(first_down)]
+    parts = lax.all_to_all(gw, ("xh", "y"), split_axis=0, concat_axis=0, tiled=True)
+    ups, downs = [da, up(da)], [da, down(da)]
     (piece,) = call(
-        sum_kernel, vm(after(parts, ups[2], downs[2], early[0])), [((8, 16, 128), BF16)]
-    )
-    ups.append(up(after(ups[2], early[0])))
-    downs.append(down(after(downs[2], early[0])))
+        functools.partial(sum_kernel, 8),
+        vm(after(parts, ups[1], downs[1], qps[2], qps[6], early[0])),
+        [((8, 128, 128), BF16)],
+    )
+    line = lax.all_to_all(piece, "z", split_axis=0, concat_axis=0, tiled=True)
+    ups.append(up(after(ups[1], early[0])))
+    downs.append(down(after(downs[1], early[0])))
+    ups.append(up(ups[2]))
+    downs.append(down(downs[2]))
     ups.append(up(ups[3]))
     das = ups + downs[:0:-1]
     (sc,) = call(
@@ -525,30 +551,33 @@
         [pltpu.VMEM((32, 160, 128), BF16), sems],
     )
     early = swap(early)
-    line = lax.all_to_all(piece, "z", split_axis=0, concat_axis=0, tiled=True)
     (lines,) = call(
-        spread_kernel, vm(after(line, ups[3], downs[3], sc)), [((16, 8, 16, 128), BF16)]
-    )
-    near = lax.all_to_all(
-        after(lines, ups[4]), ("xh", "y", "xl"), split_axis=0, concat_axis=0, tiled=True
-    )
-    late = call(
-        key_kernel,
-        facts + vm(kv, sc) + raw(qps) + raw(das),
-        [((3, 128, 128), BF16)] * 4,
+        functools.partial(sum_kernel, 16),
+        vm(after(line, ups[2], downs[2], *early[1:])),
+        [((16, 128, 128), BF16)],
+    )
+    near = lax.all_to_all(lines, ("xh", "y", "xl"), split_axis=0, concat_axis=0, tiled=True)
+    (key_sums,) = call(
+        key_near_kernel,
+        facts + vm(kv) + raw(qps[:4] + qps[5:]) + raw(das[:4] + das[5:]),
+        [((4, 2, 128, 128), F32)],
         [
             pltpu.VMEM((32, 160, 128), BF16),
             pltpu.VMEM((32, 128, 128), BF16),
-            pltpu.VMEM((4, 2, 128, 128), BF16),
             places,
-            sems,
-            sems,
+            pltpu.SemaphoreType.DMA((14,)),
         ],
         us=8,
-        mib=12,
+    )
+    late = call(
+        key_far_kernel,
+        facts + vm(kv, key_sums, qps[4], das[4], sc),
+        [((3, 128, 128), BF16)] * 4,
+        [pltpu.VMEM((4, 2, 128, 128), BF16)],
+        us=3,
     )
     late = swap(late)
-    far = flip(after(near, late[0]), "core")
+    far = flip(after(near, *late[1:]), "core")
     (gow,) = call(assemble_kernel, vm(near, far), [((512, 1024), F32)])
     rows = (128, 512)
     gq, gg = call(unpack_early_kernel, vm(*early), [(rows, BF16)] * 2)

time: 145 us -> 136 us (0.938)
  waiting for transfers between devices: 35.4 us -> 27.7 us
  starting transfers between devices: 72.3 us -> 67.8 us
  local copies, waits for them, and re-layouts: 0.78 us -> 2.47 us
  Pallas kernels: 35.3 us -> 36.9 us
    all_to_all x2, waiting for transfers between devices: 3.76 us -> 0.01 us  [the longest x1 0.01 us: body(): lax.all_to_all(gw, ('xh', 'y'), split_axis=0, concat_axis=0, tiled=True)]
    all_to_all x2, starting transfers between devices: 17.4 us -> 14 us  [the longest x1 7.62 us: body(): lax.all_to_all(lines, ('xh', 'y', 'xl'), split_axis=0, concat_axis=0, til...]
    ppermute x12, starting transfers between devices: 8.56 us -> 5.91 us  [up(): return lax.ppermute(array, 'z', [(i, (i + 1) % 8) for i in range(8)])]
    ppermute x12, waiting for transfers between devices: 12.9 us -> 10.2 us  [up(): return lax.ppermute(array, 'z', [(i, (i + 1) % 8) for i in range(8)])]
    ppermute x11, waiting for transfers between devices: 1.77 us -> 3.7 us  [flip(): return lax.ppermute(array, axis, [(0, 1), (1, 0)])]
    all_to_all x1, starting transfers between devices: 3.56 us -> 5.41 us  [body(): line = lax.all_to_all(piece, 'z', split_axis=0, concat_axis=0, tiled=True)]
    ppermute x5, waiting for transfers between devices: 15.4 us -> 13.7 us  [swap(): lax.ppermute(pieces[3], ('xl', 'core'), [(i, 3 - i) for i in range(4)])]
    unnamed x60, local copies, waits for them, and re-layouts: 0.78 us -> 2.47 us
  transfers between devices with their start and end apart: 40 -> 40, of which waited for: 16 -> 10; matrix products, arithmetic and copies ran while one was open for 0% -> 0% of each run, Pallas kernels for 21% -> 24%
where the time goes in v2:
time: 136 us
  starting transfers between devices  67.8 us (50%)
  Pallas kernels  36.9 us (27%)
  waiting for transfers between devices  27.7 us (20%)
  local copies, waits for them, and re-layouts  2.47 us (2%)
    pallas_call x16, Pallas kernels, call(): pl.pallas_call(kernel, in_specs=[spec for spec, _ in ins], out_specs=[VM]...  36.9 us
    ppermute x9, starting transfers between devices, down(): return lax.ppermute(array, 'z', [(i, (i + 7) % 8) for i in range(8)])  20.8 us
    ppermute x11, starting transfers between devices, flip(): return lax.ppermute(array, axis, [(0, 1), (1, 0)])  14.2 us
    ppermute x5, waiting for transfers between devices, swap(): lax.ppermute(pieces[3], ('xl', 'core'), [(i, 3 - i) for i in range(4)])  13.7 us
    ppermute x12, waiting for transfers between devices, up(): return lax.ppermute(array, 'z', [(i, (i + 1) % 8) for i in range(8)])  10.2 us
    all_to_all x1, starting transfers between devices, body(): lax.all_to_all(lines, ('xh', 'y', 'xl'), split_axis=0, concat_axis=0, til...  7.62 us
    ppermute x5, starting transfers between devices, swap(): lax.ppermute(pieces[3], ('xl', 'core'), [(i, 3 - i) for i in range(4)])  7.52 us
    all_to_all x1, starting transfers between devices, body(): lax.all_to_all(gw, ('xh', 'y'), split_axis=0, concat_axis=0, tiled=True)  6.35 us
  transfers between devices with their start and end apart: 40, of which 10 were waited for; matrix products, arithmetic and copies ran while one was open for 0% of the time, Pallas kernels for 24%

profile of v2, /device:TPU:1, one launch (start us, length us, event | category | flops | bytes accessed | tf_op | source)
XLA Modules:
  0.0 136.0 jit_solution(3385662326211456695)
XLA Ops:
  7.6 5.5 %collective-permute-done.2.p3 = bf16[544,128]{1,0:T(8,128)(2,1)S(1)} collective-permute-done((bf16[544,128]{1,0:T(8,128)(2,1)S(1)}, bf16[544,128]{1,0:T(8,128)(2,1)S(1)}, u32[]{:S(2)}, u32[]{:S(2)}) %collective-permute-start.2) | collective-permute-done | bytes 139296 | tf_op jit(solution)/shard_map/ppermute | solution.py:468
  13.8 4.0 %collective-permute-start.16 = (bf16[4,2,128,128]{3,2,1,0:T(8,128)(2,1)S(1)}, bf16[4,2,128,128]{3,2,1,0:T(8,128)(2,1)S(1)}, u32[]{:S(2)}, u32[]{:S(2)}) collective-permute-start(bf16[4,2,128,128]{3,2,1,0:T(8,128)(2,1)S(1)} %get-tuple-element.45.rest_0_.kv_ref), channel_id=1, source_target_pairs={{0,14},{2,0},{4,2},{6,4},{8,6},{10,8},{12,10},{14,12},{1,15},{3,1}... | collective-permute-start | bytes 786440 | tf_op jit(solution)/shard_map/ppermute | solution.py:442
  19.9 4.5 %collective-permute-done.3.rest_1_ = bf16[4,2,128,128]{3,2,1,0:T(8,128)(2,1)S(1)} collective-permute-done((bf16[4,2,128,128]{3,2,1,0:T(8,128)(2,1)S(1)}, bf16[4,2,128,128]{3,2,1,0:T(8,128)(2,1)S(1)}, u32[]{:S(2)}, u32[]{:S(2)}) %collective-permute-start.3) | collective-permute-done | bytes 262176 | tf_op jit(solution)/shard_map/ppermute | solution.py:438
  24.4 2.7 %collective-permute-start.17 = (bf16[4,2,128,128]{3,2,1,0:T(8,128)(2,1)S(1)}, bf16[4,2,128,128]{3,2,1,0:T(8,128)(2,1)S(1)}, u32[]{:S(2)}, u32[]{:S(2)}) collective-permute-start(bf16[4,2,128,128]{3,2,1,0:T(8,128)(2,1)S(1)} %collective-permute-done.16.rest_6_.rest_7_), channel_id=1, source_target_pairs={{0,14},{2,0},{4,2},{6,4},{8,6},{10,8},{12,10},{14,12},{1,15},{3,1}... | collective-permute-start | bytes 786440 | tf_op jit(solution)/shard_map/ppermute | solution.py:442
  27.1 4.6 %collective-permute-done.7.c3 = bf16[128,1024]{1,0:T(8,128)(2,1)S(1)} collective-permute-done((bf16[128,1024]{1,0:T(8,128)(2,1)S(1)}, bf16[128,1024]{1,0:T(8,128)(2,1)S(1)}, u32[]{:S(2)}, u32[]{:S(2)}) %collective-permute-start.7) | collective-permute-done | bytes 262176 | tf_op jit(solution)/shard_map/ppermute | solution.py:468
  33.1 2.7 %collective-permute-start.18 = (bf16[4,2,128,128]{3,2,1,0:T(8,128)(2,1)S(1)}, bf16[4,2,128,128]{3,2,1,0:T(8,128)(2,1)S(1)}, u32[]{:S(2)}, u32[]{:S(2)}) collective-permute-start(bf16[4,2,128,128]{3,2,1,0:T(8,128)(2,1)S(1)} %collective-permute-done.17.rest_5_.rest_6_), channel_id=1, source_target_pairs={{0,14},{2,0},{4,2},{6,4},{8,6},{10,8},{12,10},{14,12},{1,15},{3,1}... | collective-permute-start | bytes 786440 | tf_op jit(solution)/shard_map/ppermute | solution.py:442
  37.3 3.6 %collective-permute-done.8.rest_3_ = bf16[4,2,128,128]{3,2,1,0:T(8,128)(2,1)S(1)} collective-permute-done((bf16[4,2,128,128]{3,2,1,0:T(8,128)(2,1)S(1)}, bf16[4,2,128,128]{3,2,1,0:T(8,128)(2,1)S(1)}, u32[]{:S(2)}, u32[]{:S(2)}) %collective-permute-start.8) | collective-permute-done | bytes 262176 | tf_op jit(solution)/shard_map/ppermute | solution.py:438
  41.7 5.4 %shard_map.157.near_ref = f32[4,128,128]{2,1,0:T(8,128)S(1)} custom-call(s32[1,4]{1,0:T(1,128)S(1)} %copy-done.9, s32[1,4]{1,0:T(1,128)S(1)} %copy-done.10, s32[1,32]{1,0:T(1,128)S(1)} %copy-done.11, bf16[4,160,128]{2,1,0:T(8,128)(2,1)S(1)} %get-tuple-element.49.q_ref.rest_0_, bf16[4,2,128,128]{3,2,1,0:T(8,128)(2,1)} %copy-done.1, ...), custom_call_target="tpu_custom_call" | custom-call | flops 6000000000 | bytes 6000000 | tf_op jit(solution)/shard_map/pallas_call | solution.py:420
  47.8 2.7 %collective-permute-start.13 = (bf16[4,160,128]{2,1,0:T(8,128)(2,1)S(1)}, bf16[4,160,128]{2,1,0:T(8,128)(2,1)S(1)}, u32[]{:S(2)}, u32[]{:S(2)}) collective-permute-start(bf16[4,160,128]{2,1,0:T(8,128)(2,1)S(1)} %get-tuple-element.49.q_ref.rest_0_), channel_id=1, source_target_pairs={{0,14},{2,0},{4,2},{6,4},{8,6},{10,8},{12,10},{14,12},{1,15},{3,1}... | collective-permute-start | bytes 491528 | tf_op jit(solution)/shard_map/ppermute | solution.py:442
  50.5 2.8 %shard_map.158 = (f32[4,128,128]{2,1,0:T(8,128)S(1)}, f32[4,8,128]{2,1,0:T(8,128)S(1)}) custom-call(s32[1,4]{1,0:T(1,128)S(1)} %copy-done.9, s32[1,4]{1,0:T(1,128)S(1)} %copy-done.10, s32[1,32]{1,0:T(1,128)S(1)} %copy-done.11, bf16[4,160,128]{2,1,0:T(8,128)(2,1)S(1)} %get-tuple-element.49.q_ref.rest_0_, bf16[4,128,128]{2,1,0:T(8,128)(2,1)S(1)} %get-tuple-element.50.gate_ref, ...), custom_call_target="tpu_custom_call" | custom-call | flops 2000000000 | bytes 2000000 | tf_op jit(solution)/shard_map/pallas_call | solution.py:420
  53.3 3.9 %collective-permute-start.19 = (f32[4,8,128]{2,1,0:T(8,128)S(1)}, f32[4,8,128]{2,1,0:T(8,128)S(1)}, u32[]{:S(2)}, u32[]{:S(2)}) collective-permute-start(f32[4,8,128]{2,1,0:T(8,128)S(1)} %get-tuple-element.54.s0), channel_id=1, source_target_pairs={{0,1},{1,0},{2,3},{3,2},{4,5},{5,4},{6,7},{7,6},{8,9},{9,8},{10,11... | collective-permute-start | bytes 49160 | tf_op jit(solution)/shard_map/ppermute | solution.py:434
  62.3 2.7 %collective-permute-start.25 = (bf16[4,128,128]{2,1,0:T(8,128)(2,1)S(1)}, bf16[4,128,128]{2,1,0:T(8,128)(2,1)S(1)}, u32[]{:S(2)}, u32[]{:S(2)}) collective-permute-start(bf16[4,128,128]{2,1,0:T(8,128)(2,1)S(1)} %get-tuple-element.55.da_ref.rest_7_), channel_id=1, source_target_pairs={{0,14},{2,0},{4,2},{6,4},{8,6},{10,8},{12,10},{14,12},{1,15},{3,1}... | collective-permute-start | bytes 393224 | tf_op jit(solution)/shard_map/ppermute | solution.py:442
  66.2 6.4 %all-to-all-start = ((bf16[8,128,128]{2,1,0:T(8,128)(2,1)}), bf16[8,128,128]{2,1,0:T(8,128)(2,1)S(1)}, u32[]{:S(2)}, u32[]{:S(2)}) async-start(bf16[8,128,128]{2,1,0:T(8,128)(2,1)} %shard_map.166), calls=%async_computation | async-start | bytes 524288 | tf_op jit(solution)/shard_map/all_to_all | solution.py:533
  72.6 2.7 %collective-permute-start.14 = (bf16[4,160,128]{2,1,0:T(8,128)(2,1)S(1)}, bf16[4,160,128]{2,1,0:T(8,128)(2,1)S(1)}, u32[]{:S(2)}, u32[]{:S(2)}) collective-permute-start(bf16[4,160,128]{2,1,0:T(8,128)(2,1)S(1)} %collective-permute-done.13.rest_6_.rest_7_), channel_id=1, source_target_pairs={{0,14},{2,0},{4,2},{6,4},{8,6},{10,8},{12,10},{14,12},{1,15},{3,1}... | collective-permute-start | bytes 491528 | tf_op jit(solution)/shard_map/ppermute | solution.py:442
  75.3 5.8 %shard_map.160 = (bf16[2,128,128]{2,1,0:T(8,128)(2,1)S(1)}, bf16[2,128,128]{2,1,0:T(8,128)(2,1)S(1)}, bf16[2,128,128]{2,1,0:T(8,128)(2,1)S(1)}, bf16[2,128,128]{2,1,0:T(8,128)(2,1)S(1)}) custom-call(s32[1,4]{1,0:T(1,128)S(1)} %copy-done.9, s32[1,4]{1,0:T(1,128)S(1)} %copy-done.10, s32[1,32]{1,0:T(1,128)S(1)} %copy-done.11, ...), custom_call_target="tpu_custom_call" | custom-call | flops 6000000000 | bytes 6000000 | tf_op jit(solution)/shard_map/pallas_call | solution.py:420
  82.7 2.3 %collective-permute-start.33 = (bf16[2,128,128]{2,1,0:T(8,128)(2,1)S(1)}, bf16[2,128,128]{2,1,0:T(8,128)(2,1)S(1)}, u32[]{:S(2)}, u32[]{:S(2)}) collective-permute-start(bf16[2,128,128]{2,1,0:T(8,128)(2,1)S(1)} %get-tuple-element.66), channel_id=1, source_target_pairs={{0,1},{1,0},{2,3},{3,2},{4,5},{5,4},{6,7},{7,6},{8,9},{9,8},{10,11... | collective-permute-start | bytes 196616 | tf_op jit(solution)/shard_map/ppermute | solution.py:434
  85.0 2.7 %collective-permute-start.15 = (bf16[4,160,128]{2,1,0:T(8,128)(2,1)S(1)}, bf16[4,160,128]{2,1,0:T(8,128)(2,1)S(1)}, u32[]{:S(2)}, u32[]{:S(2)}) collective-permute-start(bf16[4,160,128]{2,1,0:T(8,128)(2,1)S(1)} %collective-permute-done.14.rest_5_.rest_6_), channel_id=1, source_target_pairs={{0,14},{2,0},{4,2},{6,4},{8,6},{10,8},{12,10},{14,12},{1,15},{3,1}... | collective-permute-start | bytes 491528 | tf_op jit(solution)/shard_map/ppermute | solution.py:442
  90.1 5.4 %all-to-all-start.1 = ((bf16[8,128,128]{2,1,0:T(8,128)(2,1)}), bf16[8,128,128]{2,1,0:T(8,128)(2,1)S(1)}, u32[]{:S(2)}, u32[]{:S(2)}) async-start(bf16[8,128,128]{2,1,0:T(8,128)(2,1)} %shard_map.167), calls=%async_computation.1 | async-start | bytes 524288 | tf_op jit(solution)/shard_map/all_to_all | solution.py:540
  95.6 4.0 %collective-permute-start.35 = (bf16[2,128,128]{2,1,0:T(8,128)(2,1)S(1)}, bf16[2,128,128]{2,1,0:T(8,128)(2,1)S(1)}, u32[]{:S(2)}, u32[]{:S(2)}) collective-permute-start(bf16[2,128,128]{2,1,0:T(8,128)(2,1)S(1)} %get-tuple-element.68), channel_id=1, source_target_pairs={{0,17},{1,16},{16,1},{17,0},{2,19},{3,18},{18,3},{19,2},{4,21},{5,... | collective-permute-start | bytes 196616 | tf_op jit(solution)/shard_map/ppermute | solution.py:468
  102.6 7.0 %shard_map.161.near_ref = f32[4,2,128,128]{3,2,1,0:T(8,128)S(1)} custom-call(s32[1,4]{1,0:T(1,128)S(1)} %copy-done.9, s32[1,4]{1,0:T(1,128)S(1)} %copy-done.10, s32[1,32]{1,0:T(1,128)S(1)} %copy-done.11, bf16[4,2,128,128]{3,2,1,0:T(8,128)(2,1)S(1)} %copy-done.2, bf16[4,160,128]{2,1,0:T(8,128)(2,1)} %copy-done.4, bf16[4,160,128]{2,1,0:T(8,128)(2,1)} %copy-done.18, ...), custom_call_target="tpu_custom_call" | custom-call | flops 8000000000 | bytes 8000000 | tf_op jit(solution)/shard_map/pallas_call | solution.py:420
  110.5 7.6 %all-to-all-start.2 = ((bf16[16,128,128]{2,1,0:T(8,128)(2,1)}), bf16[16,128,128]{2,1,0:T(8,128)(2,1)S(1)}, u32[]{:S(2)}, u32[]{:S(2)}) async-start(bf16[16,128,128]{2,1,0:T(8,128)(2,1)} %shard_map.168), calls=%async_computation.2 | async-start | bytes 1048576 | tf_op jit(solution)/shard_map/all_to_all | solution.py:559
  118.8 3.0 %shard_map.162.sc_ref = bf16[4,128,128]{2,1,0:T(8,128)(2,1)S(1)} custom-call(s32[1,4]{1,0:T(1,128)S(1)} %copy-done.9, s32[1,4]{1,0:T(1,128)S(1)} %copy-done.10, s32[1,32]{1,0:T(1,128)S(1)} %copy-done.11, bf16[512,128]{1,0:T(8,128)(2,1)S(1)} %get-tuple-element.60.mixed_ref, s32[4,128]{1,0:T(4,128)S(1)} %bitcast.1, bf16[4,160,128]{2,1,0:T(8,128)(2,1)} %copy-done.4, ...), custom_call_target="tpu_custom_call" | custom-call | flops 2000000000 | bytes 2000000 | tf_op jit(solution)/shard_map/pallas_call | solution.py:420
  122.7 2.5 %shard_map.163 = (bf16[3,128,128]{2,1,0:T(8,128)(2,1)S(1)}, bf16[3,128,128]{2,1,0:T(8,128)(2,1)S(1)}, bf16[3,128,128]{2,1,0:T(8,128)(2,1)S(1)}, bf16[3,128,128]{2,1,0:T(8,128)(2,1)S(1)}) custom-call(s32[1,4]{1,0:T(1,128)S(1)} %copy-done.9, s32[1,4]{1,0:T(1,128)S(1)} %copy-done.10, s32[1,32]{1,0:T(1,128)S(1)} %copy-done.11, ...), custom_call_target="tpu_custom_call" | custom-call | flops 3000000000 | bytes 3000000 | tf_op jit(solution)/shard_map/pallas_call | solution.py:420
  127.5 2.8 %collective-permute-done.31.p2 = bf16[3,128,128]{2,1,0:T(8,128)(2,1)S(1)} collective-permute-done((bf16[3,128,128]{2,1,0:T(8,128)(2,1)S(1)}, bf16[3,128,128]{2,1,0:T(8,128)(2,1)S(1)}, u32[]{:S(2)}, u32[]{:S(2)}) %collective-permute-start.31) | collective-permute-done | bytes 98336 | tf_op jit(solution)/shard_map/ppermute | solution.py:434
  (132 shorter events, 37.7 us)
Async XLA Ops:
  13.2 11.2 %collective-permute-start.3 = (bf16[4,2,128,128]{3,2,1,0:T(8,128)(2,1)S(1)}, bf16[4,2,128,128]{3,2,1,0:T(8,128)(2,1)S(1)}, u32[]{:S(2)}, u32[]{:S(2)}) collective-permute-start(bf16[4,2,128,128]{3,2,1,0:T(8,128)(2,1)S(1)} %get-tuple-element.45.rest_0_.kv_ref), channel_id=1, source_target_pairs={{0,2},{2,4},{4,6},{6,8},{8,10},{10,12},{12,14},{14,0},{1,3},{3,5},... | collective-permute-start | bytes 786440 | tf_op jit(solution)/shard_map/ppermute | solution.py:438
  13.8 10.7 %collective-permute-start.16 = (bf16[4,2,128,128]{3,2,1,0:T(8,128)(2,1)S(1)}, bf16[4,2,128,128]{3,2,1,0:T(8,128)(2,1)S(1)}, u32[]{:S(2)}, u32[]{:S(2)}) collective-permute-start(bf16[4,2,128,128]{3,2,1,0:T(8,128)(2,1)S(1)} %get-tuple-element.45.rest_0_.kv_ref), channel_id=1, source_target_pairs={{0,14},{2,0},{4,2},{6,4},{8,6},{10,8},{12,10},{14,12},{1,15},{3,1}... | collective-permute-start | bytes 786440 | tf_op jit(solution)/shard_map/ppermute | solution.py:442
  17.8 9.3 %collective-permute-start.5 = (bf16[128,1024]{1,0:T(8,128)(2,1)S(1)}, bf16[128,1024]{1,0:T(8,128)(2,1)S(1)}, u32[]{:S(2)}, u32[]{:S(2)}) collective-permute-start(bf16[128,1024]{1,0:T(8,128)(2,1)S(1)} %copy-done), channel_id=1, source_target_pairs={{0,1},{1,0},{2,3},{3,2},{4,5},{5,4},{6,7},{7,6},{8,9},{9,8},{10,11... | collective-permute-start | bytes 786440 | tf_op jit(solution)/shard_map/ppermute | solution.py:434
  17.8 9.3 %collective-permute-start.6 = (bf16[128,1024]{1,0:T(8,128)(2,1)S(1)}, bf16[128,1024]{1,0:T(8,128)(2,1)S(1)}, u32[]{:S(2)}, u32[]{:S(2)}) collective-permute-start(bf16[128,1024]{1,0:T(8,128)(2,1)S(1)} %copy-done), channel_id=1, source_target_pairs={{0,16},{16,0},{1,17},{17,1},{2,18},{18,2},{3,19},{19,3},{4,20},{20... | collective-permute-start | bytes 786440 | tf_op jit(solution)/shard_map/ppermute | solution.py:434
  19.0 12.8 %collective-permute-start.7 = (bf16[128,1024]{1,0:T(8,128)(2,1)S(1)}, bf16[128,1024]{1,0:T(8,128)(2,1)S(1)}, u32[]{:S(2)}, u32[]{:S(2)}) collective-permute-start(bf16[128,1024]{1,0:T(8,128)(2,1)S(1)} %copy-done), channel_id=1, source_target_pairs={{0,17},{1,16},{16,1},{17,0},{2,19},{3,18},{18,3},{19,2},{4,21},{5,... | collective-permute-start | bytes 786440 | tf_op jit(solution)/shard_map/ppermute | solution.py:468
  24.4 8.7 %collective-permute-start.4 = (bf16[4,2,128,128]{3,2,1,0:T(8,128)(2,1)S(1)}, bf16[4,2,128,128]{3,2,1,0:T(8,128)(2,1)S(1)}, u32[]{:S(2)}, u32[]{:S(2)}) collective-permute-start(bf16[4,2,128,128]{3,2,1,0:T(8,128)(2,1)S(1)} %collective-permute-done.3.rest_1_), channel_id=1, source_target_pairs={{0,2},{2,4},{4,6},{6,8},{8,10},{10,12},{12,14},{14,0},{1,3},{3,5},... | collective-permute-start | bytes 786440 | tf_op jit(solution)/shard_map/ppermute | solution.py:438
  47.8 11.1 %collective-permute-start.10 = (bf16[4,160,128]{2,1,0:T(8,128)(2,1)S(1)}, bf16[4,160,128]{2,1,0:T(8,128)(2,1)S(1)}, u32[]{:S(2)}, u32[]{:S(2)}) collective-permute-start(bf16[4,160,128]{2,1,0:T(8,128)(2,1)S(1)} %get-tuple-element.49.q_ref.rest_0_), channel_id=1, source_target_pairs={{0,2},{2,4},{4,6},{6,8},{8,10},{10,12},{12,14},{14,0},{1,3},{3,5},... | collective-permute-start | bytes 491528 | tf_op jit(solution)/shard_map/ppermute | solution.py:438
  47.8 11.1 %collective-permute-start.13 = (bf16[4,160,128]{2,1,0:T(8,128)(2,1)S(1)}, bf16[4,160,128]{2,1,0:T(8,128)(2,1)S(1)}, u32[]{:S(2)}, u32[]{:S(2)}) collective-permute-start(bf16[4,160,128]{2,1,0:T(8,128)(2,1)S(1)} %get-tuple-element.49.q_ref.rest_0_), channel_id=1, source_target_pairs={{0,14},{2,0},{4,2},{6,4},{8,6},{10,8},{12,10},{14,12},{1,15},{3,1}... | collective-permute-start | bytes 491528 | tf_op jit(solution)/shard_map/ppermute | solution.py:442
  62.2 19.4 %collective-permute-start.22 = (bf16[4,128,128]{2,1,0:T(8,128)(2,1)S(1)}, bf16[4,128,128]{2,1,0:T(8,128)(2,1)S(1)}, u32[]{:S(2)}, u32[]{:S(2)}) collective-permute-start(bf16[4,128,128]{2,1,0:T(8,128)(2,1)S(1)} %get-tuple-element.55.da_ref.rest_7_), channel_id=1, source_target_pairs={{0,2},{2,4},{4,6},{6,8},{8,10},{10,12},{12,14},{14,0},{1,3},{3,5},... | collective-permute-start | bytes 393224 | tf_op jit(solution)/shard_map/ppermute | solution.py:438
  62.3 18.8 %collective-permute-start.25 = (bf16[4,128,128]{2,1,0:T(8,128)(2,1)S(1)}, bf16[4,128,128]{2,1,0:T(8,128)(2,1)S(1)}, u32[]{:S(2)}, u32[]{:S(2)}) collective-permute-start(bf16[4,128,128]{2,1,0:T(8,128)(2,1)S(1)} %get-tuple-element.55.da_ref.rest_7_), channel_id=1, source_target_pairs={{0,14},{2,0},{4,2},{6,4},{8,6},{10,8},{12,10},{14,12},{1,15},{3,1}... | collective-permute-start | bytes 393224 | tf_op jit(solution)/shard_map/ppermute | solution.py:442
  66.2 21.5 %all-to-all-start = ((bf16[8,128,128]{2,1,0:T(8,128)(2,1)}), bf16[8,128,128]{2,1,0:T(8,128)(2,1)S(1)}, u32[]{:S(2)}, u32[]{:S(2)}) async-start(bf16[8,128,128]{2,1,0:T(8,128)(2,1)} %shard_map.166), calls=%async_computation | async-start | bytes 524288 | tf_op jit(solution)/shard_map/all_to_all | solution.py:533
  72.5 12.5 %collective-permute-start.11 = (bf16[4,160,128]{2,1,0:T(8,128)(2,1)S(1)}, bf16[4,160,128]{2,1,0:T(8,128)(2,1)S(1)}, u32[]{:S(2)}, u32[]{:S(2)}) collective-permute-start(bf16[4,160,128]{2,1,0:T(8,128)(2,1)S(1)} %collective-permute-done.10.rest_1_), channel_id=1, source_target_pairs={{0,2},{2,4},{4,6},{6,8},{8,10},{10,12},{12,14},{14,0},{1,3},{3,5},... | collective-permute-start | bytes 491528 | tf_op jit(solution)/shard_map/ppermute | solution.py:438
  72.6 12.4 %collective-permute-start.14 = (bf16[4,160,128]{2,1,0:T(8,128)(2,1)S(1)}, bf16[4,160,128]{2,1,0:T(8,128)(2,1)S(1)}, u32[]{:S(2)}, u32[]{:S(2)}) collective-permute-start(bf16[4,160,128]{2,1,0:T(8,128)(2,1)S(1)} %collective-permute-done.13.rest_6_.rest_7_), channel_id=1, source_target_pairs={{0,14},{2,0},{4,2},{6,4},{8,6},{10,8},{12,10},{14,12},{1,15},{3,1}... | collective-permute-start | bytes 491528 | tf_op jit(solution)/shard_map/ppermute | solution.py:442
  82.7 26.9 %collective-permute-start.33 = (bf16[2,128,128]{2,1,0:T(8,128)(2,1)S(1)}, bf16[2,128,128]{2,1,0:T(8,128)(2,1)S(1)}, u32[]{:S(2)}, u32[]{:S(2)}) collective-permute-start(bf16[2,128,128]{2,1,0:T(8,128)(2,1)S(1)} %get-tuple-element.66), channel_id=1, source_target_pairs={{0,1},{1,0},{2,3},{3,2},{4,5},{5,4},{6,7},{7,6},{8,9},{9,8},{10,11... | collective-permute-start | bytes 196616 | tf_op jit(solution)/shard_map/ppermute | solution.py:434
  85.0 10.5 %collective-permute-start.12 = (bf16[4,160,128]{2,1,0:T(8,128)(2,1)S(1)}, bf16[4,160,128]{2,1,0:T(8,128)(2,1)S(1)}, u32[]{:S(2)}, u32[]{:S(2)}) collective-permute-start(bf16[4,160,128]{2,1,0:T(8,128)(2,1)S(1)} %collective-permute-done.11.rest_2_), channel_id=1, source_target_pairs={{0,2},{2,4},{4,6},{6,8},{8,10},{10,12},{12,14},{14,0},{1,3},{3,5},... | collective-permute-start | bytes 491528 | tf_op jit(solution)/shard_map/ppermute | solution.py:438
  85.0 10.6 %collective-permute-start.15 = (bf16[4,160,128]{2,1,0:T(8,128)(2,1)S(1)}, bf16[4,160,128]{2,1,0:T(8,128)(2,1)S(1)}, u32[]{:S(2)}, u32[]{:S(2)}) collective-permute-start(bf16[4,160,128]{2,1,0:T(8,128)(2,1)S(1)} %collective-permute-done.14.rest_5_.rest_6_), channel_id=1, source_target_pairs={{0,14},{2,0},{4,2},{6,4},{8,6},{10,8},{12,10},{14,12},{1,15},{3,1}... | collective-permute-start | bytes 491528 | tf_op jit(solution)/shard_map/ppermute | solution.py:442
  87.7 11.9 %collective-permute-start.27 = (bf16[4,128,128]{2,1,0:T(8,128)(2,1)S(1)}, bf16[4,128,128]{2,1,0:T(8,128)(2,1)S(1)}, u32[]{:S(2)}, u32[]{:S(2)}) collective-permute-start(bf16[4,128,128]{2,1,0:T(8,128)(2,1)S(1)} %collective-permute-done.26.rest_12_), channel_id=1, source_target_pairs={{0,14},{2,0},{4,2},{6,4},{8,6},{10,8},{12,10},{14,12},{1,15},{3,1}... | collective-permute-start | bytes 393224 | tf_op jit(solution)/shard_map/ppermute | solution.py:442
  88.0 13.4 %collective-permute-start.24 = (bf16[4,128,128]{2,1,0:T(8,128)(2,1)S(1)}, bf16[4,128,128]{2,1,0:T(8,128)(2,1)S(1)}, u32[]{:S(2)}, u32[]{:S(2)}) collective-permute-start(bf16[4,128,128]{2,1,0:T(8,128)(2,1)S(1)} %collective-permute-done.23.rest_9_), channel_id=1, source_target_pairs={{0,2},{2,4},{4,6},{6,8},{8,10},{10,12},{12,14},{14,0},{1,3},{3,5},... | collective-permute-start | bytes 393224 | tf_op jit(solution)/shard_map/ppermute | solution.py:438
  90.1 19.5 %all-to-all-start.1 = ((bf16[8,128,128]{2,1,0:T(8,128)(2,1)}), bf16[8,128,128]{2,1,0:T(8,128)(2,1)S(1)}, u32[]{:S(2)}, u32[]{:S(2)}) async-start(bf16[8,128,128]{2,1,0:T(8,128)(2,1)} %shard_map.167), calls=%async_computation.1 | async-start | bytes 524288 | tf_op jit(solution)/shard_map/all_to_all | solution.py:540
  95.5 14.1 %collective-permute-start.34 = (bf16[2,128,128]{2,1,0:T(8,128)(2,1)S(1)}, bf16[2,128,128]{2,1,0:T(8,128)(2,1)S(1)}, u32[]{:S(2)}, u32[]{:S(2)}) collective-permute-start(bf16[2,128,128]{2,1,0:T(8,128)(2,1)S(1)} %get-tuple-element.67), channel_id=1, source_target_pairs={{0,16},{16,0},{1,17},{17,1},{2,18},{18,2},{3,19},{19,3},{4,20},{20... | collective-permute-start | bytes 196616 | tf_op jit(solution)/shard_map/ppermute | solution.py:434
  95.6 14.0 %collective-permute-start.35 = (bf16[2,128,128]{2,1,0:T(8,128)(2,1)S(1)}, bf16[2,128,128]{2,1,0:T(8,128)(2,1)S(1)}, u32[]{:S(2)}, u32[]{:S(2)}) collective-permute-start(bf16[2,128,128]{2,1,0:T(8,128)(2,1)S(1)} %get-tuple-element.68), channel_id=1, source_target_pairs={{0,17},{1,16},{16,1},{17,0},{2,19},{3,18},{18,3},{19,2},{4,21},{5,... | collective-permute-start | bytes 196616 | tf_op jit(solution)/shard_map/ppermute | solution.py:468
  99.6 18.5 %collective-permute-start.28 = (bf16[4,160,128]{2,1,0:T(8,128)(2,1)S(1)}, bf16[4,160,128]{2,1,0:T(8,128)(2,1)S(1)}, u32[]{:S(2)}, u32[]{:S(2)}) collective-permute-start(bf16[4,160,128]{2,1,0:T(8,128)(2,1)S(1)} %collective-permute-done.12.rest_3_), channel_id=1, source_target_pairs={{0,2},{2,4},{4,6},{6,8},{8,10},{10,12},{12,14},{14,0},{1,3},{3,5},... | collective-permute-start | bytes 491528 | tf_op jit(solution)/shard_map/ppermute | solution.py:438
  101.4 20.4 %collective-permute-start.29 = (bf16[4,128,128]{2,1,0:T(8,128)(2,1)S(1)}, bf16[4,128,128]{2,1,0:T(8,128)(2,1)S(1)}, u32[]{:S(2)}, u32[]{:S(2)}) collective-permute-start(bf16[4,128,128]{2,1,0:T(8,128)(2,1)S(1)} %collective-permute-done.24.rest_10_), channel_id=1, source_target_pairs={{0,2},{2,4},{4,6},{6,8},{8,10},{10,12},{12,14},{14,0},{1,3},{3,5},... | collective-permute-start | bytes 393224 | tf_op jit(solution)/shard_map/ppermute | solution.py:438
  110.5 22.0 %all-to-all-start.2 = ((bf16[16,128,128]{2,1,0:T(8,128)(2,1)}), bf16[16,128,128]{2,1,0:T(8,128)(2,1)S(1)}, u32[]{:S(2)}, u32[]{:S(2)}) async-start(bf16[16,128,128]{2,1,0:T(8,128)(2,1)} %shard_map.168), calls=%async_computation.2 | async-start | bytes 1048576 | tf_op jit(solution)/shard_map/all_to_all | solution.py:559
  (46 other events, 422.4 us)

commit v3 on v2

--- a/solution.py
+++ b/solution.py
@@ -202,7 +202,7 @@
 
 
 def norm_kernel(
-    ub, tl, pk, att_ref, s0, s1, s2, s3, gate_ref, gm_ref, da_ref, gg_ref, mixed_ref
+    ub, tl, pk, att_ref, s0, s1, s2, s3, gate_ref, gm_ref, qp_ref, all_ref, gg_ref, mixed_ref
 ):
     line = iota((128, 128), 0)
     for slot in range(4):
@@ -235,7 +235,8 @@
         gate = gate_ref[slot].astype(F32)
         gmix = jnp.where(valid, gm_ref[slot], 0.0)
         da = (gmix * gate - total - normed * cross) * inv_std
-        da_ref[slot] = jnp.where(valid, da, 0.0).astype(BF16)
+        all_ref[slot, :160] = qp_ref[slot]
+        all_ref[slot, 160:] = jnp.where(valid, da, 0.0).astype(BF16)
         gg_ref[slot] = (gmix * normed).astype(BF16)
         mixed_ref[pl.ds(slot * 128, 128), :] = jnp.where(valid, normed * gate, 0.0).astype(BF16)
 
@@ -250,12 +251,17 @@
 
 
 def score_kernel(ub, tl, pk, mixed_ref, cand_ref, *rest):
-    chunks, (sc_ref,), (qp, sems) = rest[:8], rest[8:9], rest[9:]
-    copies = load_chunks(chunks, qp, sems)
+    chunks, (sc_ref,), (tables, sems) = rest[:8], rest[8:9], rest[9:]
+    copies = [
+        pltpu.make_async_copy(ref.at[:, pl.ds(128, 32)], tables.at[pl.ds(4 * i, 4)], sems.at[i])
+        for i, ref in enumerate(chunks)
+    ]
+    for copy in copies:
+        copy.start()
     row = iota((32, 128), 0)
     for copy in copies:
         copy.wait()
-    table = jnp.concatenate([qp[p, 128:160] for p in range(32)], axis=0).T
+    table = jnp.concatenate([tables[p] for p in range(32)], axis=0).T
     for slot in range(4):
         user = user_of(ub, tl, pk[0, slot_of(slot)])[0]
         cand = jnp.broadcast_to(cand_ref[pl.ds(user, 1), :], (32, 128))
@@ -266,7 +272,7 @@
         sc_ref[slot] = dot(mixed_ref[pl.ds(slot * 128, 128), :], chosen, 1, 0).astype(BF16)
 
 
-def query_kernel(ub, tl, pk, q_ref, da_ref, gg_ref, *rest):
+def query_kernel(ub, tl, pk, all_ref, gg_ref, *rest):
     chunks, outs, (kv, gq, inv, sems) = rest[:8], rest[8:12], rest[12:]
     copies = load_chunks(chunks, kv, sems)
     fill_places(pk, inv)
@@ -279,8 +285,8 @@
         logical = pk[0, slot_of(slot)]
         first = user_of(ub, tl, logical)[1]
         own = logical - first
-        query = q_ref[slot, :128]
-        grad = da_ref[slot]
+        query = all_ref[slot, :128]
+        grad = all_ref[slot, 160:]
 
         def step(j, acc):
             places = [inv[first + jnp.minimum(4 * j + i, own)] for i in range(4)]
@@ -323,11 +329,11 @@
 
 
 def key_near_kernel(ub, tl, pk, kv_ref, *rest):
-    qs, das, (sum_ref,), (qbuf, dbuf, inv, sems) = rest[:7], rest[7:14], rest[14:15], rest[15:]
-    copies = []
-    for i, c in enumerate((0, 1, 2, 3, 5, 6, 7)):
-        copies.append(pltpu.make_async_copy(qs[i], qbuf.at[pl.ds(4 * c, 4)], sems.at[i]))
-        copies.append(pltpu.make_async_copy(das[i], dbuf.at[pl.ds(4 * c, 4)], sems.at[7 + i]))
+    chunks, (sum_ref,), (buf, inv, sems) = rest[:7], rest[7:8], rest[8:]
+    copies = [
+        pltpu.make_async_copy(ref, buf.at[pl.ds(4 * c, 4)], sems.at[c])
+        for c, ref in zip((0, 1, 2, 3, 5, 6, 7), chunks)
+    ]
     for copy in copies:
         copy.start()
     fill_places(pk, inv)
@@ -347,8 +353,8 @@
                 late = (place // 4 == 4) | (entry >= count)
                 spots.append(jnp.where(late, 0, place))
                 reach.append(jnp.where(late, 1, jnp.where(entry == 0, 0, -1)))
-            queries = jnp.concatenate([qbuf[p, :128] for p in spots], axis=0)
-            grads = jnp.concatenate([dbuf[p] for p in spots], axis=0)
+            queries = jnp.concatenate([buf[p, :128] for p in spots], axis=0)
+            grads = jnp.concatenate([buf[p, 160:] for p in spots], axis=0)
             return key_step(kv_ref[slot, 0], kv_ref[slot, 1], queries, grads, reach, carry)
 
         zero = jnp.zeros((128, 128), F32)
@@ -360,7 +366,13 @@
     lax.fori_loop(0, 4, one, 0)
 
 
-def key_far_kernel(ub, tl, pk, kv_ref, near_ref, q_ref, da_ref, sc_ref, o0, o1, o2, o3, both):
+def key_far_kernel(
+    ub, tl, pk, kv_ref, near_ref, sc_ref, all_ref, o0, o1, o2, o3, both, buf, sem
+):
+    copy = pltpu.make_async_copy(all_ref, buf, sem)
+    copy.start()
+    copy.wait()
+
     def one(slot, carry):
         logical = pk[0, slot_of(slot)]
         user, first, blocks, tail = user_of(ub, tl, logical)
@@ -368,8 +380,8 @@
         for i in range(4):
             other = pk[0, slot_of(16 + i)]
             reach.append(jnp.where((other > logical) & (other < first + blocks), -1, 1))
-        queries = jnp.concatenate([q_ref[i, :128] for i in range(4)], axis=0)
-        grads = jnp.concatenate([da_ref[i] for i in range(4)], axis=0)
+        queries = jnp.concatenate([buf[i, :128] for i in range(4)], axis=0)
+        grads = jnp.concatenate([buf[i, 160:] for i in range(4)], axis=0)
         gk, gv = key_step(
             kv_ref[slot, 0], kv_ref[slot, 1], queries, grads, reach,
             (near_ref[slot, 0], near_ref[slot, 1]),
@@ -515,65 +527,64 @@
         facts + vm(qp, gate_h, gm, att_near, kvs[4]),
         [(block, F32), ((4, 8, 128), F32)],
     )
-    qps = ring(after(qp, kvs[4]), lambda n: [])
     all_stats = swap([stats] * 4)
-    da, gg, mixed = call(
+    both, gg, mixed = call(
         norm_kernel,
-        facts + vm(after(att, qps[1], qps[7]), *all_stats, gate_h, gm),
-        [(block, BF16), (block, BF16), ((512, 128), BF16)],
+        facts + vm(att, *all_stats, gate_h, gm, qp),
+        [((4, 288, 128), BF16), (block, BF16), ((512, 128), BF16)],
     )
     (gw,) = call(weight_kernel, vm(mixed, *cots), [((8, 128, 128), BF16)])
+    parts = lax.all_to_all(gw, ("xh", "y"), split_axis=0, concat_axis=0, tiled=True)
+    ups, downs = [both, up(both)], [both, down(both)]
     early = call(
         query_kernel,
-        facts + vm(qp, da, gg) + raw(kvs),
+        facts + vm(after(both, ups[1], downs[1]), gg) + raw(kvs),
         [((2, 128, 128), BF16)] * 4,
         [kv_buffer, pltpu.VMEM(block, BF16), places, sems],
-        us=6,
-    )
-    parts = lax.all_to_all(gw, ("xh", "y"), split_axis=0, concat_axis=0, tiled=True)
-    ups, downs = [da, up(da)], [da, down(da)]
+        us=8,
+    )
+    ups.append(up(ups[1]))
+    downs.append(down(downs[1]))
     (piece,) = call(
         functools.partial(sum_kernel, 8),
-        vm(after(parts, ups[1], downs[1], qps[2], qps[6], early[0])),
+        vm(after(parts, ups[2], downs[2], early[0])),
         [((8, 128, 128), BF16)],
+        us=8,
     )
     line = lax.all_to_all(piece, "z", split_axis=0, concat_axis=0, tiled=True)
-    ups.append(up(after(ups[1], early[0])))
-    downs.append(down(after(downs[1], early[0])))
     ups.append(up(ups[2]))
     downs.append(down(downs[2]))
     ups.append(up(ups[3]))
-    das = ups + downs[:0:-1]
+    pairs = ups + downs[:0:-1]
     (sc,) = call(
         score_kernel,
-        facts + vm(mixed, cand_ids[0]) + raw(qps),
+        facts + vm(mixed, cand_ids[0]) + raw(pairs),
         [(block, BF16)],
-        [pltpu.VMEM((32, 160, 128), BF16), sems],
+        [pltpu.VMEM((32, 32, 128), BF16), sems],
     )
     early = swap(early)
     (lines,) = call(
         functools.partial(sum_kernel, 16),
-        vm(after(line, ups[2], downs[2], *early[1:])),
+        vm(after(line, ups[3], downs[3], *early[1:])),
         [((16, 128, 128), BF16)],
     )
     near = lax.all_to_all(lines, ("xh", "y", "xl"), split_axis=0, concat_axis=0, tiled=True)
     (key_sums,) = call(
         key_near_kernel,
-        facts + vm(kv) + raw(qps[:4] + qps[5:]) + raw(das[:4] + das[5:]),
+        facts + vm(kv) + raw(pairs[:4] + pairs[5:]),
         [((4, 2, 128, 128), F32)],
-        [
-            pltpu.VMEM((32, 160, 128), BF16),
-            pltpu.VMEM((32, 128, 128), BF16),
-            places,
-            pltpu.SemaphoreType.DMA((14,)),
-        ],
+        [pltpu.VMEM((32, 288, 128), BF16), places, sems],
         us=8,
     )
     late = call(
         key_far_kernel,
-        facts + vm(kv, key_sums, qps[4], das[4], sc),
+        facts + vm(kv, key_sums, sc) + raw([pairs[4]]),
         [((3, 128, 128), BF16)] * 4,
-        [pltpu.VMEM((4, 2, 128, 128), BF16)],
+        [
+            pltpu.VMEM((4, 2, 128, 128), BF16),
+            pltpu.VMEM((4, 288, 128), BF16),
+            pltpu.SemaphoreType.DMA,
+        ],
         us=3,
     )
     late = swap(late)

time: 136 us -> 130 us (0.956)
  starting transfers between devices: 67.8 us -> 58.6 us
  waiting for transfers between devices: 27.7 us -> 30.4 us
    ppermute x12 -> x8, starting transfers between devices: 5.91 us -> 1.5 us  [up(): return lax.ppermute(array, 'z', [(i, (i + 1) % 8) for i in range(8)])]
    ppermute x9 -> x6, starting transfers between devices: 20.8 us -> 17.3 us  [down(): return lax.ppermute(array, 'z', [(i, (i + 7) % 8) for i in range(8)])]
    ppermute x5, starting transfers between devices: 7.52 us -> 5.19 us  [swap(): lax.ppermute(pieces[3], ('xl', 'core'), [(i, 3 - i) for i in range(4)])]
    all_to_all x1, waiting for transfers between devices: 0.01 us -> 2.22 us  [body(): line = lax.all_to_all(piece, 'z', split_axis=0, concat_axis=0, tiled=True)]
    ppermute x11, starting transfers between devices: 14.2 us -> 16.2 us  [flip(): return lax.ppermute(array, axis, [(0, 1), (1, 0)])]
    ppermute x12 -> x8, waiting for transfers between devices: 10.2 us -> 10.6 us  [up(): return lax.ppermute(array, 'z', [(i, (i + 1) % 8) for i in range(8)])]
  transfers between devices with their start and end apart: 40 -> 33, of which waited for: 10 -> 12; matrix products, arithmetic and copies ran while one was open for 0% -> 0% of each run, Pallas kernels for 24% -> 23%
where the time goes in v3:
time: 130 us; the launch traced here: 129 us
  starting transfers between devices  58.6 us (45%)
  Pallas kernels  37 us (28%)
  waiting for transfers between devices  30.4 us (23%)
  local copies, waits for them, and re-layouts  2.29 us (2%)
    pallas_call x16, Pallas kernels, call(): pl.pallas_call(kernel, in_specs=[spec for spec, _ in ins], out_specs=[VM]...  37 us
    ppermute x6, starting transfers between devices, down(): return lax.ppermute(array, 'z', [(i, (i + 7) % 8) for i in range(8)])  17.3 us
    ppermute x11, starting transfers between devices, flip(): return lax.ppermute(array, axis, [(0, 1), (1, 0)])  16.2 us
    ppermute x5, waiting for transfers between devices, swap(): lax.ppermute(pieces[3], ('xl', 'core'), [(i, 3 - i) for i in range(4)])  13.7 us
    ppermute x8, waiting for transfers between devices, up(): return lax.ppermute(array, 'z', [(i, (i + 1) % 8) for i in range(8)])  10.6 us
    all_to_all x1, starting transfers between devices, body(): lax.all_to_all(lines, ('xh', 'y', 'xl'), split_axis=0, concat_axis=0, til...  6.5 us
    all_to_all x1, starting transfers between devices, body(): lax.all_to_all(gw, ('xh', 'y'), split_axis=0, concat_axis=0, tiled=True)  6.35 us
    all_to_all x1, starting transfers between devices, body(): line = lax.all_to_all(piece, 'z', split_axis=0, concat_axis=0, tiled=True)  5.41 us
  transfers between devices with their start and end apart: 33, of which 12 were waited for; matrix products, arithmetic and copies ran while one was open for 0% of the time, Pallas kernels for 23%

profile of v3, /device:TPU:1, one launch (start us, length us, event | category | flops | bytes accessed | tf_op | source)
XLA Modules:
  0.0 129.3 jit_solution(2008970554239408211)
XLA Ops:
  2.6 2.1 %collective-permute-start.1 = (bf16[544,128]{1,0:T(8,128)(2,1)S(1)}, bf16[544,128]{1,0:T(8,128)(2,1)S(1)}, u32[]{:S(2)}, u32[]{:S(2)}) collective-permute-start(bf16[544,128]{1,0:T(8,128)(2,1)S(1)} %get-tuple-element.40), channel_id=1, source_target_pairs={{0,16},{16,0},{1,17},{17,1},{2,18},{18,2},{3,19},{19,3},{4,20},{20... | collective-permute-start | bytes 417800 | tf_op jit(solution)/shard_map/ppermute | solution.py:446
  7.6 5.5 %collective-permute-done.2.p3 = bf16[544,128]{1,0:T(8,128)(2,1)S(1)} collective-permute-done((bf16[544,128]{1,0:T(8,128)(2,1)S(1)}, bf16[544,128]{1,0:T(8,128)(2,1)S(1)}, u32[]{:S(2)}, u32[]{:S(2)}) %collective-permute-start.2) | collective-permute-done | bytes 139296 | tf_op jit(solution)/shard_map/ppermute | solution.py:480
  13.7 4.0 %collective-permute-start.9 = (bf16[4,2,128,128]{3,2,1,0:T(8,128)(2,1)S(1)}, bf16[4,2,128,128]{3,2,1,0:T(8,128)(2,1)S(1)}, u32[]{:S(2)}, u32[]{:S(2)}) collective-permute-start(bf16[4,2,128,128]{3,2,1,0:T(8,128)(2,1)S(1)} %get-tuple-element.42.rest_0_.kv_ref), channel_id=1, source_target_pairs={{0,14},{2,0},{4,2},{6,4},{8,6},{10,8},{12,10},{14,12},{1,15},{3,1}... | collective-permute-start | bytes 786440 | tf_op jit(solution)/shard_map/ppermute | solution.py:454
  19.9 4.5 %collective-permute-done.6.rest_1_ = bf16[4,2,128,128]{3,2,1,0:T(8,128)(2,1)S(1)} collective-permute-done((bf16[4,2,128,128]{3,2,1,0:T(8,128)(2,1)S(1)}, bf16[4,2,128,128]{3,2,1,0:T(8,128)(2,1)S(1)}, u32[]{:S(2)}, u32[]{:S(2)}) %collective-permute-start.6) | collective-permute-done | bytes 262176 | tf_op jit(solution)/shard_map/ppermute | solution.py:450
  24.4 2.7 %collective-permute-start.10 = (bf16[4,2,128,128]{3,2,1,0:T(8,128)(2,1)S(1)}, bf16[4,2,128,128]{3,2,1,0:T(8,128)(2,1)S(1)}, u32[]{:S(2)}, u32[]{:S(2)}) collective-permute-start(bf16[4,2,128,128]{3,2,1,0:T(8,128)(2,1)S(1)} %collective-permute-done.9.rest_6_.rest_7_), channel_id=1, source_target_pairs={{0,14},{2,0},{4,2},{6,4},{8,6},{10,8},{12,10},{14,12},{1,15},{3,1}... | collective-permute-start | bytes 786440 | tf_op jit(solution)/shard_map/ppermute | solution.py:454
  27.1 4.6 %collective-permute-done.5.c3 = bf16[128,1024]{1,0:T(8,128)(2,1)S(1)} collective-permute-done((bf16[128,1024]{1,0:T(8,128)(2,1)S(1)}, bf16[128,1024]{1,0:T(8,128)(2,1)S(1)}, u32[]{:S(2)}, u32[]{:S(2)}) %collective-permute-start.5) | collective-permute-done | bytes 262176 | tf_op jit(solution)/shard_map/ppermute | solution.py:480
  33.1 2.7 %collective-permute-start.11 = (bf16[4,2,128,128]{3,2,1,0:T(8,128)(2,1)S(1)}, bf16[4,2,128,128]{3,2,1,0:T(8,128)(2,1)S(1)}, u32[]{:S(2)}, u32[]{:S(2)}) collective-permute-start(bf16[4,2,128,128]{3,2,1,0:T(8,128)(2,1)S(1)} %collective-permute-done.10.rest_5_.rest_6_), channel_id=1, source_target_pairs={{0,14},{2,0},{4,2},{6,4},{8,6},{10,8},{12,10},{14,12},{1,15},{3,1}... | collective-permute-start | bytes 786440 | tf_op jit(solution)/shard_map/ppermute | solution.py:454
  37.3 3.6 %collective-permute-done.8.rest_3_ = bf16[4,2,128,128]{3,2,1,0:T(8,128)(2,1)S(1)} collective-permute-done((bf16[4,2,128,128]{3,2,1,0:T(8,128)(2,1)S(1)}, bf16[4,2,128,128]{3,2,1,0:T(8,128)(2,1)S(1)}, u32[]{:S(2)}, u32[]{:S(2)}) %collective-permute-start.8) | collective-permute-done | bytes 262176 | tf_op jit(solution)/shard_map/ppermute | solution.py:450
  41.7 5.8 %shard_map.157.near_ref = f32[4,128,128]{2,1,0:T(8,128)S(1)} custom-call(s32[1,4]{1,0:T(1,128)S(1)} %copy-done.6, s32[1,4]{1,0:T(1,128)S(1)} %copy-done.7, s32[1,32]{1,0:T(1,128)S(1)} %copy-done.8, bf16[4,160,128]{2,1,0:T(8,128)(2,1)S(1)} %get-tuple-element.43.q_ref.qp_ref, bf16[4,2,128,128]{3,2,1,0:T(8,128)(2,1)} %copy-done.2, ...), custom_call_target="tpu_custom_call" | custom-call | flops 6000000000 | bytes 6000000 | tf_op jit(solution)/shard_map/pallas_call | solution.py:432
  47.8 2.8 %shard_map.158 = (f32[4,128,128]{2,1,0:T(8,128)S(1)}, f32[4,8,128]{2,1,0:T(8,128)S(1)}) custom-call(s32[1,4]{1,0:T(1,128)S(1)} %copy-done.6, s32[1,4]{1,0:T(1,128)S(1)} %copy-done.7, s32[1,32]{1,0:T(1,128)S(1)} %copy-done.8, bf16[4,160,128]{2,1,0:T(8,128)(2,1)S(1)} %get-tuple-element.43.q_ref.qp_ref, bf16[4,128,128]{2,1,0:T(8,128)(2,1)S(1)} %get-tuple-element.44.gate_ref, ...), custom_call_target="tpu_custom_call" | custom-call | flops 2000000000 | bytes 2000000 | tf_op jit(solution)/shard_map/pallas_call | solution.py:432
  50.6 3.1 %collective-permute-start.13 = (f32[4,8,128]{2,1,0:T(8,128)S(1)}, f32[4,8,128]{2,1,0:T(8,128)S(1)}, u32[]{:S(2)}, u32[]{:S(2)}) collective-permute-start(f32[4,8,128]{2,1,0:T(8,128)S(1)} %get-tuple-element.49.s0), channel_id=1, source_target_pairs={{0,1},{1,0},{2,3},{3,2},{4,5},{5,4},{6,7},{7,6},{8,9},{9,8},{10,11... | collective-permute-start | bytes 49160 | tf_op jit(solution)/shard_map/ppermute | solution.py:446
  58.9 2.7 %collective-permute-start.19 = (bf16[4,288,128]{2,1,0:T(8,128)(2,1)S(1)}, bf16[4,288,128]{2,1,0:T(8,128)(2,1)S(1)}, u32[]{:S(2)}, u32[]{:S(2)}) collective-permute-start(bf16[4,288,128]{2,1,0:T(8,128)(2,1)S(1)} %get-tuple-element.57.rest_0_.all_ref), channel_id=1, source_target_pairs={{0,14},{2,0},{4,2},{6,4},{8,6},{10,8},{12,10},{14,12},{1,15},{3,1}... | collective-permute-start | bytes 884744 | tf_op jit(solution)/shard_map/ppermute | solution.py:454
  62.7 6.4 %all-to-all-start = ((bf16[8,128,128]{2,1,0:T(8,128)(2,1)}), bf16[8,128,128]{2,1,0:T(8,128)(2,1)S(1)}, u32[]{:S(2)}, u32[]{:S(2)}) async-start(bf16[8,128,128]{2,1,0:T(8,128)(2,1)} %shard_map.166), calls=%async_computation | async-start | bytes 524288 | tf_op jit(solution)/shard_map/all_to_all | solution.py:537
  69.2 2.7 %collective-permute-start.20 = (bf16[4,288,128]{2,1,0:T(8,128)(2,1)S(1)}, bf16[4,288,128]{2,1,0:T(8,128)(2,1)S(1)}, u32[]{:S(2)}, u32[]{:S(2)}) collective-permute-start(bf16[4,288,128]{2,1,0:T(8,128)(2,1)S(1)} %collective-permute-done.19.rest_6_.rest_7_), channel_id=1, source_target_pairs={{0,14},{2,0},{4,2},{6,4},{8,6},{10,8},{12,10},{14,12},{1,15},{3,1}... | collective-permute-start | bytes 884744 | tf_op jit(solution)/shard_map/ppermute | solution.py:454
  71.9 6.2 %shard_map.164 = (bf16[2,128,128]{2,1,0:T(8,128)(2,1)S(1)}, bf16[2,128,128]{2,1,0:T(8,128)(2,1)S(1)}, bf16[2,128,128]{2,1,0:T(8,128)(2,1)S(1)}, bf16[2,128,128]{2,1,0:T(8,128)(2,1)S(1)}) custom-call(s32[1,4]{1,0:T(1,128)S(1)} %copy-done.6, s32[1,4]{1,0:T(1,128)S(1)} %copy-done.7, s32[1,32]{1,0:T(1,128)S(1)} %copy-done.8, ...), custom_call_target="tpu_custom_call" | custom-call | flops 8000000000 | bytes 8000000 | tf_op jit(solution)/shard_map/pallas_call | solution.py:432
  81.9 2.7 %collective-permute-start.21 = (bf16[4,288,128]{2,1,0:T(8,128)(2,1)S(1)}, bf16[4,288,128]{2,1,0:T(8,128)(2,1)S(1)}, u32[]{:S(2)}, u32[]{:S(2)}) collective-permute-start(bf16[4,288,128]{2,1,0:T(8,128)(2,1)S(1)} %collective-permute-done.20.rest_5_.rest_6_), channel_id=1, source_target_pairs={{0,14},{2,0},{4,2},{6,4},{8,6},{10,8},{12,10},{14,12},{1,15},{3,1}... | collective-permute-start | bytes 884744 | tf_op jit(solution)/shard_map/ppermute | solution.py:454
  85.3 5.4 %all-to-all-start.1 = ((bf16[8,128,128]{2,1,0:T(8,128)(2,1)}), bf16[8,128,128]{2,1,0:T(8,128)(2,1)S(1)}, u32[]{:S(2)}, u32[]{:S(2)}) async-start(bf16[8,128,128]{2,1,0:T(8,128)(2,1)} %shard_map.167), calls=%async_computation.1 | async-start | bytes 524288 | tf_op jit(solution)/shard_map/all_to_all | solution.py:554
  93.0 5.8 %shard_map.160.near_ref = f32[4,2,128,128]{3,2,1,0:T(8,128)S(1)} custom-call(s32[1,4]{1,0:T(1,128)S(1)} %copy-done.6, s32[1,4]{1,0:T(1,128)S(1)} %copy-done.7, s32[1,32]{1,0:T(1,128)S(1)} %copy-done.8, bf16[4,2,128,128]{3,2,1,0:T(8,128)(2,1)S(1)} %copy-done.3, bf16[4,288,128]{2,1,0:T(8,128)(2,1)} %copy-done, bf16[4,288,128]{2,1,0:T(8,128)(2,1)} %copy-done.9, ...), custom_call_target="tpu_custom_call" | custom-call | flops 8000000000 | bytes 8000000 | tf_op jit(solution)/shard_map/pallas_call | solution.py:432
  98.9 2.2 %all-to-all-done.1.parts_ref = bf16[8,128,128]{2,1,0:T(8,128)(2,1)S(1)} async-done(((bf16[8,128,128]{2,1,0:T(8,128)(2,1)}), bf16[8,128,128]{2,1,0:T(8,128)(2,1)S(1)}, u32[]{:S(2)}, u32[]{:S(2)}) %all-to-all-start.1) | async-done | bytes 262176 | tf_op jit(solution)/shard_map/all_to_all | solution.py:554
  101.9 6.5 %all-to-all-start.2 = ((bf16[16,128,128]{2,1,0:T(8,128)(2,1)}), bf16[16,128,128]{2,1,0:T(8,128)(2,1)S(1)}, u32[]{:S(2)}, u32[]{:S(2)}) async-start(bf16[16,128,128]{2,1,0:T(8,128)(2,1)} %shard_map.168), calls=%async_computation.2 | async-start | bytes 1048576 | tf_op jit(solution)/shard_map/all_to_all | solution.py:571
  109.2 2.5 %shard_map.161.sc_ref = bf16[4,128,128]{2,1,0:T(8,128)(2,1)S(1)} custom-call(s32[1,4]{1,0:T(1,128)S(1)} %copy-done.6, s32[1,4]{1,0:T(1,128)S(1)} %copy-done.7, s32[1,32]{1,0:T(1,128)S(1)} %copy-done.8, bf16[512,128]{1,0:T(8,128)(2,1)S(1)} %get-tuple-element.51.mixed_ref, s32[4,128]{1,0:T(4,128)S(1)} %bitcast.1, bf16[4,288,128]{2,1,0:T(8,128)(2,1)} %copy-done, ...), custom_call_target="tpu_custom_call" | custom-call | flops 2000000000 | bytes 2000000 | tf_op jit(solution)/shard_map/pallas_call | solution.py:432
  111.7 3.5 %shard_map.162 = (bf16[3,128,128]{2,1,0:T(8,128)(2,1)S(1)}, bf16[3,128,128]{2,1,0:T(8,128)(2,1)S(1)}, bf16[3,128,128]{2,1,0:T(8,128)(2,1)S(1)}, bf16[3,128,128]{2,1,0:T(8,128)(2,1)S(1)}) custom-call(s32[1,4]{1,0:T(1,128)S(1)} %copy-done.6, s32[1,4]{1,0:T(1,128)S(1)} %copy-done.7, s32[1,32]{1,0:T(1,128)S(1)} %copy-done.8, ...), custom_call_target="tpu_custom_call" | custom-call | flops 3000000000 | bytes 3000000 | tf_op jit(solution)/shard_map/pallas_call | solution.py:432
  115.2 3.8 %collective-permute-start.23 = (bf16[3,128,128]{2,1,0:T(8,128)(2,1)S(1)}, bf16[3,128,128]{2,1,0:T(8,128)(2,1)S(1)}, u32[]{:S(2)}, u32[]{:S(2)}) collective-permute-start(bf16[3,128,128]{2,1,0:T(8,128)(2,1)S(1)} %get-tuple-element.53), channel_id=1, source_target_pairs={{0,1},{1,0},{2,3},{3,2},{4,5},{5,4},{6,7},{7,6},{8,9},{9,8},{10,11... | collective-permute-start | bytes 294920 | tf_op jit(solution)/shard_map/ppermute | solution.py:446
  120.7 3.0 %collective-permute-done.24.p2 = bf16[3,128,128]{2,1,0:T(8,128)(2,1)S(1)} collective-permute-done((bf16[3,128,128]{2,1,0:T(8,128)(2,1)S(1)}, bf16[3,128,128]{2,1,0:T(8,128)(2,1)S(1)}, u32[]{:S(2)}, u32[]{:S(2)}) %collective-permute-start.24) | collective-permute-done | bytes 98336 | tf_op jit(solution)/shard_map/ppermute | solution.py:446
  (102 shorter events, 33.5 us)
Async XLA Ops:
  6.1 7.1 %collective-permute-start.2 = (bf16[544,128]{1,0:T(8,128)(2,1)S(1)}, bf16[544,128]{1,0:T(8,128)(2,1)S(1)}, u32[]{:S(2)}, u32[]{:S(2)}) collective-permute-start(bf16[544,128]{1,0:T(8,128)(2,1)S(1)} %get-tuple-element.41), channel_id=1, source_target_pairs={{0,17},{1,16},{16,1},{17,0},{2,19},{3,18},{18,3},{19,2},{4,21},{5,... | collective-permute-start | bytes 417800 | tf_op jit(solution)/shard_map/ppermute | solution.py:480
  13.2 11.2 %collective-permute-start.6 = (bf16[4,2,128,128]{3,2,1,0:T(8,128)(2,1)S(1)}, bf16[4,2,128,128]{3,2,1,0:T(8,128)(2,1)S(1)}, u32[]{:S(2)}, u32[]{:S(2)}) collective-permute-start(bf16[4,2,128,128]{3,2,1,0:T(8,128)(2,1)S(1)} %get-tuple-element.42.rest_0_.kv_ref), channel_id=1, source_target_pairs={{0,2},{2,4},{4,6},{6,8},{8,10},{10,12},{12,14},{14,0},{1,3},{3,5},... | collective-permute-start | bytes 786440 | tf_op jit(solution)/shard_map/ppermute | solution.py:450
  13.7 10.7 %collective-permute-start.9 = (bf16[4,2,128,128]{3,2,1,0:T(8,128)(2,1)S(1)}, bf16[4,2,128,128]{3,2,1,0:T(8,128)(2,1)S(1)}, u32[]{:S(2)}, u32[]{:S(2)}) collective-permute-start(bf16[4,2,128,128]{3,2,1,0:T(8,128)(2,1)S(1)} %get-tuple-element.42.rest_0_.kv_ref), channel_id=1, source_target_pairs={{0,14},{2,0},{4,2},{6,4},{8,6},{10,8},{12,10},{14,12},{1,15},{3,1}... | collective-permute-start | bytes 786440 | tf_op jit(solution)/shard_map/ppermute | solution.py:454
  17.8 9.3 %collective-permute-start.3 = (bf16[128,1024]{1,0:T(8,128)(2,1)S(1)}, bf16[128,1024]{1,0:T(8,128)(2,1)S(1)}, u32[]{:S(2)}, u32[]{:S(2)}) collective-permute-start(bf16[128,1024]{1,0:T(8,128)(2,1)S(1)} %copy-done.1), channel_id=1, source_target_pairs={{0,1},{1,0},{2,3},{3,2},{4,5},{5,4},{6,7},{7,6},{8,9},{9,8},{10,11... | collective-permute-start | bytes 786440 | tf_op jit(solution)/shard_map/ppermute | solution.py:446
  17.8 9.3 %collective-permute-start.4 = (bf16[128,1024]{1,0:T(8,128)(2,1)S(1)}, bf16[128,1024]{1,0:T(8,128)(2,1)S(1)}, u32[]{:S(2)}, u32[]{:S(2)}) collective-permute-start(bf16[128,1024]{1,0:T(8,128)(2,1)S(1)} %copy-done.1), channel_id=1, source_target_pairs={{0,16},{16,0},{1,17},{17,1},{2,18},{18,2},{3,19},{19,3},{4,20},{20... | collective-permute-start | bytes 786440 | tf_op jit(solution)/shard_map/ppermute | solution.py:446
  19.0 12.8 %collective-permute-start.5 = (bf16[128,1024]{1,0:T(8,128)(2,1)S(1)}, bf16[128,1024]{1,0:T(8,128)(2,1)S(1)}, u32[]{:S(2)}, u32[]{:S(2)}) collective-permute-start(bf16[128,1024]{1,0:T(8,128)(2,1)S(1)} %copy-done.1), channel_id=1, source_target_pairs={{0,17},{1,16},{16,1},{17,0},{2,19},{3,18},{18,3},{19,2},{4,21},{5,... | collective-permute-start | bytes 786440 | tf_op jit(solution)/shard_map/ppermute | solution.py:480
  24.4 8.7 %collective-permute-start.7 = (bf16[4,2,128,128]{3,2,1,0:T(8,128)(2,1)S(1)}, bf16[4,2,128,128]{3,2,1,0:T(8,128)(2,1)S(1)}, u32[]{:S(2)}, u32[]{:S(2)}) collective-permute-start(bf16[4,2,128,128]{3,2,1,0:T(8,128)(2,1)S(1)} %collective-permute-done.6.rest_1_), channel_id=1, source_target_pairs={{0,2},{2,4},{4,6},{6,8},{8,10},{10,12},{12,14},{14,0},{1,3},{3,5},... | collective-permute-start | bytes 786440 | tf_op jit(solution)/shard_map/ppermute | solution.py:450
  24.4 8.7 %collective-permute-start.10 = (bf16[4,2,128,128]{3,2,1,0:T(8,128)(2,1)S(1)}, bf16[4,2,128,128]{3,2,1,0:T(8,128)(2,1)S(1)}, u32[]{:S(2)}, u32[]{:S(2)}) collective-permute-start(bf16[4,2,128,128]{3,2,1,0:T(8,128)(2,1)S(1)} %collective-permute-done.9.rest_6_.rest_7_), channel_id=1, source_target_pairs={{0,14},{2,0},{4,2},{6,4},{8,6},{10,8},{12,10},{14,12},{1,15},{3,1}... | collective-permute-start | bytes 786440 | tf_op jit(solution)/shard_map/ppermute | solution.py:454
  33.1 7.8 %collective-permute-start.8 = (bf16[4,2,128,128]{3,2,1,0:T(8,128)(2,1)S(1)}, bf16[4,2,128,128]{3,2,1,0:T(8,128)(2,1)S(1)}, u32[]{:S(2)}, u32[]{:S(2)}) collective-permute-start(bf16[4,2,128,128]{3,2,1,0:T(8,128)(2,1)S(1)} %collective-permute-done.7.rest_2_), channel_id=1, source_target_pairs={{0,2},{2,4},{4,6},{6,8},{8,10},{10,12},{12,14},{14,0},{1,3},{3,5},... | collective-permute-start | bytes 786440 | tf_op jit(solution)/shard_map/ppermute | solution.py:450
  33.1 7.8 %collective-permute-start.11 = (bf16[4,2,128,128]{3,2,1,0:T(8,128)(2,1)S(1)}, bf16[4,2,128,128]{3,2,1,0:T(8,128)(2,1)S(1)}, u32[]{:S(2)}, u32[]{:S(2)}) collective-permute-start(bf16[4,2,128,128]{3,2,1,0:T(8,128)(2,1)S(1)} %collective-permute-done.10.rest_5_.rest_6_), channel_id=1, source_target_pairs={{0,14},{2,0},{4,2},{6,4},{8,6},{10,8},{12,10},{14,12},{1,15},{3,1}... | collective-permute-start | bytes 786440 | tf_op jit(solution)/shard_map/ppermute | solution.py:454
  40.9 6.9 %collective-permute-start.12 = (bf16[4,2,128,128]{3,2,1,0:T(8,128)(2,1)S(1)}, bf16[4,2,128,128]{3,2,1,0:T(8,128)(2,1)S(1)}, u32[]{:S(2)}, u32[]{:S(2)}) collective-permute-start(bf16[4,2,128,128]{3,2,1,0:T(8,128)(2,1)S(1)} %collective-permute-done.8.rest_3_), channel_id=1, source_target_pairs={{0,2},{2,4},{4,6},{6,8},{8,10},{10,12},{12,14},{14,0},{1,3},{3,5},... | collective-permute-start | bytes 786440 | tf_op jit(solution)/shard_map/ppermute | solution.py:450
  58.8 10.3 %collective-permute-start.16 = (bf16[4,288,128]{2,1,0:T(8,128)(2,1)S(1)}, bf16[4,288,128]{2,1,0:T(8,128)(2,1)S(1)}, u32[]{:S(2)}, u32[]{:S(2)}) collective-permute-start(bf16[4,288,128]{2,1,0:T(8,128)(2,1)S(1)} %get-tuple-element.57.rest_0_.all_ref), channel_id=1, source_target_pairs={{0,2},{2,4},{4,6},{6,8},{8,10},{10,12},{12,14},{14,0},{1,3},{3,5},... | collective-permute-start | bytes 884744 | tf_op jit(solution)/shard_map/ppermute | solution.py:450
  58.9 10.2 %collective-permute-start.19 = (bf16[4,288,128]{2,1,0:T(8,128)(2,1)S(1)}, bf16[4,288,128]{2,1,0:T(8,128)(2,1)S(1)}, u32[]{:S(2)}, u32[]{:S(2)}) collective-permute-start(bf16[4,288,128]{2,1,0:T(8,128)(2,1)S(1)} %get-tuple-element.57.rest_0_.all_ref), channel_id=1, source_target_pairs={{0,14},{2,0},{4,2},{6,4},{8,6},{10,8},{12,10},{14,12},{1,15},{3,1}... | collective-permute-start | bytes 884744 | tf_op jit(solution)/shard_map/ppermute | solution.py:454
  62.7 19.0 %all-to-all-start = ((bf16[8,128,128]{2,1,0:T(8,128)(2,1)}), bf16[8,128,128]{2,1,0:T(8,128)(2,1)S(1)}, u32[]{:S(2)}, u32[]{:S(2)}) async-start(bf16[8,128,128]{2,1,0:T(8,128)(2,1)} %shard_map.166), calls=%async_computation | async-start | bytes 524288 | tf_op jit(solution)/shard_map/all_to_all | solution.py:537
  69.1 12.6 %collective-permute-start.17 = (bf16[4,288,128]{2,1,0:T(8,128)(2,1)S(1)}, bf16[4,288,128]{2,1,0:T(8,128)(2,1)S(1)}, u32[]{:S(2)}, u32[]{:S(2)}) collective-permute-start(bf16[4,288,128]{2,1,0:T(8,128)(2,1)S(1)} %collective-permute-done.16.rest_1_), channel_id=1, source_target_pairs={{0,2},{2,4},{4,6},{6,8},{8,10},{10,12},{12,14},{14,0},{1,3},{3,5},... | collective-permute-start | bytes 884744 | tf_op jit(solution)/shard_map/ppermute | solution.py:450
  69.2 12.5 %collective-permute-start.20 = (bf16[4,288,128]{2,1,0:T(8,128)(2,1)S(1)}, bf16[4,288,128]{2,1,0:T(8,128)(2,1)S(1)}, u32[]{:S(2)}, u32[]{:S(2)}) collective-permute-start(bf16[4,288,128]{2,1,0:T(8,128)(2,1)S(1)} %collective-permute-done.19.rest_6_.rest_7_), channel_id=1, source_target_pairs={{0,14},{2,0},{4,2},{6,4},{8,6},{10,8},{12,10},{14,12},{1,15},{3,1}... | collective-permute-start | bytes 884744 | tf_op jit(solution)/shard_map/ppermute | solution.py:454
  78.1 20.7 %collective-permute-start.26 = (bf16[2,128,128]{2,1,0:T(8,128)(2,1)S(1)}, bf16[2,128,128]{2,1,0:T(8,128)(2,1)S(1)}, u32[]{:S(2)}, u32[]{:S(2)}) collective-permute-start(bf16[2,128,128]{2,1,0:T(8,128)(2,1)S(1)} %get-tuple-element.60), channel_id=1, source_target_pairs={{0,1},{1,0},{2,3},{3,2},{4,5},{5,4},{6,7},{7,6},{8,9},{9,8},{10,11... | collective-permute-start | bytes 196616 | tf_op jit(solution)/shard_map/ppermute | solution.py:446
  80.0 18.9 %collective-permute-start.27 = (bf16[2,128,128]{2,1,0:T(8,128)(2,1)S(1)}, bf16[2,128,128]{2,1,0:T(8,128)(2,1)S(1)}, u32[]{:S(2)}, u32[]{:S(2)}) collective-permute-start(bf16[2,128,128]{2,1,0:T(8,128)(2,1)S(1)} %get-tuple-element.61), channel_id=1, source_target_pairs={{0,16},{16,0},{1,17},{17,1},{2,18},{18,2},{3,19},{19,3},{4,20},{20... | collective-permute-start | bytes 196616 | tf_op jit(solution)/shard_map/ppermute | solution.py:446
  80.0 18.9 %collective-permute-start.28 = (bf16[2,128,128]{2,1,0:T(8,128)(2,1)S(1)}, bf16[2,128,128]{2,1,0:T(8,128)(2,1)S(1)}, u32[]{:S(2)}, u32[]{:S(2)}) collective-permute-start(bf16[2,128,128]{2,1,0:T(8,128)(2,1)S(1)} %get-tuple-element.62), channel_id=1, source_target_pairs={{0,17},{1,16},{16,1},{17,0},{2,19},{3,18},{18,3},{19,2},{4,21},{5,... | collective-permute-start | bytes 196616 | tf_op jit(solution)/shard_map/ppermute | solution.py:480
  81.8 9.7 %collective-permute-start.18 = (bf16[4,288,128]{2,1,0:T(8,128)(2,1)S(1)}, bf16[4,288,128]{2,1,0:T(8,128)(2,1)S(1)}, u32[]{:S(2)}, u32[]{:S(2)}) collective-permute-start(bf16[4,288,128]{2,1,0:T(8,128)(2,1)S(1)} %collective-permute-done.17.rest_2_), channel_id=1, source_target_pairs={{0,2},{2,4},{4,6},{6,8},{8,10},{10,12},{12,14},{14,0},{1,3},{3,5},... | collective-permute-start | bytes 884744 | tf_op jit(solution)/shard_map/ppermute | solution.py:450
  81.9 10.4 %collective-permute-start.21 = (bf16[4,288,128]{2,1,0:T(8,128)(2,1)S(1)}, bf16[4,288,128]{2,1,0:T(8,128)(2,1)S(1)}, u32[]{:S(2)}, u32[]{:S(2)}) collective-permute-start(bf16[4,288,128]{2,1,0:T(8,128)(2,1)S(1)} %collective-permute-done.20.rest_5_.rest_6_), channel_id=1, source_target_pairs={{0,14},{2,0},{4,2},{6,4},{8,6},{10,8},{12,10},{14,12},{1,15},{3,1}... | collective-permute-start | bytes 884744 | tf_op jit(solution)/shard_map/ppermute | solution.py:454
  85.3 15.8 %all-to-all-start.1 = ((bf16[8,128,128]{2,1,0:T(8,128)(2,1)}), bf16[8,128,128]{2,1,0:T(8,128)(2,1)S(1)}, u32[]{:S(2)}, u32[]{:S(2)}) async-start(bf16[8,128,128]{2,1,0:T(8,128)(2,1)} %shard_map.167), calls=%async_computation.1 | async-start | bytes 524288 | tf_op jit(solution)/shard_map/all_to_all | solution.py:554
  91.5 16.9 %collective-permute-start.22 = (bf16[4,288,128]{2,1,0:T(8,128)(2,1)S(1)}, bf16[4,288,128]{2,1,0:T(8,128)(2,1)S(1)}, u32[]{:S(2)}, u32[]{:S(2)}) collective-permute-start(bf16[4,288,128]{2,1,0:T(8,128)(2,1)S(1)} %collective-permute-done.18.rest_3_), channel_id=1, source_target_pairs={{0,2},{2,4},{4,6},{6,8},{8,10},{10,12},{12,14},{14,0},{1,3},{3,5},... | collective-permute-start | bytes 884744 | tf_op jit(solution)/shard_map/ppermute | solution.py:450
  101.9 23.8 %all-to-all-start.2 = ((bf16[16,128,128]{2,1,0:T(8,128)(2,1)}), bf16[16,128,128]{2,1,0:T(8,128)(2,1)S(1)}, u32[]{:S(2)}, u32[]{:S(2)}) async-start(bf16[16,128,128]{2,1,0:T(8,128)(2,1)} %shard_map.168), calls=%async_computation.2 | async-start | bytes 1048576 | tf_op jit(solution)/shard_map/all_to_all | solution.py:571
  (31 other events, 250.0 us)

commit v4 on v3

--- a/solution.py
+++ b/solution.py
@@ -152,7 +152,7 @@
         own = logical - first
         query = q_ref[slot, :128]
 
-        def step(j, acc):
+        def group(j, acc):
             spots, reach = [], []
             for i in range(4):
                 entry = 4 * j + i
@@ -162,7 +162,10 @@
                 reach.append(jnp.where(late, 1, jnp.where(entry == own, 0, -1)))
             return masked_step(query, kv, spots, reach, acc)
 
-        att_ref[slot] = lax.fori_loop(0, own // 4 + 1, step, jnp.zeros((128, 128), F32))
+        def step(j, acc):
+            return group(2 * j + 1, group(2 * j, acc))
+
+        att_ref[slot] = lax.fori_loop(0, own // 8 + 1, step, jnp.zeros((128, 128), F32))
         return carry
 
     lax.fori_loop(0, 4, one, 0)
@@ -173,7 +176,7 @@
 ):
     lane = iota((128, 128), 1)
 
-    def one(slot, carry):
+    for slot in range(4):
         logical = pk[0, slot_of(slot)]
         user, first, blocks, tail = user_of(ub, tl, logical)
         own = logical - first
@@ -196,9 +199,6 @@
             lane == 0, mean, jnp.where(lane == 1, spread, jnp.where(lane == 2, total, cross))
         )
         stat_ref[slot] = stats.T[:8]
-        return carry
-
-    lax.fori_loop(0, 4, one, 0)
 
 
 def norm_kernel(
@@ -288,7 +288,7 @@
         query = all_ref[slot, :128]
         grad = all_ref[slot, 160:]
 
-        def step(j, acc):
+        def group(j, acc):
             places = [inv[first + jnp.minimum(4 * j + i, own)] for i in range(4)]
             keys = jnp.concatenate([kv[p, 0] for p in places], axis=0)
             values = jnp.concatenate([kv[p, 1] for p in places], axis=0)
@@ -299,7 +299,10 @@
             ds = jnp.where(col + (4 * j - own) * 128 <= row, slopes * slope, 0.0).astype(BF16)
             return acc + dot(ds, keys, 1, 0)
 
-        acc = lax.fori_loop(0, own // 4 + 1, step, jnp.zeros((128, 128), F32))
+        def step(j, acc):
+            return group(2 * j + 1, group(2 * j, acc))
+
+        acc = lax.fori_loop(0, own // 8 + 1, step, jnp.zeros((128, 128), F32))
         gq[slot] = (acc * SCALE).astype(BF16)
         return carry
 
@@ -328,12 +331,13 @@
     return gk, gv
 
 
-def key_near_kernel(ub, tl, pk, kv_ref, *rest):
-    chunks, (sum_ref,), (buf, inv, sems) = rest[:7], rest[7:8], rest[8:]
+def key_near_kernel(ub, tl, pk, kv_hbm, *rest):
+    chunks, (sum_ref,), (kv_ref, buf, inv, sems) = rest[:7], rest[7:8], rest[8:]
     copies = [
         pltpu.make_async_copy(ref, buf.at[pl.ds(4 * c, 4)], sems.at[c])
         for c, ref in zip((0, 1, 2, 3, 5, 6, 7), chunks)
     ]
+    copies.append(pltpu.make_async_copy(kv_hbm, kv_ref, sems.at[4]))
     for copy in copies:
         copy.start()
     fill_places(pk, inv)
@@ -345,7 +349,7 @@
         user, first, blocks, tail = user_of(ub, tl, logical)
         count = first + blocks - logical
 
-        def step(j, carry):
+        def group(j, carry):
             spots, reach = [], []
             for i in range(4):
                 entry = 4 * j + i
@@ -358,7 +362,10 @@
             return key_step(kv_ref[slot, 0], kv_ref[slot, 1], queries, grads, reach, carry)
 
         zero = jnp.zeros((128, 128), F32)
-        gk, gv = lax.fori_loop(0, (count + 3) // 4, step, (zero, zero))
+        def step(j, carry):
+            return group(2 * j + 1, group(2 * j, carry))
+
+        gk, gv = lax.fori_loop(0, (count + 7) // 8, step, (zero, zero))
         sum_ref[slot, 0] = gk
         sum_ref[slot, 1] = gv
         return carry
@@ -367,13 +374,18 @@
 
 
 def key_far_kernel(
-    ub, tl, pk, kv_ref, near_ref, sc_ref, all_ref, o0, o1, o2, o3, both, buf, sem
+    ub, tl, pk, kv_hbm, near_ref, sc_ref, all_ref, o0, o1, o2, o3, kv_ref, buf, sems
 ):
-    copy = pltpu.make_async_copy(all_ref, buf, sem)
-    copy.start()
-    copy.wait()
-
-    def one(slot, carry):
+    copies = [
+        pltpu.make_async_copy(all_ref, buf, sems.at[0]),
+        pltpu.make_async_copy(kv_hbm, kv_ref, sems.at[1]),
+    ]
+    for copy in copies:
+        copy.start()
+    for copy in copies:
+        copy.wait()
+
+    for slot, out in enumerate((o0, o1, o2, o3)):
         logical = pk[0, slot_of(slot)]
         user, first, blocks, tail = user_of(ub, tl, logical)
         reach = []
@@ -386,13 +398,8 @@
             kv_ref[slot, 0], kv_ref[slot, 1], queries, grads, reach,
             (near_ref[slot, 0], near_ref[slot, 1]),
         )
-        both[slot, 0] = (gk * SCALE).astype(BF16)
-        both[slot, 1] = gv.astype(BF16)
-        return carry
-
-    lax.fori_loop(0, 4, one, 0)
-    for slot, out in enumerate((o0, o1, o2, o3)):
-        out[:2] = both[slot]
+        out[0] = (gk * SCALE).astype(BF16)
+        out[1] = gv.astype(BF16)
         out[2] = sc_ref[slot]
 
 
@@ -562,36 +569,36 @@
         [(block, BF16)],
         [pltpu.VMEM((32, 32, 128), BF16), sems],
     )
-    early = swap(early)
+    early = swap([after(rows, piece) for rows in early])
+    rows = (128, 512)
+    gq, gg = call(unpack_early_kernel, vm(*early), [(rows, BF16)] * 2)
     (lines,) = call(
         functools.partial(sum_kernel, 16),
-        vm(after(line, ups[3], downs[3], *early[1:])),
+        vm(after(line, ups[3], downs[3], gq)),
         [((16, 128, 128), BF16)],
     )
     near = lax.all_to_all(lines, ("xh", "y", "xl"), split_axis=0, concat_axis=0, tiled=True)
     (key_sums,) = call(
         key_near_kernel,
-        facts + vm(kv) + raw(pairs[:4] + pairs[5:]),
+        facts + raw([kv] + pairs[:4] + pairs[5:]),
         [((4, 2, 128, 128), F32)],
-        [pltpu.VMEM((32, 288, 128), BF16), places, sems],
+        [pltpu.VMEM((4, 2, 128, 128), BF16), pltpu.VMEM((32, 288, 128), BF16), places, sems],
         us=8,
     )
     late = call(
         key_far_kernel,
-        facts + vm(kv, key_sums, sc) + raw([pairs[4]]),
+        facts + raw([kv]) + vm(key_sums, sc) + raw([pairs[4]]),
         [((3, 128, 128), BF16)] * 4,
         [
             pltpu.VMEM((4, 2, 128, 128), BF16),
             pltpu.VMEM((4, 288, 128), BF16),
-            pltpu.SemaphoreType.DMA,
+            pltpu.SemaphoreType.DMA((2,)),
         ],
         us=3,
     )
     late = swap(late)
     far = flip(after(near, *late[1:]), "core")
     (gow,) = call(assemble_kernel, vm(near, far), [((512, 1024), F32)])
-    rows = (128, 512)
-    gq, gg = call(unpack_early_kernel, vm(*early), [(rows, BF16)] * 2)
     gk, gv, scores = call(
         unpack_late_kernel, vm(*late), [(rows, BF16), (rows, BF16), ((128, 128), F32)]
     )

time: 130 us -> 130 us (level)
    ppermute x8, starting transfers between devices: 1.5 us -> 2.96 us  [up(): return lax.ppermute(array, 'z', [(i, (i + 1) % 8) for i in range(8)])]
where the time goes in v4:
time: 130 us; the launch traced here: 129 us
  starting transfers between devices  59.6 us (46%)
  Pallas kernels  35.7 us (27%)
  waiting for transfers between devices  30.1 us (23%)
  local copies, waits for them, and re-layouts  2.29 us (2%)
    pallas_call x16, Pallas kernels, call(): pl.pallas_call(kernel, in_specs=[spec for spec, _ in ins], out_specs=[VM]...  35.7 us
    ppermute x6, starting transfers between devices, down(): return lax.ppermute(array, 'z', [(i, (i + 7) % 8) for i in range(8)])  16.6 us
    ppermute x11, starting transfers between devices, flip(): return lax.ppermute(array, axis, [(0, 1), (1, 0)])  15.2 us
    ppermute x5, waiting for transfers between devices, swap(): lax.ppermute(pieces[3], ('xl', 'core'), [(i, 3 - i) for i in range(4)])  13.7 us
    ppermute x8, waiting for transfers between devices, up(): return lax.ppermute(array, 'z', [(i, (i + 1) % 8) for i in range(8)])  9.71 us
    all_to_all x1, starting transfers between devices, body(): lax.all_to_all(lines, ('xh', 'y', 'xl'), split_axis=0, concat_axis=0, til...  7.46 us
    all_to_all x1, starting transfers between devices, body(): lax.all_to_all(gw, ('xh', 'y'), split_axis=0, concat_axis=0, tiled=True)  6.36 us
    ppermute x5, starting transfers between devices, swap(): lax.ppermute(pieces[3], ('xl', 'core'), [(i, 3 - i) for i in range(4)])  5.61 us
  transfers between devices with their start and end apart: 33, of which 12 were waited for; matrix products, arithmetic and copies ran while one was open for 0% of the time, Pallas kernels for 23%

profile of v4, /device:TPU:1, one launch (start us, length us, event | category | flops | bytes accessed | tf_op | source)
XLA Modules:
  0.0 128.7 jit_solution(1845444401397341669)
XLA Ops:
  2.6 2.1 %collective-permute-start.1 = (bf16[544,128]{1,0:T(8,128)(2,1)S(1)}, bf16[544,128]{1,0:T(8,128)(2,1)S(1)}, u32[]{:S(2)}, u32[]{:S(2)}) collective-permute-start(bf16[544,128]{1,0:T(8,128)(2,1)S(1)} %get-tuple-element.44), channel_id=1, source_target_pairs={{0,16},{16,0},{1,17},{17,1},{2,18},{18,2},{3,19},{19,3},{4,20},{20... | collective-permute-start | bytes 417800 | tf_op jit(solution)/shard_map/ppermute | solution.py:453
  7.6 5.5 %collective-permute-done.2.p3 = bf16[544,128]{1,0:T(8,128)(2,1)S(1)} collective-permute-done((bf16[544,128]{1,0:T(8,128)(2,1)S(1)}, bf16[544,128]{1,0:T(8,128)(2,1)S(1)}, u32[]{:S(2)}, u32[]{:S(2)}) %collective-permute-start.2) | collective-permute-done | bytes 139296 | tf_op jit(solution)/shard_map/ppermute | solution.py:487
  13.7 4.0 %collective-permute-start.9 = (bf16[4,2,128,128]{3,2,1,0:T(8,128)(2,1)S(1)}, bf16[4,2,128,128]{3,2,1,0:T(8,128)(2,1)S(1)}, u32[]{:S(2)}, u32[]{:S(2)}) collective-permute-start(bf16[4,2,128,128]{3,2,1,0:T(8,128)(2,1)S(1)} %get-tuple-element.46.rest_0_.kv_hbm), channel_id=1, source_target_pairs={{0,14},{2,0},{4,2},{6,4},{8,6},{10,8},{12,10},{14,12},{1,15},{3,1}... | collective-permute-start | bytes 786440 | tf_op jit(solution)/shard_map/ppermute | solution.py:461
  19.9 4.5 %collective-permute-done.6.rest_1_ = bf16[4,2,128,128]{3,2,1,0:T(8,128)(2,1)S(1)} collective-permute-done((bf16[4,2,128,128]{3,2,1,0:T(8,128)(2,1)S(1)}, bf16[4,2,128,128]{3,2,1,0:T(8,128)(2,1)S(1)}, u32[]{:S(2)}, u32[]{:S(2)}) %collective-permute-start.6) | collective-permute-done | bytes 262176 | tf_op jit(solution)/shard_map/ppermute | solution.py:457
  24.4 2.7 %collective-permute-start.10 = (bf16[4,2,128,128]{3,2,1,0:T(8,128)(2,1)S(1)}, bf16[4,2,128,128]{3,2,1,0:T(8,128)(2,1)S(1)}, u32[]{:S(2)}, u32[]{:S(2)}) collective-permute-start(bf16[4,2,128,128]{3,2,1,0:T(8,128)(2,1)S(1)} %collective-permute-done.9.rest_6_.rest_7_), channel_id=1, source_target_pairs={{0,14},{2,0},{4,2},{6,4},{8,6},{10,8},{12,10},{14,12},{1,15},{3,1}... | collective-permute-start | bytes 786440 | tf_op jit(solution)/shard_map/ppermute | solution.py:461
  27.1 4.6 %collective-permute-done.5.c3 = bf16[128,1024]{1,0:T(8,128)(2,1)S(1)} collective-permute-done((bf16[128,1024]{1,0:T(8,128)(2,1)S(1)}, bf16[128,1024]{1,0:T(8,128)(2,1)S(1)}, u32[]{:S(2)}, u32[]{:S(2)}) %collective-permute-start.5) | collective-permute-done | bytes 262176 | tf_op jit(solution)/shard_map/ppermute | solution.py:487
  33.1 2.7 %collective-permute-start.11 = (bf16[4,2,128,128]{3,2,1,0:T(8,128)(2,1)S(1)}, bf16[4,2,128,128]{3,2,1,0:T(8,128)(2,1)S(1)}, u32[]{:S(2)}, u32[]{:S(2)}) collective-permute-start(bf16[4,2,128,128]{3,2,1,0:T(8,128)(2,1)S(1)} %collective-permute-done.10.rest_5_.rest_6_), channel_id=1, source_target_pairs={{0,14},{2,0},{4,2},{6,4},{8,6},{10,8},{12,10},{14,12},{1,15},{3,1}... | collective-permute-start | bytes 786440 | tf_op jit(solution)/shard_map/ppermute | solution.py:461
  37.3 3.6 %collective-permute-done.8.rest_3_ = bf16[4,2,128,128]{3,2,1,0:T(8,128)(2,1)S(1)} collective-permute-done((bf16[4,2,128,128]{3,2,1,0:T(8,128)(2,1)S(1)}, bf16[4,2,128,128]{3,2,1,0:T(8,128)(2,1)S(1)}, u32[]{:S(2)}, u32[]{:S(2)}) %collective-permute-start.8) | collective-permute-done | bytes 262176 | tf_op jit(solution)/shard_map/ppermute | solution.py:457
  41.7 5.9 %shard_map.157.near_ref = f32[4,128,128]{2,1,0:T(8,128)S(1)} custom-call(s32[1,4]{1,0:T(1,128)S(1)} %copy-done.5, s32[1,4]{1,0:T(1,128)S(1)} %copy-done.6, s32[1,32]{1,0:T(1,128)S(1)} %copy-done.7, bf16[4,160,128]{2,1,0:T(8,128)(2,1)S(1)} %get-tuple-element.47.q_ref.qp_ref, bf16[4,2,128,128]{3,2,1,0:T(8,128)(2,1)} %copy-done.2, ...), custom_call_target="tpu_custom_call" | custom-call | flops 6000000000 | bytes 6000000 | tf_op jit(solution)/shard_map/pallas_call | solution.py:439
  49.5 3.1 %collective-permute-start.13 = (f32[4,8,128]{2,1,0:T(8,128)S(1)}, f32[4,8,128]{2,1,0:T(8,128)S(1)}, u32[]{:S(2)}, u32[]{:S(2)}) collective-permute-start(f32[4,8,128]{2,1,0:T(8,128)S(1)} %get-tuple-element.53.s0), channel_id=1, source_target_pairs={{0,1},{1,0},{2,3},{3,2},{4,5},{5,4},{6,7},{7,6},{8,9},{9,8},{10,11... | collective-permute-start | bytes 49160 | tf_op jit(solution)/shard_map/ppermute | solution.py:453
  57.8 2.7 %collective-permute-start.19 = (bf16[4,288,128]{2,1,0:T(8,128)(2,1)S(1)}, bf16[4,288,128]{2,1,0:T(8,128)(2,1)S(1)}, u32[]{:S(2)}, u32[]{:S(2)}) collective-permute-start(bf16[4,288,128]{2,1,0:T(8,128)(2,1)S(1)} %get-tuple-element.61.rest_0_.all_ref), channel_id=1, source_target_pairs={{0,14},{2,0},{4,2},{6,4},{8,6},{10,8},{12,10},{14,12},{1,15},{3,1}... | collective-permute-start | bytes 884744 | tf_op jit(solution)/shard_map/ppermute | solution.py:461
  61.7 6.4 %all-to-all-start = ((bf16[8,128,128]{2,1,0:T(8,128)(2,1)}), bf16[8,128,128]{2,1,0:T(8,128)(2,1)S(1)}, u32[]{:S(2)}, u32[]{:S(2)}) async-start(bf16[8,128,128]{2,1,0:T(8,128)(2,1)} %shard_map.165), calls=%async_computation | async-start | bytes 524288 | tf_op jit(solution)/shard_map/all_to_all | solution.py:544
  68.5 2.3 %collective-permute-start.20 = (bf16[4,288,128]{2,1,0:T(8,128)(2,1)S(1)}, bf16[4,288,128]{2,1,0:T(8,128)(2,1)S(1)}, u32[]{:S(2)}, u32[]{:S(2)}) collective-permute-start(bf16[4,288,128]{2,1,0:T(8,128)(2,1)S(1)} %collective-permute-done.19.rest_6_.rest_7_), channel_id=1, source_target_pairs={{0,14},{2,0},{4,2},{6,4},{8,6},{10,8},{12,10},{14,12},{1,15},{3,1}... | collective-permute-start | bytes 884744 | tf_op jit(solution)/shard_map/ppermute | solution.py:461
  70.8 6.6 %shard_map.164 = (bf16[2,128,128]{2,1,0:T(8,128)(2,1)S(1)}, bf16[2,128,128]{2,1,0:T(8,128)(2,1)S(1)}, bf16[2,128,128]{2,1,0:T(8,128)(2,1)S(1)}, bf16[2,128,128]{2,1,0:T(8,128)(2,1)S(1)}) custom-call(s32[1,4]{1,0:T(1,128)S(1)} %copy-done.5, s32[1,4]{1,0:T(1,128)S(1)} %copy-done.6, s32[1,32]{1,0:T(1,128)S(1)} %copy-done.7, ...), custom_call_target="tpu_custom_call" | custom-call | flops 8000000000 | bytes 8000000 | tf_op jit(solution)/shard_map/pallas_call | solution.py:439
  77.9 2.3 %collective-permute-start.21 = (bf16[4,288,128]{2,1,0:T(8,128)(2,1)S(1)}, bf16[4,288,128]{2,1,0:T(8,128)(2,1)S(1)}, u32[]{:S(2)}, u32[]{:S(2)}) collective-permute-start(bf16[4,288,128]{2,1,0:T(8,128)(2,1)S(1)} %collective-permute-done.20.rest_5_.rest_6_), channel_id=1, source_target_pairs={{0,14},{2,0},{4,2},{6,4},{8,6},{10,8},{12,10},{14,12},{1,15},{3,1}... | collective-permute-start | bytes 884744 | tf_op jit(solution)/shard_map/ppermute | solution.py:461
  80.9 2.1 %collective-permute-start.28 = (bf16[2,128,128]{2,1,0:T(8,128)(2,1)S(1)}, bf16[2,128,128]{2,1,0:T(8,128)(2,1)S(1)}, u32[]{:S(2)}, u32[]{:S(2)}) collective-permute-start(bf16[2,128,128]{2,1,0:T(8,128)(2,1)S(1)} %get-tuple-element.71), channel_id=1, source_target_pairs={{0,17},{1,16},{16,1},{17,0},{2,19},{3,18},{18,3},{19,2},{4,21},{5,... | collective-permute-start | bytes 196616 | tf_op jit(solution)/shard_map/ppermute | solution.py:487
  84.6 5.4 %all-to-all-start.1 = ((bf16[8,128,128]{2,1,0:T(8,128)(2,1)}), bf16[8,128,128]{2,1,0:T(8,128)(2,1)S(1)}, u32[]{:S(2)}, u32[]{:S(2)}) async-start(bf16[8,128,128]{2,1,0:T(8,128)(2,1)} %shard_map.166), calls=%async_computation.1 | async-start | bytes 524288 | tf_op jit(solution)/shard_map/all_to_all | solution.py:561
  93.0 5.6 %shard_map.160.near_ref = f32[4,2,128,128]{3,2,1,0:T(8,128)S(1)} custom-call(s32[1,4]{1,0:T(1,128)S(1)} %copy-done.5, s32[1,4]{1,0:T(1,128)S(1)} %copy-done.6, s32[1,32]{1,0:T(1,128)S(1)} %copy-done.7, bf16[4,2,128,128]{3,2,1,0:T(8,128)(2,1)} %copy-done.2, bf16[4,288,128]{2,1,0:T(8,128)(2,1)} %copy-done, bf16[4,288,128]{2,1,0:T(8,128)(2,1)} %copy-done.8, ...), custom_call_target="tpu_custom_call" | custom-call | flops 8000000000 | bytes 8000000 | tf_op jit(solution)/shard_map/pallas_call | solution.py:439
  101.6 7.5 %all-to-all-start.2 = ((bf16[16,128,128]{2,1,0:T(8,128)(2,1)}), bf16[16,128,128]{2,1,0:T(8,128)(2,1)S(1)}, u32[]{:S(2)}, u32[]{:S(2)}) async-start(bf16[16,128,128]{2,1,0:T(8,128)(2,1)} %shard_map.168), calls=%async_computation.2 | async-start | bytes 1048576 | tf_op jit(solution)/shard_map/all_to_all | solution.py:580
  109.8 2.5 %shard_map.161.sc_ref = bf16[4,128,128]{2,1,0:T(8,128)(2,1)S(1)} custom-call(s32[1,4]{1,0:T(1,128)S(1)} %copy-done.5, s32[1,4]{1,0:T(1,128)S(1)} %copy-done.6, s32[1,32]{1,0:T(1,128)S(1)} %copy-done.7, bf16[512,128]{1,0:T(8,128)(2,1)S(1)} %get-tuple-element.55.mixed_ref, s32[4,128]{1,0:T(4,128)S(1)} %bitcast.1, bf16[4,288,128]{2,1,0:T(8,128)(2,1)} %copy-done, ...), custom_call_target="tpu_custom_call" | custom-call | flops 2000000000 | bytes 2000000 | tf_op jit(solution)/shard_map/pallas_call | solution.py:439
  112.4 3.0 %shard_map.162 = (bf16[3,128,128]{2,1,0:T(8,128)(2,1)S(1)}, bf16[3,128,128]{2,1,0:T(8,128)(2,1)S(1)}, bf16[3,128,128]{2,1,0:T(8,128)(2,1)S(1)}, bf16[3,128,128]{2,1,0:T(8,128)(2,1)S(1)}) custom-call(s32[1,4]{1,0:T(1,128)S(1)} %copy-done.5, s32[1,4]{1,0:T(1,128)S(1)} %copy-done.6, s32[1,32]{1,0:T(1,128)S(1)} %copy-done.7, bf16[4,2,128,128]{3,2,1,0:T(8,128)(2,1)} %copy-done.2, ...), custom_call_target="tpu_custom_call" | custom-call | flops 3000000000 | bytes 3000000 | tf_op jit(solution)/shard_map/pallas_call | solution.py:439
  115.4 3.0 %collective-permute-start.23 = (bf16[3,128,128]{2,1,0:T(8,128)(2,1)S(1)}, bf16[3,128,128]{2,1,0:T(8,128)(2,1)S(1)}, u32[]{:S(2)}, u32[]{:S(2)}) collective-permute-start(bf16[3,128,128]{2,1,0:T(8,128)(2,1)S(1)} %get-tuple-element.57), channel_id=1, source_target_pairs={{0,1},{1,0},{2,3},{3,2},{4,5},{5,4},{6,7},{7,6},{8,9},{9,8},{10,11... | collective-permute-start | bytes 294920 | tf_op jit(solution)/shard_map/ppermute | solution.py:453
  120.1 2.9 %collective-permute-done.24.p2 = bf16[3,128,128]{2,1,0:T(8,128)(2,1)S(1)} collective-permute-done((bf16[3,128,128]{2,1,0:T(8,128)(2,1)S(1)}, bf16[3,128,128]{2,1,0:T(8,128)(2,1)S(1)}, u32[]{:S(2)}, u32[]{:S(2)}) %collective-permute-start.24) | collective-permute-done | bytes 98336 | tf_op jit(solution)/shard_map/ppermute | solution.py:453
  123.1 2.1 %collective-permute-done.25.p3 = bf16[3,128,128]{2,1,0:T(8,128)(2,1)S(1)} collective-permute-done((bf16[3,128,128]{2,1,0:T(8,128)(2,1)S(1)}, bf16[3,128,128]{2,1,0:T(8,128)(2,1)S(1)}, u32[]{:S(2)}, u32[]{:S(2)}) %collective-permute-start.25) | collective-permute-done | bytes 98336 | tf_op jit(solution)/shard_map/ppermute | solution.py:487
  (100 shorter events, 34.5 us)
Async XLA Ops:
  6.1 7.1 %collective-permute-start.2 = (bf16[544,128]{1,0:T(8,128)(2,1)S(1)}, bf16[544,128]{1,0:T(8,128)(2,1)S(1)}, u32[]{:S(2)}, u32[]{:S(2)}) collective-permute-start(bf16[544,128]{1,0:T(8,128)(2,1)S(1)} %get-tuple-element.45), channel_id=1, source_target_pairs={{0,17},{1,16},{16,1},{17,0},{2,19},{3,18},{18,3},{19,2},{4,21},{5,... | collective-permute-start | bytes 417800 | tf_op jit(solution)/shard_map/ppermute | solution.py:487
  13.2 11.2 %collective-permute-start.6 = (bf16[4,2,128,128]{3,2,1,0:T(8,128)(2,1)S(1)}, bf16[4,2,128,128]{3,2,1,0:T(8,128)(2,1)S(1)}, u32[]{:S(2)}, u32[]{:S(2)}) collective-permute-start(bf16[4,2,128,128]{3,2,1,0:T(8,128)(2,1)S(1)} %get-tuple-element.46.rest_0_.kv_hbm), channel_id=1, source_target_pairs={{0,2},{2,4},{4,6},{6,8},{8,10},{10,12},{12,14},{14,0},{1,3},{3,5},... | collective-permute-start | bytes 786440 | tf_op jit(solution)/shard_map/ppermute | solution.py:457
  13.7 10.7 %collective-permute-start.9 = (bf16[4,2,128,128]{3,2,1,0:T(8,128)(2,1)S(1)}, bf16[4,2,128,128]{3,2,1,0:T(8,128)(2,1)S(1)}, u32[]{:S(2)}, u32[]{:S(2)}) collective-permute-start(bf16[4,2,128,128]{3,2,1,0:T(8,128)(2,1)S(1)} %get-tuple-element.46.rest_0_.kv_hbm), channel_id=1, source_target_pairs={{0,14},{2,0},{4,2},{6,4},{8,6},{10,8},{12,10},{14,12},{1,15},{3,1}... | collective-permute-start | bytes 786440 | tf_op jit(solution)/shard_map/ppermute | solution.py:461
  17.8 9.3 %collective-permute-start.3 = (bf16[128,1024]{1,0:T(8,128)(2,1)S(1)}, bf16[128,1024]{1,0:T(8,128)(2,1)S(1)}, u32[]{:S(2)}, u32[]{:S(2)}) collective-permute-start(bf16[128,1024]{1,0:T(8,128)(2,1)S(1)} %copy-done.1), channel_id=1, source_target_pairs={{0,1},{1,0},{2,3},{3,2},{4,5},{5,4},{6,7},{7,6},{8,9},{9,8},{10,11... | collective-permute-start | bytes 786440 | tf_op jit(solution)/shard_map/ppermute | solution.py:453
  17.8 9.3 %collective-permute-start.4 = (bf16[128,1024]{1,0:T(8,128)(2,1)S(1)}, bf16[128,1024]{1,0:T(8,128)(2,1)S(1)}, u32[]{:S(2)}, u32[]{:S(2)}) collective-permute-start(bf16[128,1024]{1,0:T(8,128)(2,1)S(1)} %copy-done.1), channel_id=1, source_target_pairs={{0,16},{16,0},{1,17},{17,1},{2,18},{18,2},{3,19},{19,3},{4,20},{20... | collective-permute-start | bytes 786440 | tf_op jit(solution)/shard_map/ppermute | solution.py:453
  19.0 12.8 %collective-permute-start.5 = (bf16[128,1024]{1,0:T(8,128)(2,1)S(1)}, bf16[128,1024]{1,0:T(8,128)(2,1)S(1)}, u32[]{:S(2)}, u32[]{:S(2)}) collective-permute-start(bf16[128,1024]{1,0:T(8,128)(2,1)S(1)} %copy-done.1), channel_id=1, source_target_pairs={{0,17},{1,16},{16,1},{17,0},{2,19},{3,18},{18,3},{19,2},{4,21},{5,... | collective-permute-start | bytes 786440 | tf_op jit(solution)/shard_map/ppermute | solution.py:487
  24.4 8.7 %collective-permute-start.7 = (bf16[4,2,128,128]{3,2,1,0:T(8,128)(2,1)S(1)}, bf16[4,2,128,128]{3,2,1,0:T(8,128)(2,1)S(1)}, u32[]{:S(2)}, u32[]{:S(2)}) collective-permute-start(bf16[4,2,128,128]{3,2,1,0:T(8,128)(2,1)S(1)} %collective-permute-done.6.rest_1_), channel_id=1, source_target_pairs={{0,2},{2,4},{4,6},{6,8},{8,10},{10,12},{12,14},{14,0},{1,3},{3,5},... | collective-permute-start | bytes 786440 | tf_op jit(solution)/shard_map/ppermute | solution.py:457
  24.4 8.7 %collective-permute-start.10 = (bf16[4,2,128,128]{3,2,1,0:T(8,128)(2,1)S(1)}, bf16[4,2,128,128]{3,2,1,0:T(8,128)(2,1)S(1)}, u32[]{:S(2)}, u32[]{:S(2)}) collective-permute-start(bf16[4,2,128,128]{3,2,1,0:T(8,128)(2,1)S(1)} %collective-permute-done.9.rest_6_.rest_7_), channel_id=1, source_target_pairs={{0,14},{2,0},{4,2},{6,4},{8,6},{10,8},{12,10},{14,12},{1,15},{3,1}... | collective-permute-start | bytes 786440 | tf_op jit(solution)/shard_map/ppermute | solution.py:461
  33.1 7.8 %collective-permute-start.8 = (bf16[4,2,128,128]{3,2,1,0:T(8,128)(2,1)S(1)}, bf16[4,2,128,128]{3,2,1,0:T(8,128)(2,1)S(1)}, u32[]{:S(2)}, u32[]{:S(2)}) collective-permute-start(bf16[4,2,128,128]{3,2,1,0:T(8,128)(2,1)S(1)} %collective-permute-done.7.rest_2_), channel_id=1, source_target_pairs={{0,2},{2,4},{4,6},{6,8},{8,10},{10,12},{12,14},{14,0},{1,3},{3,5},... | collective-permute-start | bytes 786440 | tf_op jit(solution)/shard_map/ppermute | solution.py:457
  33.1 7.8 %collective-permute-start.11 = (bf16[4,2,128,128]{3,2,1,0:T(8,128)(2,1)S(1)}, bf16[4,2,128,128]{3,2,1,0:T(8,128)(2,1)S(1)}, u32[]{:S(2)}, u32[]{:S(2)}) collective-permute-start(bf16[4,2,128,128]{3,2,1,0:T(8,128)(2,1)S(1)} %collective-permute-done.10.rest_5_.rest_6_), channel_id=1, source_target_pairs={{0,14},{2,0},{4,2},{6,4},{8,6},{10,8},{12,10},{14,12},{1,15},{3,1}... | collective-permute-start | bytes 786440 | tf_op jit(solution)/shard_map/ppermute | solution.py:461
  40.9 6.9 %collective-permute-start.12 = (bf16[4,2,128,128]{3,2,1,0:T(8,128)(2,1)S(1)}, bf16[4,2,128,128]{3,2,1,0:T(8,128)(2,1)S(1)}, u32[]{:S(2)}, u32[]{:S(2)}) collective-permute-start(bf16[4,2,128,128]{3,2,1,0:T(8,128)(2,1)S(1)} %collective-permute-done.8.rest_3_), channel_id=1, source_target_pairs={{0,2},{2,4},{4,6},{6,8},{8,10},{10,12},{12,14},{14,0},{1,3},{3,5},... | collective-permute-start | bytes 786440 | tf_op jit(solution)/shard_map/ppermute | solution.py:457
  57.7 10.3 %collective-permute-start.16 = (bf16[4,288,128]{2,1,0:T(8,128)(2,1)S(1)}, bf16[4,288,128]{2,1,0:T(8,128)(2,1)S(1)}, u32[]{:S(2)}, u32[]{:S(2)}) collective-permute-start(bf16[4,288,128]{2,1,0:T(8,128)(2,1)S(1)} %get-tuple-element.61.rest_0_.all_ref), channel_id=1, source_target_pairs={{0,2},{2,4},{4,6},{6,8},{8,10},{10,12},{12,14},{14,0},{1,3},{3,5},... | collective-permute-start | bytes 884744 | tf_op jit(solution)/shard_map/ppermute | solution.py:457
  57.8 10.2 %collective-permute-start.19 = (bf16[4,288,128]{2,1,0:T(8,128)(2,1)S(1)}, bf16[4,288,128]{2,1,0:T(8,128)(2,1)S(1)}, u32[]{:S(2)}, u32[]{:S(2)}) collective-permute-start(bf16[4,288,128]{2,1,0:T(8,128)(2,1)S(1)} %get-tuple-element.61.rest_0_.all_ref), channel_id=1, source_target_pairs={{0,14},{2,0},{4,2},{6,4},{8,6},{10,8},{12,10},{14,12},{1,15},{3,1}... | collective-permute-start | bytes 884744 | tf_op jit(solution)/shard_map/ppermute | solution.py:461
  61.7 15.7 %all-to-all-start = ((bf16[8,128,128]{2,1,0:T(8,128)(2,1)}), bf16[8,128,128]{2,1,0:T(8,128)(2,1)S(1)}, u32[]{:S(2)}, u32[]{:S(2)}) async-start(bf16[8,128,128]{2,1,0:T(8,128)(2,1)} %shard_map.165), calls=%async_computation | async-start | bytes 524288 | tf_op jit(solution)/shard_map/all_to_all | solution.py:544
  68.1 9.3 %collective-permute-start.17 = (bf16[4,288,128]{2,1,0:T(8,128)(2,1)S(1)}, bf16[4,288,128]{2,1,0:T(8,128)(2,1)S(1)}, u32[]{:S(2)}, u32[]{:S(2)}) collective-permute-start(bf16[4,288,128]{2,1,0:T(8,128)(2,1)S(1)} %collective-permute-done.16.rest_1_), channel_id=1, source_target_pairs={{0,2},{2,4},{4,6},{6,8},{8,10},{10,12},{12,14},{14,0},{1,3},{3,5},... | collective-permute-start | bytes 884744 | tf_op jit(solution)/shard_map/ppermute | solution.py:457
  68.5 8.9 %collective-permute-start.20 = (bf16[4,288,128]{2,1,0:T(8,128)(2,1)S(1)}, bf16[4,288,128]{2,1,0:T(8,128)(2,1)S(1)}, u32[]{:S(2)}, u32[]{:S(2)}) collective-permute-start(bf16[4,288,128]{2,1,0:T(8,128)(2,1)S(1)} %collective-permute-done.19.rest_6_.rest_7_), channel_id=1, source_target_pairs={{0,14},{2,0},{4,2},{6,4},{8,6},{10,8},{12,10},{14,12},{1,15},{3,1}... | collective-permute-start | bytes 884744 | tf_op jit(solution)/shard_map/ppermute | solution.py:461
  77.4 13.4 %collective-permute-start.18 = (bf16[4,288,128]{2,1,0:T(8,128)(2,1)S(1)}, bf16[4,288,128]{2,1,0:T(8,128)(2,1)S(1)}, u32[]{:S(2)}, u32[]{:S(2)}) collective-permute-start(bf16[4,288,128]{2,1,0:T(8,128)(2,1)S(1)} %collective-permute-done.17.rest_2_), channel_id=1, source_target_pairs={{0,2},{2,4},{4,6},{6,8},{8,10},{10,12},{12,14},{14,0},{1,3},{3,5},... | collective-permute-start | bytes 884744 | tf_op jit(solution)/shard_map/ppermute | solution.py:457
  77.9 14.4 %collective-permute-start.21 = (bf16[4,288,128]{2,1,0:T(8,128)(2,1)S(1)}, bf16[4,288,128]{2,1,0:T(8,128)(2,1)S(1)}, u32[]{:S(2)}, u32[]{:S(2)}) collective-permute-start(bf16[4,288,128]{2,1,0:T(8,128)(2,1)S(1)} %collective-permute-done.20.rest_5_.rest_6_), channel_id=1, source_target_pairs={{0,14},{2,0},{4,2},{6,4},{8,6},{10,8},{12,10},{14,12},{1,15},{3,1}... | collective-permute-start | bytes 884744 | tf_op jit(solution)/shard_map/ppermute | solution.py:461
  80.9 9.1 %collective-permute-start.28 = (bf16[2,128,128]{2,1,0:T(8,128)(2,1)S(1)}, bf16[2,128,128]{2,1,0:T(8,128)(2,1)S(1)}, u32[]{:S(2)}, u32[]{:S(2)}) collective-permute-start(bf16[2,128,128]{2,1,0:T(8,128)(2,1)S(1)} %get-tuple-element.71), channel_id=1, source_target_pairs={{0,17},{1,16},{16,1},{17,0},{2,19},{3,18},{18,3},{19,2},{4,21},{5,... | collective-permute-start | bytes 196616 | tf_op jit(solution)/shard_map/ppermute | solution.py:487
  83.1 6.9 %collective-permute-start.27 = (bf16[2,128,128]{2,1,0:T(8,128)(2,1)S(1)}, bf16[2,128,128]{2,1,0:T(8,128)(2,1)S(1)}, u32[]{:S(2)}, u32[]{:S(2)}) collective-permute-start(bf16[2,128,128]{2,1,0:T(8,128)(2,1)S(1)} %get-tuple-element.69), channel_id=1, source_target_pairs={{0,16},{16,0},{1,17},{17,1},{2,18},{18,2},{3,19},{19,3},{4,20},{20... | collective-permute-start | bytes 196616 | tf_op jit(solution)/shard_map/ppermute | solution.py:453
  84.6 5.4 %collective-permute-start.26 = (bf16[2,128,128]{2,1,0:T(8,128)(2,1)S(1)}, bf16[2,128,128]{2,1,0:T(8,128)(2,1)S(1)}, u32[]{:S(2)}, u32[]{:S(2)}) collective-permute-start(bf16[2,128,128]{2,1,0:T(8,128)(2,1)S(1)} %get-tuple-element.67), channel_id=1, source_target_pairs={{0,1},{1,0},{2,3},{3,2},{4,5},{5,4},{6,7},{7,6},{8,9},{9,8},{10,11... | collective-permute-start | bytes 196616 | tf_op jit(solution)/shard_map/ppermute | solution.py:453
  84.6 16.2 %all-to-all-start.1 = ((bf16[8,128,128]{2,1,0:T(8,128)(2,1)}), bf16[8,128,128]{2,1,0:T(8,128)(2,1)S(1)}, u32[]{:S(2)}, u32[]{:S(2)}) async-start(bf16[8,128,128]{2,1,0:T(8,128)(2,1)} %shard_map.166), calls=%async_computation.1 | async-start | bytes 524288 | tf_op jit(solution)/shard_map/all_to_all | solution.py:561
  90.8 18.3 %collective-permute-start.22 = (bf16[4,288,128]{2,1,0:T(8,128)(2,1)S(1)}, bf16[4,288,128]{2,1,0:T(8,128)(2,1)S(1)}, u32[]{:S(2)}, u32[]{:S(2)}) collective-permute-start(bf16[4,288,128]{2,1,0:T(8,128)(2,1)S(1)} %collective-permute-done.18.rest_3_), channel_id=1, source_target_pairs={{0,2},{2,4},{4,6},{6,8},{8,10},{10,12},{12,14},{14,0},{1,3},{3,5},... | collective-permute-start | bytes 884744 | tf_op jit(solution)/shard_map/ppermute | solution.py:457
  101.6 23.5 %all-to-all-start.2 = ((bf16[16,128,128]{2,1,0:T(8,128)(2,1)}), bf16[16,128,128]{2,1,0:T(8,128)(2,1)S(1)}, u32[]{:S(2)}, u32[]{:S(2)}) async-start(bf16[16,128,128]{2,1,0:T(8,128)(2,1)} %shard_map.168), calls=%async_computation.2 | async-start | bytes 1048576 | tf_op jit(solution)/shard_map/all_to_all | solution.py:580
  (30 other events, 237.0 us)

commit v5 on v4

--- a/solution.py
+++ b/solution.py
@@ -12,6 +12,7 @@
 DP = ("xh", "y")
 CTX = ("xl", "z", "core")
 SCALE = 128 ** (-0.5)
+TO_EXP2 = -SCALE * 1.4426950408889634
 EPS = 1e-05
 F32 = jnp.float32
 BF16 = jnp.bfloat16
@@ -121,12 +122,16 @@
         gate_ref[d] = piece[384:512]
 
 
+def sigmoid(raw):
+    return 1.0 / (1.0 + jnp.exp2(raw * TO_EXP2))
+
+
 def masked_step(query, kv, spots, reach, acc):
     keys = jnp.concatenate([kv[p, 0] for p in spots], axis=0)
     values = jnp.concatenate([kv[p, 1] for p in spots], axis=0)
     row = iota((128, 128), 0) - iota((128, 128), 1)
-    logits = dot(query, keys, 1, 1) * SCALE
-    silu = logits / (1.0 + jnp.exp(-logits))
+    raw = dot(query, keys, 1, 1)
+    silu = raw * SCALE * sigmoid(raw)
     weights = [
         jnp.where(row >= reach[i] * 128, silu[:, i * 128 : i * 128 + 128], 0.0).astype(BF16)
         for i in range(4)
@@ -292,10 +297,10 @@
             places = [inv[first + jnp.minimum(4 * j + i, own)] for i in range(4)]
             keys = jnp.concatenate([kv[p, 0] for p in places], axis=0)
             values = jnp.concatenate([kv[p, 1] for p in places], axis=0)
-            logits = dot(query, keys, 1, 1) * SCALE
+            raw = dot(query, keys, 1, 1)
             slopes = dot(grad, values, 1, 1)
-            sigma = 1.0 / (1.0 + jnp.exp(-logits))
-            slope = sigma * (1.0 + logits * (1.0 - sigma))
+            sigma = sigmoid(raw)
+            slope = sigma + raw * SCALE * sigma * (1.0 - sigma)
             ds = jnp.where(col + (4 * j - own) * 128 <= row, slopes * slope, 0.0).astype(BF16)
             return acc + dot(ds, keys, 1, 0)
 
@@ -315,11 +320,11 @@
 def key_step(key, value, queries, grads, reach, carry):
     gk, gv = carry
     col = iota((128, 128), 1) - iota((128, 128), 0)
-    logits = dot(key, queries, 1, 1) * SCALE
+    raw = dot(key, queries, 1, 1)
     slopes = dot(value, grads, 1, 1)
-    sigma = 1.0 / (1.0 + jnp.exp(-logits))
-    silu = logits * sigma
-    change = slopes * (sigma * (1.0 + logits * (1.0 - sigma)))
+    sigma = sigmoid(raw)
+    silu = raw * SCALE * sigma
+    change = slopes * (sigma + silu * (1.0 - sigma))
     weights, ds = [], []
     for i in range(4):
         cols = slice(i * 128, i * 128 + 128)
@@ -569,7 +574,7 @@
         [(block, BF16)],
         [pltpu.VMEM((32, 32, 128), BF16), sems],
     )
-    early = swap([after(rows, piece) for rows in early])
+    early = swap([after(rows, ups[3]) for rows in early])
     rows = (128, 512)
     gq, gg = call(unpack_early_kernel, vm(*early), [(rows, BF16)] * 2)
     (lines,) = call(

time: 130 us -> 127 us (0.977)
  waiting for transfers between devices: 30.1 us -> 28.8 us
    all_to_all x1, waiting for transfers between devices: 2.11 us -> 0.01 us  [body(): line = lax.all_to_all(piece, 'z', split_axis=0, concat_axis=0, tiled=True)]
    ppermute x11, starting transfers between devices: 15.2 us -> 13.3 us  [flip(): return lax.ppermute(array, axis, [(0, 1), (1, 0)])]
  transfers between devices with their start and end apart: 33 -> 33, of which waited for: 12 -> 12; matrix products, arithmetic and copies ran while one was open for 0% -> 0% of each run, Pallas kernels for 23% -> 22%
where the time goes in v5:
time: 127 us; the launch traced here: 126 us
  starting transfers between devices  59.7 us (47%)
  Pallas kernels  34.6 us (27%)
  waiting for transfers between devices  28.8 us (23%)
  local copies, waits for them, and re-layouts  2.28 us (2%)
    pallas_call x16, Pallas kernels, call(): pl.pallas_call(kernel, in_specs=[spec for spec, _ in ins], out_specs=[VM]...  34.6 us
    ppermute x6, starting transfers between devices, down(): return lax.ppermute(array, 'z', [(i, (i + 7) % 8) for i in range(8)])  15.9 us
    ppermute x5, waiting for transfers between devices, swap(): lax.ppermute(pieces[3], ('xl', 'core'), [(i, 3 - i) for i in range(4)])  13.7 us
    ppermute x11, starting transfers between devices, flip(): return lax.ppermute(array, axis, [(0, 1), (1, 0)])  13.3 us
    ppermute x8, waiting for transfers between devices, up(): return lax.ppermute(array, 'z', [(i, (i + 1) % 8) for i in range(8)])  10.5 us
    all_to_all x1, starting transfers between devices, body(): lax.all_to_all(lines, ('xh', 'y', 'xl'), split_axis=0, concat_axis=0, til...  7.8 us
    all_to_all x1, starting transfers between devices, body(): line = lax.all_to_all(piece, 'z', split_axis=0, concat_axis=0, tiled=True)  6.39 us
    all_to_all x1, starting transfers between devices, body(): lax.all_to_all(gw, ('xh', 'y'), split_axis=0, concat_axis=0, tiled=True)  6.35 us
  transfers between devices with their start and end apart: 33, of which 12 were waited for; matrix products, arithmetic and copies ran while one was open for 0% of the time, Pallas kernels for 22%

profile of v5, /device:TPU:1, one launch (start us, length us, event | category | flops | bytes accessed | tf_op | source)
XLA Modules:
  0.0 126.4 jit_solution(4695275584953477505)
XLA Ops:
  0.6 2.0 %shard_map.154 = (bf16[544,128]{1,0:T(8,128)(2,1)S(1)}, bf16[544,128]{1,0:T(8,128)(2,1)S(1)}, bf16[544,128]{1,0:T(8,128)(2,1)S(1)}, bf16[544,128]{1,0:T(8,128)(2,1)S(1)}) custom-call(bf16[128,512]{1,0:T(8,128)(2,1)} %k_ref.1, bf16[128,512]{1,0:T(8,128)(2,1)} %v_ref.1, bf16[128,512]{1,0:T(8,128)(2,1)} %q_ref.1, bf16[128,512]{1,0:T(8,128)(2,1)} %g_ref.1, ...), custom_call_target="tpu_custom_call" | custom-call | flops 2000000000 | bytes 2000000 | tf_op jit(solution)/shard_map/pallas_call | solution.py:444
  2.6 2.1 %collective-permute-start.1 = (bf16[544,128]{1,0:T(8,128)(2,1)S(1)}, bf16[544,128]{1,0:T(8,128)(2,1)S(1)}, u32[]{:S(2)}, u32[]{:S(2)}) collective-permute-start(bf16[544,128]{1,0:T(8,128)(2,1)S(1)} %get-tuple-element.44), channel_id=1, source_target_pairs={{0,16},{16,0},{1,17},{17,1},{2,18},{18,2},{3,19},{19,3},{4,20},{20... | collective-permute-start | bytes 417800 | tf_op jit(solution)/shard_map/ppermute | solution.py:458
  7.6 5.5 %collective-permute-done.2.p3 = bf16[544,128]{1,0:T(8,128)(2,1)S(1)} collective-permute-done((bf16[544,128]{1,0:T(8,128)(2,1)S(1)}, bf16[544,128]{1,0:T(8,128)(2,1)S(1)}, u32[]{:S(2)}, u32[]{:S(2)}) %collective-permute-start.2) | collective-permute-done | bytes 139296 | tf_op jit(solution)/shard_map/ppermute | solution.py:492
  13.7 4.0 %collective-permute-start.9 = (bf16[4,2,128,128]{3,2,1,0:T(8,128)(2,1)S(1)}, bf16[4,2,128,128]{3,2,1,0:T(8,128)(2,1)S(1)}, u32[]{:S(2)}, u32[]{:S(2)}) collective-permute-start(bf16[4,2,128,128]{3,2,1,0:T(8,128)(2,1)S(1)} %get-tuple-element.46.rest_0_.kv_hbm), channel_id=1, source_target_pairs={{0,14},{2,0},{4,2},{6,4},{8,6},{10,8},{12,10},{14,12},{1,15},{3,1}... | collective-permute-start | bytes 786440 | tf_op jit(solution)/shard_map/ppermute | solution.py:466
  19.9 4.5 %collective-permute-done.6.rest_1_ = bf16[4,2,128,128]{3,2,1,0:T(8,128)(2,1)S(1)} collective-permute-done((bf16[4,2,128,128]{3,2,1,0:T(8,128)(2,1)S(1)}, bf16[4,2,128,128]{3,2,1,0:T(8,128)(2,1)S(1)}, u32[]{:S(2)}, u32[]{:S(2)}) %collective-permute-start.6) | collective-permute-done | bytes 262176 | tf_op jit(solution)/shard_map/ppermute | solution.py:462
  24.4 2.7 %collective-permute-start.10 = (bf16[4,2,128,128]{3,2,1,0:T(8,128)(2,1)S(1)}, bf16[4,2,128,128]{3,2,1,0:T(8,128)(2,1)S(1)}, u32[]{:S(2)}, u32[]{:S(2)}) collective-permute-start(bf16[4,2,128,128]{3,2,1,0:T(8,128)(2,1)S(1)} %collective-permute-done.9.rest_6_.rest_7_), channel_id=1, source_target_pairs={{0,14},{2,0},{4,2},{6,4},{8,6},{10,8},{12,10},{14,12},{1,15},{3,1}... | collective-permute-start | bytes 786440 | tf_op jit(solution)/shard_map/ppermute | solution.py:466
  27.1 4.6 %collective-permute-done.5.c3 = bf16[128,1024]{1,0:T(8,128)(2,1)S(1)} collective-permute-done((bf16[128,1024]{1,0:T(8,128)(2,1)S(1)}, bf16[128,1024]{1,0:T(8,128)(2,1)S(1)}, u32[]{:S(2)}, u32[]{:S(2)}) %collective-permute-start.5) | collective-permute-done | bytes 262176 | tf_op jit(solution)/shard_map/ppermute | solution.py:492
  33.1 2.7 %collective-permute-start.11 = (bf16[4,2,128,128]{3,2,1,0:T(8,128)(2,1)S(1)}, bf16[4,2,128,128]{3,2,1,0:T(8,128)(2,1)S(1)}, u32[]{:S(2)}, u32[]{:S(2)}) collective-permute-start(bf16[4,2,128,128]{3,2,1,0:T(8,128)(2,1)S(1)} %collective-permute-done.10.rest_5_.rest_6_), channel_id=1, source_target_pairs={{0,14},{2,0},{4,2},{6,4},{8,6},{10,8},{12,10},{14,12},{1,15},{3,1}... | collective-permute-start | bytes 786440 | tf_op jit(solution)/shard_map/ppermute | solution.py:466
  37.3 3.6 %collective-permute-done.8.rest_3_ = bf16[4,2,128,128]{3,2,1,0:T(8,128)(2,1)S(1)} collective-permute-done((bf16[4,2,128,128]{3,2,1,0:T(8,128)(2,1)S(1)}, bf16[4,2,128,128]{3,2,1,0:T(8,128)(2,1)S(1)}, u32[]{:S(2)}, u32[]{:S(2)}) %collective-permute-start.8) | collective-permute-done | bytes 262176 | tf_op jit(solution)/shard_map/ppermute | solution.py:462
  41.7 5.2 %shard_map.157.near_ref = f32[4,128,128]{2,1,0:T(8,128)S(1)} custom-call(s32[1,4]{1,0:T(1,128)S(1)} %copy-done.5, s32[1,4]{1,0:T(1,128)S(1)} %copy-done.6, s32[1,32]{1,0:T(1,128)S(1)} %copy-done.7, bf16[4,160,128]{2,1,0:T(8,128)(2,1)S(1)} %get-tuple-element.47.q_ref.qp_ref, bf16[4,2,128,128]{3,2,1,0:T(8,128)(2,1)} %copy-done.2, ...), custom_call_target="tpu_custom_call" | custom-call | flops 6000000000 | bytes 6000000 | tf_op jit(solution)/shard_map/pallas_call | solution.py:444
  47.8 1.7 %shard_map.158 = (f32[4,128,128]{2,1,0:T(8,128)S(1)}, f32[4,8,128]{2,1,0:T(8,128)S(1)}) custom-call(s32[1,4]{1,0:T(1,128)S(1)} %copy-done.5, s32[1,4]{1,0:T(1,128)S(1)} %copy-done.6, s32[1,32]{1,0:T(1,128)S(1)} %copy-done.7, bf16[4,160,128]{2,1,0:T(8,128)(2,1)S(1)} %get-tuple-element.47.q_ref.qp_ref, bf16[4,128,128]{2,1,0:T(8,128)(2,1)S(1)} %get-tuple-element.48.gate_ref, ...), custom_call_target="tpu_custom_call" | custom-call | flops 2000000000 | bytes 2000000 | tf_op jit(solution)/shard_map/pallas_call | solution.py:444
  49.5 3.1 %collective-permute-start.13 = (f32[4,8,128]{2,1,0:T(8,128)S(1)}, f32[4,8,128]{2,1,0:T(8,128)S(1)}, u32[]{:S(2)}, u32[]{:S(2)}) collective-permute-start(f32[4,8,128]{2,1,0:T(8,128)S(1)} %get-tuple-element.53.s0), channel_id=1, source_target_pairs={{0,1},{1,0},{2,3},{3,2},{4,5},{5,4},{6,7},{7,6},{8,9},{9,8},{10,11... | collective-permute-start | bytes 49160 | tf_op jit(solution)/shard_map/ppermute | solution.py:458
  57.8 2.7 %collective-permute-start.19 = (bf16[4,288,128]{2,1,0:T(8,128)(2,1)S(1)}, bf16[4,288,128]{2,1,0:T(8,128)(2,1)S(1)}, u32[]{:S(2)}, u32[]{:S(2)}) collective-permute-start(bf16[4,288,128]{2,1,0:T(8,128)(2,1)S(1)} %get-tuple-element.61.rest_0_.all_ref), channel_id=1, source_target_pairs={{0,14},{2,0},{4,2},{6,4},{8,6},{10,8},{12,10},{14,12},{1,15},{3,1}... | collective-permute-start | bytes 884744 | tf_op jit(solution)/shard_map/ppermute | solution.py:466
  61.6 6.4 %all-to-all-start = ((bf16[8,128,128]{2,1,0:T(8,128)(2,1)}), bf16[8,128,128]{2,1,0:T(8,128)(2,1)S(1)}, u32[]{:S(2)}, u32[]{:S(2)}) async-start(bf16[8,128,128]{2,1,0:T(8,128)(2,1)} %shard_map.166), calls=%async_computation | async-start | bytes 524288 | tf_op jit(solution)/shard_map/all_to_all | solution.py:549
  68.4 2.4 %collective-permute-start.20 = (bf16[4,288,128]{2,1,0:T(8,128)(2,1)S(1)}, bf16[4,288,128]{2,1,0:T(8,128)(2,1)S(1)}, u32[]{:S(2)}, u32[]{:S(2)}) collective-permute-start(bf16[4,288,128]{2,1,0:T(8,128)(2,1)S(1)} %collective-permute-done.19.rest_6_.rest_7_), channel_id=1, source_target_pairs={{0,14},{2,0},{4,2},{6,4},{8,6},{10,8},{12,10},{14,12},{1,15},{3,1}... | collective-permute-start | bytes 884744 | tf_op jit(solution)/shard_map/ppermute | solution.py:466
  70.8 5.6 %shard_map.164 = (bf16[2,128,128]{2,1,0:T(8,128)(2,1)S(1)}, bf16[2,128,128]{2,1,0:T(8,128)(2,1)S(1)}, bf16[2,128,128]{2,1,0:T(8,128)(2,1)S(1)}, bf16[2,128,128]{2,1,0:T(8,128)(2,1)S(1)}) custom-call(s32[1,4]{1,0:T(1,128)S(1)} %copy-done.5, s32[1,4]{1,0:T(1,128)S(1)} %copy-done.6, s32[1,32]{1,0:T(1,128)S(1)} %copy-done.7, ...), custom_call_target="tpu_custom_call" | custom-call | flops 8000000000 | bytes 8000000 | tf_op jit(solution)/shard_map/pallas_call | solution.py:444
  80.1 6.4 %all-to-all-start.1 = ((bf16[8,128,128]{2,1,0:T(8,128)(2,1)}), bf16[8,128,128]{2,1,0:T(8,128)(2,1)S(1)}, u32[]{:S(2)}, u32[]{:S(2)}) async-start(bf16[8,128,128]{2,1,0:T(8,128)(2,1)} %shard_map.167), calls=%async_computation.1 | async-start | bytes 524288 | tf_op jit(solution)/shard_map/all_to_all | solution.py:566
  86.5 2.5 %collective-permute-start.28 = (bf16[2,128,128]{2,1,0:T(8,128)(2,1)S(1)}, bf16[2,128,128]{2,1,0:T(8,128)(2,1)S(1)}, u32[]{:S(2)}, u32[]{:S(2)}) collective-permute-start(bf16[2,128,128]{2,1,0:T(8,128)(2,1)S(1)} %get-tuple-element.70), channel_id=1, source_target_pairs={{0,17},{1,16},{16,1},{17,0},{2,19},{3,18},{18,3},{19,2},{4,21},{5,... | collective-permute-start | bytes 196616 | tf_op jit(solution)/shard_map/ppermute | solution.py:492
  93.0 6.2 %shard_map.160.near_ref = f32[4,2,128,128]{3,2,1,0:T(8,128)S(1)} custom-call(s32[1,4]{1,0:T(1,128)S(1)} %copy-done.5, s32[1,4]{1,0:T(1,128)S(1)} %copy-done.6, s32[1,32]{1,0:T(1,128)S(1)} %copy-done.7, bf16[4,2,128,128]{3,2,1,0:T(8,128)(2,1)} %copy-done.2, bf16[4,288,128]{2,1,0:T(8,128)(2,1)} %copy-done, bf16[4,288,128]{2,1,0:T(8,128)(2,1)} %copy-done.8, ...), custom_call_target="tpu_custom_call" | custom-call | flops 8000000000 | bytes 8000000 | tf_op jit(solution)/shard_map/pallas_call | solution.py:444
  100.9 7.8 %all-to-all-start.2 = ((bf16[16,128,128]{2,1,0:T(8,128)(2,1)}), bf16[16,128,128]{2,1,0:T(8,128)(2,1)S(1)}, u32[]{:S(2)}, u32[]{:S(2)}) async-start(bf16[16,128,128]{2,1,0:T(8,128)(2,1)} %shard_map.168), calls=%async_computation.2 | async-start | bytes 1048576 | tf_op jit(solution)/shard_map/all_to_all | solution.py:585
  109.5 2.5 %shard_map.161.sc_ref = bf16[4,128,128]{2,1,0:T(8,128)(2,1)S(1)} custom-call(s32[1,4]{1,0:T(1,128)S(1)} %copy-done.5, s32[1,4]{1,0:T(1,128)S(1)} %copy-done.6, s32[1,32]{1,0:T(1,128)S(1)} %copy-done.7, bf16[512,128]{1,0:T(8,128)(2,1)S(1)} %get-tuple-element.55.mixed_ref, s32[4,128]{1,0:T(4,128)S(1)} %bitcast.1, bf16[4,288,128]{2,1,0:T(8,128)(2,1)} %copy-done, ...), custom_call_target="tpu_custom_call" | custom-call | flops 2000000000 | bytes 2000000 | tf_op jit(solution)/shard_map/pallas_call | solution.py:444
  112.0 2.9 %shard_map.162 = (bf16[3,128,128]{2,1,0:T(8,128)(2,1)S(1)}, bf16[3,128,128]{2,1,0:T(8,128)(2,1)S(1)}, bf16[3,128,128]{2,1,0:T(8,128)(2,1)S(1)}, bf16[3,128,128]{2,1,0:T(8,128)(2,1)S(1)}) custom-call(s32[1,4]{1,0:T(1,128)S(1)} %copy-done.5, s32[1,4]{1,0:T(1,128)S(1)} %copy-done.6, s32[1,32]{1,0:T(1,128)S(1)} %copy-done.7, bf16[4,2,128,128]{3,2,1,0:T(8,128)(2,1)} %copy-done.2, ...), custom_call_target="tpu_custom_call" | custom-call | flops 3000000000 | bytes 3000000 | tf_op jit(solution)/shard_map/pallas_call | solution.py:444
  117.8 3.0 %collective-permute-done.24.p2 = bf16[3,128,128]{2,1,0:T(8,128)(2,1)S(1)} collective-permute-done((bf16[3,128,128]{2,1,0:T(8,128)(2,1)S(1)}, bf16[3,128,128]{2,1,0:T(8,128)(2,1)S(1)}, u32[]{:S(2)}, u32[]{:S(2)}) %collective-permute-start.24) | collective-permute-done | bytes 98336 | tf_op jit(solution)/shard_map/ppermute | solution.py:458
  120.8 2.1 %collective-permute-done.25.p3 = bf16[3,128,128]{2,1,0:T(8,128)(2,1)S(1)} collective-permute-done((bf16[3,128,128]{2,1,0:T(8,128)(2,1)S(1)}, bf16[3,128,128]{2,1,0:T(8,128)(2,1)S(1)}, u32[]{:S(2)}, u32[]{:S(2)}) %collective-permute-start.25) | collective-permute-done | bytes 98336 | tf_op jit(solution)/shard_map/ppermute | solution.py:492
  (100 shorter events, 33.1 us)
Async XLA Ops:
  6.1 7.1 %collective-permute-start.2 = (bf16[544,128]{1,0:T(8,128)(2,1)S(1)}, bf16[544,128]{1,0:T(8,128)(2,1)S(1)}, u32[]{:S(2)}, u32[]{:S(2)}) collective-permute-start(bf16[544,128]{1,0:T(8,128)(2,1)S(1)} %get-tuple-element.45), channel_id=1, source_target_pairs={{0,17},{1,16},{16,1},{17,0},{2,19},{3,18},{18,3},{19,2},{4,21},{5,... | collective-permute-start | bytes 417800 | tf_op jit(solution)/shard_map/ppermute | solution.py:492
  13.2 11.2 %collective-permute-start.6 = (bf16[4,2,128,128]{3,2,1,0:T(8,128)(2,1)S(1)}, bf16[4,2,128,128]{3,2,1,0:T(8,128)(2,1)S(1)}, u32[]{:S(2)}, u32[]{:S(2)}) collective-permute-start(bf16[4,2,128,128]{3,2,1,0:T(8,128)(2,1)S(1)} %get-tuple-element.46.rest_0_.kv_hbm), channel_id=1, source_target_pairs={{0,2},{2,4},{4,6},{6,8},{8,10},{10,12},{12,14},{14,0},{1,3},{3,5},... | collective-permute-start | bytes 786440 | tf_op jit(solution)/shard_map/ppermute | solution.py:462
  13.7 10.7 %collective-permute-start.9 = (bf16[4,2,128,128]{3,2,1,0:T(8,128)(2,1)S(1)}, bf16[4,2,128,128]{3,2,1,0:T(8,128)(2,1)S(1)}, u32[]{:S(2)}, u32[]{:S(2)}) collective-permute-start(bf16[4,2,128,128]{3,2,1,0:T(8,128)(2,1)S(1)} %get-tuple-element.46.rest_0_.kv_hbm), channel_id=1, source_target_pairs={{0,14},{2,0},{4,2},{6,4},{8,6},{10,8},{12,10},{14,12},{1,15},{3,1}... | collective-permute-start | bytes 786440 | tf_op jit(solution)/shard_map/ppermute | solution.py:466
  17.8 9.3 %collective-permute-start.3 = (bf16[128,1024]{1,0:T(8,128)(2,1)S(1)}, bf16[128,1024]{1,0:T(8,128)(2,1)S(1)}, u32[]{:S(2)}, u32[]{:S(2)}) collective-permute-start(bf16[128,1024]{1,0:T(8,128)(2,1)S(1)} %copy-done.1), channel_id=1, source_target_pairs={{0,1},{1,0},{2,3},{3,2},{4,5},{5,4},{6,7},{7,6},{8,9},{9,8},{10,11... | collective-permute-start | bytes 786440 | tf_op jit(solution)/shard_map/ppermute | solution.py:458
  17.8 9.3 %collective-permute-start.4 = (bf16[128,1024]{1,0:T(8,128)(2,1)S(1)}, bf16[128,1024]{1,0:T(8,128)(2,1)S(1)}, u32[]{:S(2)}, u32[]{:S(2)}) collective-permute-start(bf16[128,1024]{1,0:T(8,128)(2,1)S(1)} %copy-done.1), channel_id=1, source_target_pairs={{0,16},{16,0},{1,17},{17,1},{2,18},{18,2},{3,19},{19,3},{4,20},{20... | collective-permute-start | bytes 786440 | tf_op jit(solution)/shard_map/ppermute | solution.py:458
  19.0 12.8 %collective-permute-start.5 = (bf16[128,1024]{1,0:T(8,128)(2,1)S(1)}, bf16[128,1024]{1,0:T(8,128)(2,1)S(1)}, u32[]{:S(2)}, u32[]{:S(2)}) collective-permute-start(bf16[128,1024]{1,0:T(8,128)(2,1)S(1)} %copy-done.1), channel_id=1, source_target_pairs={{0,17},{1,16},{16,1},{17,0},{2,19},{3,18},{18,3},{19,2},{4,21},{5,... | collective-permute-start | bytes 786440 | tf_op jit(solution)/shard_map/ppermute | solution.py:492
  24.4 8.7 %collective-permute-start.7 = (bf16[4,2,128,128]{3,2,1,0:T(8,128)(2,1)S(1)}, bf16[4,2,128,128]{3,2,1,0:T(8,128)(2,1)S(1)}, u32[]{:S(2)}, u32[]{:S(2)}) collective-permute-start(bf16[4,2,128,128]{3,2,1,0:T(8,128)(2,1)S(1)} %collective-permute-done.6.rest_1_), channel_id=1, source_target_pairs={{0,2},{2,4},{4,6},{6,8},{8,10},{10,12},{12,14},{14,0},{1,3},{3,5},... | collective-permute-start | bytes 786440 | tf_op jit(solution)/shard_map/ppermute | solution.py:462
  24.4 8.7 %collective-permute-start.10 = (bf16[4,2,128,128]{3,2,1,0:T(8,128)(2,1)S(1)}, bf16[4,2,128,128]{3,2,1,0:T(8,128)(2,1)S(1)}, u32[]{:S(2)}, u32[]{:S(2)}) collective-permute-start(bf16[4,2,128,128]{3,2,1,0:T(8,128)(2,1)S(1)} %collective-permute-done.9.rest_6_.rest_7_), channel_id=1, source_target_pairs={{0,14},{2,0},{4,2},{6,4},{8,6},{10,8},{12,10},{14,12},{1,15},{3,1}... | collective-permute-start | bytes 786440 | tf_op jit(solution)/shard_map/ppermute | solution.py:466
  33.1 7.8 %collective-permute-start.8 = (bf16[4,2,128,128]{3,2,1,0:T(8,128)(2,1)S(1)}, bf16[4,2,128,128]{3,2,1,0:T(8,128)(2,1)S(1)}, u32[]{:S(2)}, u32[]{:S(2)}) collective-permute-start(bf16[4,2,128,128]{3,2,1,0:T(8,128)(2,1)S(1)} %collective-permute-done.7.rest_2_), channel_id=1, source_target_pairs={{0,2},{2,4},{4,6},{6,8},{8,10},{10,12},{12,14},{14,0},{1,3},{3,5},... | collective-permute-start | bytes 786440 | tf_op jit(solution)/shard_map/ppermute | solution.py:462
  33.1 7.8 %collective-permute-start.11 = (bf16[4,2,128,128]{3,2,1,0:T(8,128)(2,1)S(1)}, bf16[4,2,128,128]{3,2,1,0:T(8,128)(2,1)S(1)}, u32[]{:S(2)}, u32[]{:S(2)}) collective-permute-start(bf16[4,2,128,128]{3,2,1,0:T(8,128)(2,1)S(1)} %collective-permute-done.10.rest_5_.rest_6_), channel_id=1, source_target_pairs={{0,14},{2,0},{4,2},{6,4},{8,6},{10,8},{12,10},{14,12},{1,15},{3,1}... | collective-permute-start | bytes 786440 | tf_op jit(solution)/shard_map/ppermute | solution.py:466
  40.9 6.9 %collective-permute-start.12 = (bf16[4,2,128,128]{3,2,1,0:T(8,128)(2,1)S(1)}, bf16[4,2,128,128]{3,2,1,0:T(8,128)(2,1)S(1)}, u32[]{:S(2)}, u32[]{:S(2)}) collective-permute-start(bf16[4,2,128,128]{3,2,1,0:T(8,128)(2,1)S(1)} %collective-permute-done.8.rest_3_), channel_id=1, source_target_pairs={{0,2},{2,4},{4,6},{6,8},{8,10},{10,12},{12,14},{14,0},{1,3},{3,5},... | collective-permute-start | bytes 786440 | tf_op jit(solution)/shard_map/ppermute | solution.py:462
  57.7 10.3 %collective-permute-start.16 = (bf16[4,288,128]{2,1,0:T(8,128)(2,1)S(1)}, bf16[4,288,128]{2,1,0:T(8,128)(2,1)S(1)}, u32[]{:S(2)}, u32[]{:S(2)}) collective-permute-start(bf16[4,288,128]{2,1,0:T(8,128)(2,1)S(1)} %get-tuple-element.61.rest_0_.all_ref), channel_id=1, source_target_pairs={{0,2},{2,4},{4,6},{6,8},{8,10},{10,12},{12,14},{14,0},{1,3},{3,5},... | collective-permute-start | bytes 884744 | tf_op jit(solution)/shard_map/ppermute | solution.py:462
  57.8 10.2 %collective-permute-start.19 = (bf16[4,288,128]{2,1,0:T(8,128)(2,1)S(1)}, bf16[4,288,128]{2,1,0:T(8,128)(2,1)S(1)}, u32[]{:S(2)}, u32[]{:S(2)}) collective-permute-start(bf16[4,288,128]{2,1,0:T(8,128)(2,1)S(1)} %get-tuple-element.61.rest_0_.all_ref), channel_id=1, source_target_pairs={{0,14},{2,0},{4,2},{6,4},{8,6},{10,8},{12,10},{14,12},{1,15},{3,1}... | collective-permute-start | bytes 884744 | tf_op jit(solution)/shard_map/ppermute | solution.py:466
  61.6 14.8 %all-to-all-start = ((bf16[8,128,128]{2,1,0:T(8,128)(2,1)}), bf16[8,128,128]{2,1,0:T(8,128)(2,1)S(1)}, u32[]{:S(2)}, u32[]{:S(2)}) async-start(bf16[8,128,128]{2,1,0:T(8,128)(2,1)} %shard_map.166), calls=%async_computation | async-start | bytes 524288 | tf_op jit(solution)/shard_map/all_to_all | solution.py:549
  68.0 8.6 %collective-permute-start.17 = (bf16[4,288,128]{2,1,0:T(8,128)(2,1)S(1)}, bf16[4,288,128]{2,1,0:T(8,128)(2,1)S(1)}, u32[]{:S(2)}, u32[]{:S(2)}) collective-permute-start(bf16[4,288,128]{2,1,0:T(8,128)(2,1)S(1)} %collective-permute-done.16.rest_1_), channel_id=1, source_target_pairs={{0,2},{2,4},{4,6},{6,8},{8,10},{10,12},{12,14},{14,0},{1,3},{3,5},... | collective-permute-start | bytes 884744 | tf_op jit(solution)/shard_map/ppermute | solution.py:462
  68.4 8.2 %collective-permute-start.20 = (bf16[4,288,128]{2,1,0:T(8,128)(2,1)S(1)}, bf16[4,288,128]{2,1,0:T(8,128)(2,1)S(1)}, u32[]{:S(2)}, u32[]{:S(2)}) collective-permute-start(bf16[4,288,128]{2,1,0:T(8,128)(2,1)S(1)} %collective-permute-done.19.rest_6_.rest_7_), channel_id=1, source_target_pairs={{0,14},{2,0},{4,2},{6,4},{8,6},{10,8},{12,10},{14,12},{1,15},{3,1}... | collective-permute-start | bytes 884744 | tf_op jit(solution)/shard_map/ppermute | solution.py:466
  76.6 9.9 %collective-permute-start.18 = (bf16[4,288,128]{2,1,0:T(8,128)(2,1)S(1)}, bf16[4,288,128]{2,1,0:T(8,128)(2,1)S(1)}, u32[]{:S(2)}, u32[]{:S(2)}) collective-permute-start(bf16[4,288,128]{2,1,0:T(8,128)(2,1)S(1)} %collective-permute-done.17.rest_2_), channel_id=1, source_target_pairs={{0,2},{2,4},{4,6},{6,8},{8,10},{10,12},{12,14},{14,0},{1,3},{3,5},... | collective-permute-start | bytes 884744 | tf_op jit(solution)/shard_map/ppermute | solution.py:462
  77.9 14.4 %collective-permute-start.21 = (bf16[4,288,128]{2,1,0:T(8,128)(2,1)S(1)}, bf16[4,288,128]{2,1,0:T(8,128)(2,1)S(1)}, u32[]{:S(2)}, u32[]{:S(2)}) collective-permute-start(bf16[4,288,128]{2,1,0:T(8,128)(2,1)S(1)} %collective-permute-done.20.rest_5_.rest_6_), channel_id=1, source_target_pairs={{0,14},{2,0},{4,2},{6,4},{8,6},{10,8},{12,10},{14,12},{1,15},{3,1}... | collective-permute-start | bytes 884744 | tf_op jit(solution)/shard_map/ppermute | solution.py:466
  80.1 20.0 %all-to-all-start.1 = ((bf16[8,128,128]{2,1,0:T(8,128)(2,1)}), bf16[8,128,128]{2,1,0:T(8,128)(2,1)S(1)}, u32[]{:S(2)}, u32[]{:S(2)}) async-start(bf16[8,128,128]{2,1,0:T(8,128)(2,1)} %shard_map.167), calls=%async_computation.1 | async-start | bytes 524288 | tf_op jit(solution)/shard_map/all_to_all | solution.py:566
  86.5 12.8 %collective-permute-start.28 = (bf16[2,128,128]{2,1,0:T(8,128)(2,1)S(1)}, bf16[2,128,128]{2,1,0:T(8,128)(2,1)S(1)}, u32[]{:S(2)}, u32[]{:S(2)}) collective-permute-start(bf16[2,128,128]{2,1,0:T(8,128)(2,1)S(1)} %get-tuple-element.70), channel_id=1, source_target_pairs={{0,17},{1,16},{16,1},{17,0},{2,19},{3,18},{18,3},{19,2},{4,21},{5,... | collective-permute-start | bytes 196616 | tf_op jit(solution)/shard_map/ppermute | solution.py:492
  89.0 10.3 %collective-permute-start.27 = (bf16[2,128,128]{2,1,0:T(8,128)(2,1)S(1)}, bf16[2,128,128]{2,1,0:T(8,128)(2,1)S(1)}, u32[]{:S(2)}, u32[]{:S(2)}) collective-permute-start(bf16[2,128,128]{2,1,0:T(8,128)(2,1)S(1)} %get-tuple-element.68), channel_id=1, source_target_pairs={{0,16},{16,0},{1,17},{17,1},{2,18},{18,2},{3,19},{19,3},{4,20},{20... | collective-permute-start | bytes 196616 | tf_op jit(solution)/shard_map/ppermute | solution.py:458
  90.6 8.7 %collective-permute-start.26 = (bf16[2,128,128]{2,1,0:T(8,128)(2,1)S(1)}, bf16[2,128,128]{2,1,0:T(8,128)(2,1)S(1)}, u32[]{:S(2)}, u32[]{:S(2)}) collective-permute-start(bf16[2,128,128]{2,1,0:T(8,128)(2,1)S(1)} %get-tuple-element.66), channel_id=1, source_target_pairs={{0,1},{1,0},{2,3},{3,2},{4,5},{5,4},{6,7},{7,6},{8,9},{9,8},{10,11... | collective-permute-start | bytes 196616 | tf_op jit(solution)/shard_map/ppermute | solution.py:458
  90.6 18.2 %collective-permute-start.22 = (bf16[4,288,128]{2,1,0:T(8,128)(2,1)S(1)}, bf16[4,288,128]{2,1,0:T(8,128)(2,1)S(1)}, u32[]{:S(2)}, u32[]{:S(2)}) collective-permute-start(bf16[4,288,128]{2,1,0:T(8,128)(2,1)S(1)} %collective-permute-done.18.rest_3_), channel_id=1, source_target_pairs={{0,2},{2,4},{4,6},{6,8},{8,10},{10,12},{12,14},{14,0},{1,3},{3,5},... | collective-permute-start | bytes 884744 | tf_op jit(solution)/shard_map/ppermute | solution.py:462
  100.9 21.9 %all-to-all-start.2 = ((bf16[16,128,128]{2,1,0:T(8,128)(2,1)}), bf16[16,128,128]{2,1,0:T(8,128)(2,1)S(1)}, u32[]{:S(2)}, u32[]{:S(2)}) async-start(bf16[16,128,128]{2,1,0:T(8,128)(2,1)} %shard_map.168), calls=%async_computation.2 | async-start | bytes 1048576 | tf_op jit(solution)/shard_map/all_to_all | solution.py:585
  (30 other events, 237.9 us)

commit v6 on v5

--- a/solution.py
+++ b/solution.py
@@ -488,6 +488,10 @@
     return [(HBM, pltpu.with_memory_space_constraint(a, pltpu.HBM)) for a in arrays]
 
 
+def loose(arrays):
+    return [(HBM, a) if i in (3, 4) else raw([a])[0] for i, a in enumerate(arrays)]
+
+
 def swap(pieces):
     both = lax.ppermute(pieces[3], ("xl", "core"), [(i, 3 - i) for i in range(4)])
     return [pieces[0], flip(pieces[1], "core"), flip(pieces[2], "xl"), both]
@@ -529,7 +533,7 @@
     )
     (att_near,) = call(
         forward_near_kernel,
-        facts + vm(qp) + raw(kvs[:4] + kvs[5:]),
+        facts + vm(qp) + loose(kvs[:4] + kvs[5:]),
         [(block, F32)],
         [kv_buffer, places, sems],
         us=6,
@@ -585,7 +589,7 @@
     near = lax.all_to_all(lines, ("xh", "y", "xl"), split_axis=0, concat_axis=0, tiled=True)
     (key_sums,) = call(
         key_near_kernel,
-        facts + raw([kv] + pairs[:4] + pairs[5:]),
+        facts + raw([kv]) + loose(pairs[:4] + pairs[5:]),
         [((4, 2, 128, 128), F32)],
         [pltpu.VMEM((4, 2, 128, 128), BF16), pltpu.VMEM((32, 288, 128), BF16), places, sems],
         us=8,

time: 127 us -> 125 us (0.984)
  starting transfers between devices: 59.7 us -> 57 us
  local copies, waits for them, and re-layouts: 2.28 us -> 0.79 us
  Pallas kernels: 34.6 us -> 35.9 us
    all_to_all x1, starting transfers between devices: 7.8 us -> 5.25 us  [body(): lax.all_to_all(lines, ('xh', 'y', 'xl'), split_axis=0, concat_axis=0, til...]
    unnamed x42, local copies, waits for them, and re-layouts: 2.28 us -> 0.79 us
  transfers between devices with their start and end apart: 33 -> 33, of which waited for: 12 -> 12; matrix products, arithmetic and copies ran while one was open for 0% -> 0% of each run, Pallas kernels for 22% -> 24%
where the time goes in v6:
time: 125 us; the launch traced here: 124 us
  starting transfers between devices  57 us (46%)
  Pallas kernels  35.9 us (29%)
  waiting for transfers between devices  29.7 us (24%)
    pallas_call x16, Pallas kernels, call(): pl.pallas_call(kernel, in_specs=[spec for spec, _ in ins], out_specs=[VM]...  35.9 us
    ppermute x6, starting transfers between devices, down(): return lax.ppermute(array, 'z', [(i, (i + 7) % 8) for i in range(8)])  16.2 us
    ppermute x5, waiting for transfers between devices, swap(): lax.ppermute(pieces[3], ('xl', 'core'), [(i, 3 - i) for i in range(4)])  13.7 us
    ppermute x11, starting transfers between devices, flip(): return lax.ppermute(array, axis, [(0, 1), (1, 0)])  13.4 us
    ppermute x8, waiting for transfers between devices, up(): return lax.ppermute(array, 'z', [(i, (i + 1) % 8) for i in range(8)])  11.4 us
    all_to_all x1, starting transfers between devices, body(): lax.all_to_all(gw, ('xh', 'y'), split_axis=0, concat_axis=0, tiled=True)  6.36 us
    ppermute x5, starting transfers between devices, swap(): lax.ppermute(pieces[3], ('xl', 'core'), [(i, 3 - i) for i in range(4)])  6.34 us
    all_to_all x1, starting transfers between devices, body(): line = lax.all_to_all(piece, 'z', split_axis=0, concat_axis=0, tiled=True)  5.83 us
  transfers between devices with their start and end apart: 33, of which 12 were waited for; matrix products, arithmetic and copies ran while one was open for 0% of the time, Pallas kernels for 24%

profile of v6, /device:TPU:1, one launch (start us, length us, event | category | flops | bytes accessed | tf_op | source)
XLA Modules:
  0.0 124.4 jit_solution(4022497932135926456)
XLA Ops:
  0.6 2.0 %shard_map.154 = (bf16[544,128]{1,0:T(8,128)(2,1)S(1)}, bf16[544,128]{1,0:T(8,128)(2,1)S(1)}, bf16[544,128]{1,0:T(8,128)(2,1)S(1)}, bf16[544,128]{1,0:T(8,128)(2,1)S(1)}) custom-call(bf16[128,512]{1,0:T(8,128)(2,1)} %k_ref.1, bf16[128,512]{1,0:T(8,128)(2,1)} %v_ref.1, bf16[128,512]{1,0:T(8,128)(2,1)} %q_ref.1, bf16[128,512]{1,0:T(8,128)(2,1)} %g_ref.1, ...), custom_call_target="tpu_custom_call" | custom-call | flops 2000000000 | bytes 2000000 | tf_op jit(solution)/shard_map/pallas_call | solution.py:444
  2.6 2.1 %collective-permute-start.1 = (bf16[544,128]{1,0:T(8,128)(2,1)S(1)}, bf16[544,128]{1,0:T(8,128)(2,1)S(1)}, u32[]{:S(2)}, u32[]{:S(2)}) collective-permute-start(bf16[544,128]{1,0:T(8,128)(2,1)S(1)} %get-tuple-element.44), channel_id=1, source_target_pairs={{0,16},{16,0},{1,17},{17,1},{2,18},{18,2},{3,19},{19,3},{4,20},{20... | collective-permute-start | bytes 417800 | tf_op jit(solution)/shard_map/ppermute | solution.py:458
  7.6 5.5 %collective-permute-done.2.p3 = bf16[544,128]{1,0:T(8,128)(2,1)S(1)} collective-permute-done((bf16[544,128]{1,0:T(8,128)(2,1)S(1)}, bf16[544,128]{1,0:T(8,128)(2,1)S(1)}, u32[]{:S(2)}, u32[]{:S(2)}) %collective-permute-start.2) | collective-permute-done | bytes 139296 | tf_op jit(solution)/shard_map/ppermute | solution.py:496
  13.7 4.0 %collective-permute-start.9 = (bf16[4,2,128,128]{3,2,1,0:T(8,128)(2,1)S(1)}, bf16[4,2,128,128]{3,2,1,0:T(8,128)(2,1)S(1)}, u32[]{:S(2)}, u32[]{:S(2)}) collective-permute-start(bf16[4,2,128,128]{3,2,1,0:T(8,128)(2,1)S(1)} %get-tuple-element.46.rest_0_.kv_hbm), channel_id=1, source_target_pairs={{0,14},{2,0},{4,2},{6,4},{8,6},{10,8},{12,10},{14,12},{1,15},{3,1}... | collective-permute-start | bytes 786440 | tf_op jit(solution)/shard_map/ppermute | solution.py:466
  19.9 4.5 %collective-permute-done.6.rest_1_ = bf16[4,2,128,128]{3,2,1,0:T(8,128)(2,1)S(1)} collective-permute-done((bf16[4,2,128,128]{3,2,1,0:T(8,128)(2,1)S(1)}, bf16[4,2,128,128]{3,2,1,0:T(8,128)(2,1)S(1)}, u32[]{:S(2)}, u32[]{:S(2)}) %collective-permute-start.6) | collective-permute-done | bytes 262176 | tf_op jit(solution)/shard_map/ppermute | solution.py:462
  24.4 2.7 %collective-permute-start.10 = (bf16[4,2,128,128]{3,2,1,0:T(8,128)(2,1)S(1)}, bf16[4,2,128,128]{3,2,1,0:T(8,128)(2,1)S(1)}, u32[]{:S(2)}, u32[]{:S(2)}) collective-permute-start(bf16[4,2,128,128]{3,2,1,0:T(8,128)(2,1)S(1)} %collective-permute-done.9.rest_6_.rest_7_), channel_id=1, source_target_pairs={{0,14},{2,0},{4,2},{6,4},{8,6},{10,8},{12,10},{14,12},{1,15},{3,1}... | collective-permute-start | bytes 786440 | tf_op jit(solution)/shard_map/ppermute | solution.py:466
  27.1 4.6 %collective-permute-done.5.c3 = bf16[128,1024]{1,0:T(8,128)(2,1)S(1)} collective-permute-done((bf16[128,1024]{1,0:T(8,128)(2,1)S(1)}, bf16[128,1024]{1,0:T(8,128)(2,1)S(1)}, u32[]{:S(2)}, u32[]{:S(2)}) %collective-permute-start.5) | collective-permute-done | bytes 262176 | tf_op jit(solution)/shard_map/ppermute | solution.py:496
  33.1 2.7 %collective-permute-start.11 = (bf16[4,2,128,128]{3,2,1,0:T(8,128)(2,1)S(1)}, bf16[4,2,128,128]{3,2,1,0:T(8,128)(2,1)S(1)}, u32[]{:S(2)}, u32[]{:S(2)}) collective-permute-start(bf16[4,2,128,128]{3,2,1,0:T(8,128)(2,1)S(1)} %collective-permute-done.10.rest_5_.rest_6_), channel_id=1, source_target_pairs={{0,14},{2,0},{4,2},{6,4},{8,6},{10,8},{12,10},{14,12},{1,15},{3,1}... | collective-permute-start | bytes 786440 | tf_op jit(solution)/shard_map/ppermute | solution.py:466
  37.3 3.6 %collective-permute-done.8.rest_3_ = bf16[4,2,128,128]{3,2,1,0:T(8,128)(2,1)S(1)} collective-permute-done((bf16[4,2,128,128]{3,2,1,0:T(8,128)(2,1)S(1)}, bf16[4,2,128,128]{3,2,1,0:T(8,128)(2,1)S(1)}, u32[]{:S(2)}, u32[]{:S(2)}) %collective-permute-start.8) | collective-permute-done | bytes 262176 | tf_op jit(solution)/shard_map/ppermute | solution.py:462
  40.9 5.0 %shard_map.157.near_ref = f32[4,128,128]{2,1,0:T(8,128)S(1)} custom-call(s32[1,4]{1,0:T(1,128)S(1)} %copy-done.9, s32[1,4]{1,0:T(1,128)S(1)} %copy-done.10, s32[1,32]{1,0:T(1,128)S(1)} %copy-done.11, bf16[4,160,128]{2,1,0:T(8,128)(2,1)S(1)} %get-tuple-element.47.q_ref.qp_ref, bf16[4,2,128,128]{3,2,1,0:T(8,128)(2,1)} %copy-done.4, ...), custom_call_target="tpu_custom_call" | custom-call | flops 6000000000 | bytes 6000000 | tf_op jit(solution)/shard_map/pallas_call | solution.py:444
  47.8 1.7 %shard_map.158 = (f32[4,128,128]{2,1,0:T(8,128)S(1)}, f32[4,8,128]{2,1,0:T(8,128)S(1)}) custom-call(s32[1,4]{1,0:T(1,128)S(1)} %copy-done.9, s32[1,4]{1,0:T(1,128)S(1)} %copy-done.10, s32[1,32]{1,0:T(1,128)S(1)} %copy-done.11, bf16[4,160,128]{2,1,0:T(8,128)(2,1)S(1)} %get-tuple-element.47.q_ref.qp_ref, bf16[4,128,128]{2,1,0:T(8,128)(2,1)S(1)} %get-tuple-element.48.gate_ref, ...), custom_call_target="tpu_custom_call" | custom-call | flops 2000000000 | bytes 2000000 | tf_op jit(solution)/shard_map/pallas_call | solution.py:444
  49.5 3.1 %collective-permute-start.13 = (f32[4,8,128]{2,1,0:T(8,128)S(1)}, f32[4,8,128]{2,1,0:T(8,128)S(1)}, u32[]{:S(2)}, u32[]{:S(2)}) collective-permute-start(f32[4,8,128]{2,1,0:T(8,128)S(1)} %get-tuple-element.53.s0), channel_id=1, source_target_pairs={{0,1},{1,0},{2,3},{3,2},{4,5},{5,4},{6,7},{7,6},{8,9},{9,8},{10,11... | collective-permute-start | bytes 49160 | tf_op jit(solution)/shard_map/ppermute | solution.py:458
  57.8 2.7 %collective-permute-start.19 = (bf16[4,288,128]{2,1,0:T(8,128)(2,1)S(1)}, bf16[4,288,128]{2,1,0:T(8,128)(2,1)S(1)}, u32[]{:S(2)}, u32[]{:S(2)}) collective-permute-start(bf16[4,288,128]{2,1,0:T(8,128)(2,1)S(1)} %get-tuple-element.61.rest_0_.all_ref), channel_id=1, source_target_pairs={{0,14},{2,0},{4,2},{6,4},{8,6},{10,8},{12,10},{14,12},{1,15},{3,1}... | collective-permute-start | bytes 884744 | tf_op jit(solution)/shard_map/ppermute | solution.py:466
  61.6 6.4 %all-to-all-start = ((bf16[8,128,128]{2,1,0:T(8,128)(2,1)}), bf16[8,128,128]{2,1,0:T(8,128)(2,1)S(1)}, u32[]{:S(2)}, u32[]{:S(2)}) async-start(bf16[8,128,128]{2,1,0:T(8,128)(2,1)} %shard_map.166), calls=%async_computation | async-start | bytes 524288 | tf_op jit(solution)/shard_map/all_to_all | solution.py:553
  68.1 2.7 %collective-permute-start.20 = (bf16[4,288,128]{2,1,0:T(8,128)(2,1)S(1)}, bf16[4,288,128]{2,1,0:T(8,128)(2,1)S(1)}, u32[]{:S(2)}, u32[]{:S(2)}) collective-permute-start(bf16[4,288,128]{2,1,0:T(8,128)(2,1)S(1)} %collective-permute-done.19.rest_6_.rest_7_), channel_id=1, source_target_pairs={{0,14},{2,0},{4,2},{6,4},{8,6},{10,8},{12,10},{14,12},{1,15},{3,1}... | collective-permute-start | bytes 884744 | tf_op jit(solution)/shard_map/ppermute | solution.py:466
  70.8 5.6 %shard_map.164 = (bf16[2,128,128]{2,1,0:T(8,128)(2,1)S(1)}, bf16[2,128,128]{2,1,0:T(8,128)(2,1)S(1)}, bf16[2,128,128]{2,1,0:T(8,128)(2,1)S(1)}, bf16[2,128,128]{2,1,0:T(8,128)(2,1)S(1)}) custom-call(s32[1,4]{1,0:T(1,128)S(1)} %copy-done.9, s32[1,4]{1,0:T(1,128)S(1)} %copy-done.10, s32[1,32]{1,0:T(1,128)S(1)} %copy-done.11, ...), custom_call_target="tpu_custom_call" | custom-call | flops 8000000000 | bytes 8000000 | tf_op jit(solution)/shard_map/pallas_call | solution.py:444
  80.1 5.8 %all-to-all-start.1 = ((bf16[8,128,128]{2,1,0:T(8,128)(2,1)}), bf16[8,128,128]{2,1,0:T(8,128)(2,1)S(1)}, u32[]{:S(2)}, u32[]{:S(2)}) async-start(bf16[8,128,128]{2,1,0:T(8,128)(2,1)} %shard_map.167), calls=%async_computation.1 | async-start | bytes 524288 | tf_op jit(solution)/shard_map/all_to_all | solution.py:570
  86.0 2.9 %collective-permute-start.28 = (bf16[2,128,128]{2,1,0:T(8,128)(2,1)S(1)}, bf16[2,128,128]{2,1,0:T(8,128)(2,1)S(1)}, u32[]{:S(2)}, u32[]{:S(2)}) collective-permute-start(bf16[2,128,128]{2,1,0:T(8,128)(2,1)S(1)} %get-tuple-element.70), channel_id=1, source_target_pairs={{0,17},{1,16},{16,1},{17,0},{2,19},{3,18},{18,3},{19,2},{4,21},{5,... | collective-permute-start | bytes 196616 | tf_op jit(solution)/shard_map/ppermute | solution.py:496
  92.1 7.6 %shard_map.160.near_ref = f32[4,2,128,128]{3,2,1,0:T(8,128)S(1)} custom-call(s32[1,4]{1,0:T(1,128)S(1)} %copy-done.9, s32[1,4]{1,0:T(1,128)S(1)} %copy-done.10, s32[1,32]{1,0:T(1,128)S(1)} %copy-done.11, bf16[4,2,128,128]{3,2,1,0:T(8,128)(2,1)} %copy-done.4, bf16[4,288,128]{2,1,0:T(8,128)(2,1)} %copy-done, bf16[4,288,128]{2,1,0:T(8,128)(2,1)} %copy-done.12, ...), custom_call_target="tpu_custom_call" | custom-call | flops 8000000000 | bytes 8000000 | tf_op jit(solution)/shard_map/pallas_call | solution.py:444
  101.4 5.2 %all-to-all-start.2 = ((bf16[16,128,128]{2,1,0:T(8,128)(2,1)}), bf16[16,128,128]{2,1,0:T(8,128)(2,1)S(1)}, u32[]{:S(2)}, u32[]{:S(2)}) async-start(bf16[16,128,128]{2,1,0:T(8,128)(2,1)} %shard_map.168), calls=%async_computation.2 | async-start | bytes 1048576 | tf_op jit(solution)/shard_map/all_to_all | solution.py:589
  107.4 2.5 %shard_map.161.sc_ref = bf16[4,128,128]{2,1,0:T(8,128)(2,1)S(1)} custom-call(s32[1,4]{1,0:T(1,128)S(1)} %copy-done.9, s32[1,4]{1,0:T(1,128)S(1)} %copy-done.10, s32[1,32]{1,0:T(1,128)S(1)} %copy-done.11, bf16[512,128]{1,0:T(8,128)(2,1)S(1)} %get-tuple-element.55.mixed_ref, s32[4,128]{1,0:T(4,128)S(1)} %bitcast.1, bf16[4,288,128]{2,1,0:T(8,128)(2,1)} %copy-done, ...), custom_call_target="tpu_custom_call" | custom-call | flops 2000000000 | bytes 2000000 | tf_op jit(solution)/shard_map/pallas_call | solution.py:444
  109.9 2.9 %shard_map.162 = (bf16[3,128,128]{2,1,0:T(8,128)(2,1)S(1)}, bf16[3,128,128]{2,1,0:T(8,128)(2,1)S(1)}, bf16[3,128,128]{2,1,0:T(8,128)(2,1)S(1)}, bf16[3,128,128]{2,1,0:T(8,128)(2,1)S(1)}) custom-call(s32[1,4]{1,0:T(1,128)S(1)} %copy-done.9, s32[1,4]{1,0:T(1,128)S(1)} %copy-done.10, s32[1,32]{1,0:T(1,128)S(1)} %copy-done.11, ...), custom_call_target="tpu_custom_call" | custom-call | flops 3000000000 | bytes 3000000 | tf_op jit(solution)/shard_map/pallas_call | solution.py:444
  115.8 3.0 %collective-permute-done.24.p2 = bf16[3,128,128]{2,1,0:T(8,128)(2,1)S(1)} collective-permute-done((bf16[3,128,128]{2,1,0:T(8,128)(2,1)S(1)}, bf16[3,128,128]{2,1,0:T(8,128)(2,1)S(1)}, u32[]{:S(2)}, u32[]{:S(2)}) %collective-permute-start.24) | collective-permute-done | bytes 98336 | tf_op jit(solution)/shard_map/ppermute | solution.py:458
  118.8 2.1 %collective-permute-done.25.p3 = bf16[3,128,128]{2,1,0:T(8,128)(2,1)S(1)} collective-permute-done((bf16[3,128,128]{2,1,0:T(8,128)(2,1)S(1)}, bf16[3,128,128]{2,1,0:T(8,128)(2,1)S(1)}, u32[]{:S(2)}, u32[]{:S(2)}) %collective-permute-start.25) | collective-permute-done | bytes 98336 | tf_op jit(solution)/shard_map/ppermute | solution.py:496
  (100 shorter events, 32.3 us)
Async XLA Ops:
  6.1 7.1 %collective-permute-start.2 = (bf16[544,128]{1,0:T(8,128)(2,1)S(1)}, bf16[544,128]{1,0:T(8,128)(2,1)S(1)}, u32[]{:S(2)}, u32[]{:S(2)}) collective-permute-start(bf16[544,128]{1,0:T(8,128)(2,1)S(1)} %get-tuple-element.45), channel_id=1, source_target_pairs={{0,17},{1,16},{16,1},{17,0},{2,19},{3,18},{18,3},{19,2},{4,21},{5,... | collective-permute-start | bytes 417800 | tf_op jit(solution)/shard_map/ppermute | solution.py:496
  13.2 11.2 %collective-permute-start.6 = (bf16[4,2,128,128]{3,2,1,0:T(8,128)(2,1)S(1)}, bf16[4,2,128,128]{3,2,1,0:T(8,128)(2,1)S(1)}, u32[]{:S(2)}, u32[]{:S(2)}) collective-permute-start(bf16[4,2,128,128]{3,2,1,0:T(8,128)(2,1)S(1)} %get-tuple-element.46.rest_0_.kv_hbm), channel_id=1, source_target_pairs={{0,2},{2,4},{4,6},{6,8},{8,10},{10,12},{12,14},{14,0},{1,3},{3,5},... | collective-permute-start | bytes 786440 | tf_op jit(solution)/shard_map/ppermute | solution.py:462
  13.7 10.7 %collective-permute-start.9 = (bf16[4,2,128,128]{3,2,1,0:T(8,128)(2,1)S(1)}, bf16[4,2,128,128]{3,2,1,0:T(8,128)(2,1)S(1)}, u32[]{:S(2)}, u32[]{:S(2)}) collective-permute-start(bf16[4,2,128,128]{3,2,1,0:T(8,128)(2,1)S(1)} %get-tuple-element.46.rest_0_.kv_hbm), channel_id=1, source_target_pairs={{0,14},{2,0},{4,2},{6,4},{8,6},{10,8},{12,10},{14,12},{1,15},{3,1}... | collective-permute-start | bytes 786440 | tf_op jit(solution)/shard_map/ppermute | solution.py:466
  17.8 9.3 %collective-permute-start.3 = (bf16[128,1024]{1,0:T(8,128)(2,1)S(1)}, bf16[128,1024]{1,0:T(8,128)(2,1)S(1)}, u32[]{:S(2)}, u32[]{:S(2)}) collective-permute-start(bf16[128,1024]{1,0:T(8,128)(2,1)S(1)} %copy-done.3), channel_id=1, source_target_pairs={{0,1},{1,0},{2,3},{3,2},{4,5},{5,4},{6,7},{7,6},{8,9},{9,8},{10,11... | collective-permute-start | bytes 786440 | tf_op jit(solution)/shard_map/ppermute | solution.py:458
  17.8 9.3 %collective-permute-start.4 = (bf16[128,1024]{1,0:T(8,128)(2,1)S(1)}, bf16[128,1024]{1,0:T(8,128)(2,1)S(1)}, u32[]{:S(2)}, u32[]{:S(2)}) collective-permute-start(bf16[128,1024]{1,0:T(8,128)(2,1)S(1)} %copy-done.3), channel_id=1, source_target_pairs={{0,16},{16,0},{1,17},{17,1},{2,18},{18,2},{3,19},{19,3},{4,20},{20... | collective-permute-start | bytes 786440 | tf_op jit(solution)/shard_map/ppermute | solution.py:458
  19.0 12.8 %collective-permute-start.5 = (bf16[128,1024]{1,0:T(8,128)(2,1)S(1)}, bf16[128,1024]{1,0:T(8,128)(2,1)S(1)}, u32[]{:S(2)}, u32[]{:S(2)}) collective-permute-start(bf16[128,1024]{1,0:T(8,128)(2,1)S(1)} %copy-done.3), channel_id=1, source_target_pairs={{0,17},{1,16},{16,1},{17,0},{2,19},{3,18},{18,3},{19,2},{4,21},{5,... | collective-permute-start | bytes 786440 | tf_op jit(solution)/shard_map/ppermute | solution.py:496
  24.4 8.7 %collective-permute-start.7 = (bf16[4,2,128,128]{3,2,1,0:T(8,128)(2,1)S(1)}, bf16[4,2,128,128]{3,2,1,0:T(8,128)(2,1)S(1)}, u32[]{:S(2)}, u32[]{:S(2)}) collective-permute-start(bf16[4,2,128,128]{3,2,1,0:T(8,128)(2,1)S(1)} %collective-permute-done.6.rest_1_), channel_id=1, source_target_pairs={{0,2},{2,4},{4,6},{6,8},{8,10},{10,12},{12,14},{14,0},{1,3},{3,5},... | collective-permute-start | bytes 786440 | tf_op jit(solution)/shard_map/ppermute | solution.py:462
  24.4 8.7 %collective-permute-start.10 = (bf16[4,2,128,128]{3,2,1,0:T(8,128)(2,1)S(1)}, bf16[4,2,128,128]{3,2,1,0:T(8,128)(2,1)S(1)}, u32[]{:S(2)}, u32[]{:S(2)}) collective-permute-start(bf16[4,2,128,128]{3,2,1,0:T(8,128)(2,1)S(1)} %collective-permute-done.9.rest_6_.rest_7_), channel_id=1, source_target_pairs={{0,14},{2,0},{4,2},{6,4},{8,6},{10,8},{12,10},{14,12},{1,15},{3,1}... | collective-permute-start | bytes 786440 | tf_op jit(solution)/shard_map/ppermute | solution.py:466
  33.1 7.8 %collective-permute-start.8 = (bf16[4,2,128,128]{3,2,1,0:T(8,128)(2,1)S(1)}, bf16[4,2,128,128]{3,2,1,0:T(8,128)(2,1)S(1)}, u32[]{:S(2)}, u32[]{:S(2)}) collective-permute-start(bf16[4,2,128,128]{3,2,1,0:T(8,128)(2,1)S(1)} %collective-permute-done.7.rest_2_), channel_id=1, source_target_pairs={{0,2},{2,4},{4,6},{6,8},{8,10},{10,12},{12,14},{14,0},{1,3},{3,5},... | collective-permute-start | bytes 786440 | tf_op jit(solution)/shard_map/ppermute | solution.py:462
  33.1 7.8 %collective-permute-start.11 = (bf16[4,2,128,128]{3,2,1,0:T(8,128)(2,1)S(1)}, bf16[4,2,128,128]{3,2,1,0:T(8,128)(2,1)S(1)}, u32[]{:S(2)}, u32[]{:S(2)}) collective-permute-start(bf16[4,2,128,128]{3,2,1,0:T(8,128)(2,1)S(1)} %collective-permute-done.10.rest_5_.rest_6_), channel_id=1, source_target_pairs={{0,14},{2,0},{4,2},{6,4},{8,6},{10,8},{12,10},{14,12},{1,15},{3,1}... | collective-permute-start | bytes 786440 | tf_op jit(solution)/shard_map/ppermute | solution.py:466
  40.9 6.9 %collective-permute-start.12 = (bf16[4,2,128,128]{3,2,1,0:T(8,128)(2,1)S(1)}, bf16[4,2,128,128]{3,2,1,0:T(8,128)(2,1)S(1)}, u32[]{:S(2)}, u32[]{:S(2)}) collective-permute-start(bf16[4,2,128,128]{3,2,1,0:T(8,128)(2,1)S(1)} %collective-permute-done.8.rest_3_), channel_id=1, source_target_pairs={{0,2},{2,4},{4,6},{6,8},{8,10},{10,12},{12,14},{14,0},{1,3},{3,5},... | collective-permute-start | bytes 786440 | tf_op jit(solution)/shard_map/ppermute | solution.py:462
  57.7 10.3 %collective-permute-start.16 = (bf16[4,288,128]{2,1,0:T(8,128)(2,1)S(1)}, bf16[4,288,128]{2,1,0:T(8,128)(2,1)S(1)}, u32[]{:S(2)}, u32[]{:S(2)}) collective-permute-start(bf16[4,288,128]{2,1,0:T(8,128)(2,1)S(1)} %get-tuple-element.61.rest_0_.all_ref), channel_id=1, source_target_pairs={{0,2},{2,4},{4,6},{6,8},{8,10},{10,12},{12,14},{14,0},{1,3},{3,5},... | collective-permute-start | bytes 884744 | tf_op jit(solution)/shard_map/ppermute | solution.py:462
  57.8 10.2 %collective-permute-start.19 = (bf16[4,288,128]{2,1,0:T(8,128)(2,1)S(1)}, bf16[4,288,128]{2,1,0:T(8,128)(2,1)S(1)}, u32[]{:S(2)}, u32[]{:S(2)}) collective-permute-start(bf16[4,288,128]{2,1,0:T(8,128)(2,1)S(1)} %get-tuple-element.61.rest_0_.all_ref), channel_id=1, source_target_pairs={{0,14},{2,0},{4,2},{6,4},{8,6},{10,8},{12,10},{14,12},{1,15},{3,1}... | collective-permute-start | bytes 884744 | tf_op jit(solution)/shard_map/ppermute | solution.py:466
  61.6 14.8 %all-to-all-start = ((bf16[8,128,128]{2,1,0:T(8,128)(2,1)}), bf16[8,128,128]{2,1,0:T(8,128)(2,1)S(1)}, u32[]{:S(2)}, u32[]{:S(2)}) async-start(bf16[8,128,128]{2,1,0:T(8,128)(2,1)} %shard_map.166), calls=%async_computation | async-start | bytes 524288 | tf_op jit(solution)/shard_map/all_to_all | solution.py:553
  68.0 8.6 %collective-permute-start.17 = (bf16[4,288,128]{2,1,0:T(8,128)(2,1)S(1)}, bf16[4,288,128]{2,1,0:T(8,128)(2,1)S(1)}, u32[]{:S(2)}, u32[]{:S(2)}) collective-permute-start(bf16[4,288,128]{2,1,0:T(8,128)(2,1)S(1)} %collective-permute-done.16.rest_1_), channel_id=1, source_target_pairs={{0,2},{2,4},{4,6},{6,8},{8,10},{10,12},{12,14},{14,0},{1,3},{3,5},... | collective-permute-start | bytes 884744 | tf_op jit(solution)/shard_map/ppermute | solution.py:462
  68.1 8.5 %collective-permute-start.20 = (bf16[4,288,128]{2,1,0:T(8,128)(2,1)S(1)}, bf16[4,288,128]{2,1,0:T(8,128)(2,1)S(1)}, u32[]{:S(2)}, u32[]{:S(2)}) collective-permute-start(bf16[4,288,128]{2,1,0:T(8,128)(2,1)S(1)} %collective-permute-done.19.rest_6_.rest_7_), channel_id=1, source_target_pairs={{0,14},{2,0},{4,2},{6,4},{8,6},{10,8},{12,10},{14,12},{1,15},{3,1}... | collective-permute-start | bytes 884744 | tf_op jit(solution)/shard_map/ppermute | solution.py:466
  76.6 9.3 %collective-permute-start.18 = (bf16[4,288,128]{2,1,0:T(8,128)(2,1)S(1)}, bf16[4,288,128]{2,1,0:T(8,128)(2,1)S(1)}, u32[]{:S(2)}, u32[]{:S(2)}) collective-permute-start(bf16[4,288,128]{2,1,0:T(8,128)(2,1)S(1)} %collective-permute-done.17.rest_2_), channel_id=1, source_target_pairs={{0,2},{2,4},{4,6},{6,8},{8,10},{10,12},{12,14},{14,0},{1,3},{3,5},... | collective-permute-start | bytes 884744 | tf_op jit(solution)/shard_map/ppermute | solution.py:462
  77.9 14.3 %collective-permute-start.21 = (bf16[4,288,128]{2,1,0:T(8,128)(2,1)S(1)}, bf16[4,288,128]{2,1,0:T(8,128)(2,1)S(1)}, u32[]{:S(2)}, u32[]{:S(2)}) collective-permute-start(bf16[4,288,128]{2,1,0:T(8,128)(2,1)S(1)} %collective-permute-done.20.rest_5_.rest_6_), channel_id=1, source_target_pairs={{0,14},{2,0},{4,2},{6,4},{8,6},{10,8},{12,10},{14,12},{1,15},{3,1}... | collective-permute-start | bytes 884744 | tf_op jit(solution)/shard_map/ppermute | solution.py:466
  80.1 20.4 %all-to-all-start.1 = ((bf16[8,128,128]{2,1,0:T(8,128)(2,1)}), bf16[8,128,128]{2,1,0:T(8,128)(2,1)S(1)}, u32[]{:S(2)}, u32[]{:S(2)}) async-start(bf16[8,128,128]{2,1,0:T(8,128)(2,1)} %shard_map.167), calls=%async_computation.1 | async-start | bytes 524288 | tf_op jit(solution)/shard_map/all_to_all | solution.py:570
  86.0 13.8 %collective-permute-start.28 = (bf16[2,128,128]{2,1,0:T(8,128)(2,1)S(1)}, bf16[2,128,128]{2,1,0:T(8,128)(2,1)S(1)}, u32[]{:S(2)}, u32[]{:S(2)}) collective-permute-start(bf16[2,128,128]{2,1,0:T(8,128)(2,1)S(1)} %get-tuple-element.70), channel_id=1, source_target_pairs={{0,17},{1,16},{16,1},{17,0},{2,19},{3,18},{18,3},{19,2},{4,21},{5,... | collective-permute-start | bytes 196616 | tf_op jit(solution)/shard_map/ppermute | solution.py:496
  88.9 10.9 %collective-permute-start.27 = (bf16[2,128,128]{2,1,0:T(8,128)(2,1)S(1)}, bf16[2,128,128]{2,1,0:T(8,128)(2,1)S(1)}, u32[]{:S(2)}, u32[]{:S(2)}) collective-permute-start(bf16[2,128,128]{2,1,0:T(8,128)(2,1)S(1)} %get-tuple-element.68), channel_id=1, source_target_pairs={{0,16},{16,0},{1,17},{17,1},{2,18},{18,2},{3,19},{19,3},{4,20},{20... | collective-permute-start | bytes 196616 | tf_op jit(solution)/shard_map/ppermute | solution.py:458
  90.4 9.4 %collective-permute-start.26 = (bf16[2,128,128]{2,1,0:T(8,128)(2,1)S(1)}, bf16[2,128,128]{2,1,0:T(8,128)(2,1)S(1)}, u32[]{:S(2)}, u32[]{:S(2)}) collective-permute-start(bf16[2,128,128]{2,1,0:T(8,128)(2,1)S(1)} %get-tuple-element.66), channel_id=1, source_target_pairs={{0,1},{1,0},{2,3},{3,2},{4,5},{5,4},{6,7},{7,6},{8,9},{9,8},{10,11... | collective-permute-start | bytes 196616 | tf_op jit(solution)/shard_map/ppermute | solution.py:458
  90.4 16.3 %collective-permute-start.22 = (bf16[4,288,128]{2,1,0:T(8,128)(2,1)S(1)}, bf16[4,288,128]{2,1,0:T(8,128)(2,1)S(1)}, u32[]{:S(2)}, u32[]{:S(2)}) collective-permute-start(bf16[4,288,128]{2,1,0:T(8,128)(2,1)S(1)} %collective-permute-done.18.rest_3_), channel_id=1, source_target_pairs={{0,2},{2,4},{4,6},{6,8},{8,10},{10,12},{12,14},{14,0},{1,3},{3,5},... | collective-permute-start | bytes 884744 | tf_op jit(solution)/shard_map/ppermute | solution.py:462
  101.4 19.5 %all-to-all-start.2 = ((bf16[16,128,128]{2,1,0:T(8,128)(2,1)}), bf16[16,128,128]{2,1,0:T(8,128)(2,1)S(1)}, u32[]{:S(2)}, u32[]{:S(2)}) async-start(bf16[16,128,128]{2,1,0:T(8,128)(2,1)} %shard_map.168), calls=%async_computation.2 | async-start | bytes 1048576 | tf_op jit(solution)/shard_map/all_to_all | solution.py:589
  (30 other events, 256.8 us)
